TPU v7x, 128 devices: a whole 4x4x4 slice. The times are simulated.
128 devices in a mesh: seq: 8 (over y, x_hi), rep: 16 (over x_lo, z, core).
Axes of the slice: x: 4 (x_hi: 2, x_lo: 2; x = x_hi * 2 + x_lo), y: 4, z: 4, core: 2. Of those that a mesh axis runs over, the one named last changes fastest.
Arguments:
- tile_embed: bfloat16 [16, 8192, 768], P('rep', 'seq'), may hold values from -6 to 6
- tile_source: int32 [16, 8192], P('rep', 'seq'), may hold values from 0 to 8191, as said below
- slide_len: int32 [16], P('rep'), may hold values from 4096 to 8192
- grad_out: bfloat16 [16, 8192, 768], P('rep', 'seq'), may hold values from -6 to 6
- w_query: bfloat16 [768, 768], replicated, may hold values from -0.11727427342914273 to 0.11727427342914273
- w_key: bfloat16 [768, 768], replicated, may hold values from -0.11727427342914273 to 0.11727427342914273
- w_value: bfloat16 [768, 768], replicated, may hold values from -0.21875 to 0.21875
- w_out: bfloat16 [768, 768], replicated, may hold values from -0.21875 to 0.21875
Outputs:
- encoded: bfloat16 [16, 8192, 768], P('rep', 'seq')
- embed_grad: bfloat16 [16, 8192, 768], P('rep', 'seq')
- grad_query: float32 [768, 768], replicated
- grad_key: float32 [768, 768], replicated
- grad_value: float32 [768, 768], replicated
- grad_outproj: float32 [768, 768], replicated
Inputs may be any that keep to these rules, and one draw needn't show every extreme that they name: For each slide, tile_source is a permutation of 0 to 8191; each run of 1024 slide positions (aligned) takes exactly 1024 // (number of such runs) rows from each aligned run of 1024 rows of tile_embed.
All inputs are finite; a program needn't handle non-finite values.
Results may differ from a plain program's by a relative error of at most 0.0025.
The roundings to bfloat16 on the way count: a program that leaves them out, or rounds other values in their place, can miss the bound.
Values may be sent and summed in bfloat16 or wider, within the bound.
A program may use at most 192 MiB of HBM per device.

v0:
```python
import jax
import jax.numpy as jnp
from jax import lax
from jax.sharding import PartitionSpec as P

HEADS = 16
SEG = 1024
RATE = 16


NEGATIVE = -1e30


def sent_together(arrays, axis, dim, along):
    both = jnp.concatenate(arrays, axis=along)
    result, at, done = (lax.all_gather(both, axis, axis=dim, tiled=True), 0, [])
    for a in arrays:
        done.append(lax.slice_in_dim(result, at, at + a.shape[along], axis=along))
        at += a.shape[along]
    return tuple(done)


def side_by_side(arrays, axis, dim, along):
    widths = [a.shape[along] for a in arrays]
    both = jnp.concatenate(arrays, axis=along)
    result = lax.psum_scatter(both, axis, scatter_dimension=dim, tiled=True)
    return tuple(jnp.split(result, [sum(widths[:k]) for k in range(1, len(widths))], axis=along))


def chosen(dilation, head_count):
    return jnp.arange(dilation)[:, None] == (jnp.arange(head_count) % dilation)[None, :]


def sparse_rows(dense, dilation):
    row_count, head_count, trailing = dense.shape
    blocks = dense.astype(jnp.float32).reshape(
        row_count // dilation, dilation, head_count, trailing
    )
    selected = chosen(dilation, head_count)[None, :, :, None]
    return jnp.sum(jnp.where(selected, blocks, jnp.float32(0.0)), axis=1)


def spread_rows(sparse, dilation, filler):
    row_count, head_count, trailing = sparse.shape
    selected = chosen(dilation, head_count)[None, :, :, None]
    spread = jnp.where(selected, sparse[:, None], jnp.float32(filler))
    return spread.reshape(row_count * dilation, head_count, trailing)


def product(pattern, left_side, right_side):
    return jnp.einsum(pattern, left_side, right_side, preferred_element_type=jnp.float32)


def masked_scores(queries, key_rows, key_ok, pieces, scaling):
    scores = product("nqd,nkd->nqk", queries, key_rows) * scaling
    return jnp.where(key_ok.reshape(pieces, 1, -1), scores, NEGATIVE)


def head_forward(queries, key_rows, values, key_ok, pieces, scaling):
    head_width = queries.shape[-1]
    queries = queries.reshape(pieces, -1, head_width)
    key_rows = key_rows.reshape(pieces, -1, head_width)
    values = values.reshape(pieces, -1, head_width)
    scores = masked_scores(queries, key_rows, key_ok, pieces, scaling)
    maxima = jnp.max(scores, axis=-1)
    weights = jnp.exp(scores - maxima[..., None])
    totals = jnp.sum(weights, axis=-1)
    numerator = product("nqk,nkd->nqd", weights.astype(jnp.bfloat16), values)
    return (numerator.reshape(-1, head_width), maxima.reshape(-1), totals.reshape(-1))


def split_pieces(arrays, pieces):
    return tuple((member.reshape(pieces, -1, member.shape[-1]) for member in arrays))


def score_terms(queries, key_rows, values, key_ok, log_total, upstream, deltas, pieces, scaling):
    scores = masked_scores(queries, key_rows, key_ok, pieces, scaling)
    probabilities = jnp.exp(scores - log_total.reshape(pieces, -1, 1))
    prob_grad = product("nqd,nkd->nqk", upstream, values)
    score_grad = (probabilities * (prob_grad - deltas.reshape(pieces, -1, 1))).astype(jnp.bfloat16)
    return (probabilities, score_grad)


def head_backward(queries, key_rows, values, key_ok, log_total, upstream, deltas, pieces, scaling):
    head_width = queries.shape[-1]
    queries, key_rows, values, upstream = split_pieces(
        (queries, key_rows, values, upstream), pieces
    )
    probabilities, score_grad = score_terms(
        queries, key_rows, values, key_ok, log_total, upstream, deltas, pieces, scaling
    )
    value_grad = product("nqk,nqd->nkd", probabilities.astype(jnp.bfloat16), upstream)
    query_grad = product("nqk,nkd->nqd", score_grad, key_rows) * scaling
    key_grad = product("nqk,nqd->nkd", score_grad, queries) * scaling
    return (
        query_grad.reshape(-1, head_width),
        key_grad.reshape(-1, head_width),
        value_grad.reshape(-1, head_width),
    )


def heads_map(function, arrays, pieces, scaling):
    transposed = tuple((jnp.moveaxis(member, 1, 0) for member in arrays))
    results = lax.map(lambda members: function(*members, pieces, scaling), transposed)
    return tuple((jnp.moveaxis(member, 0, 1) for member in results))


def merge_parts(local_part, remote, dilation):
    numer_local, max_local, total_local = local_part
    numer_far = spread_rows(remote[0], dilation, 0.0)
    max_far = spread_rows(remote[1][..., None], dilation, NEGATIVE)[..., 0]
    total_far = spread_rows(remote[2][..., None], dilation, 0.0)[..., 0]
    highest = jnp.maximum(max_local, max_far)
    weight_local = jnp.exp(max_local - highest)
    weight_far = jnp.exp(max_far - highest)
    combined = total_local * weight_local + total_far * weight_far
    output = (numer_local * weight_local[..., None] + numer_far * weight_far[..., None]) / combined[
        ..., None
    ]
    return (output, highest + jnp.log(combined))


def project(left_side, right_side):
    return jnp.dot(left_side, right_side, preferred_element_type=jnp.float32)


def per_device(tile_embed, tile_source, slide_len, grad_out, w_query, w_key, w_value, w_out):
    owned_rows = tile_embed[0]
    source = tile_source[0]
    row_count, features = owned_rows.shape
    stripes = lax.axis_size("seq")
    stripe = lax.axis_index("seq")
    portion = row_count // stripes
    owner_dev = source // row_count
    ordering = jnp.argsort(owner_dev, stable=True)
    wanted = (source % row_count)[ordering].reshape(stripes, portion)
    requested = lax.all_to_all(wanted, "seq", split_axis=0, concat_axis=0, tiled=True)
    picked = jnp.take(owned_rows, requested.reshape(-1), axis=0).reshape(stripes, portion, features)
    arrived = lax.all_to_all(picked, "seq", split_axis=0, concat_axis=0, tiled=True).reshape(
        row_count, features
    )
    embedded = jnp.zeros_like(arrived).at[ordering].set(arrived)
    length = slide_len[0]
    upstream_in = grad_out[0]
    head_dim = features // HEADS
    scaling = head_dim ** (-0.5)
    positions = stripe * row_count + jnp.arange(row_count)
    valid_rows = positions < length
    queries = project(embedded, w_query).astype(jnp.bfloat16).reshape(row_count, HEADS, head_dim)
    key_rows = project(embedded, w_key).astype(jnp.bfloat16).reshape(row_count, HEADS, head_dim)
    values = project(embedded, w_value).astype(jnp.bfloat16).reshape(row_count, HEADS, head_dim)
    local_ok = jnp.broadcast_to(valid_rows[:, None], (row_count, HEADS))
    local_part = heads_map(
        head_forward, (queries, key_rows, values, local_ok), row_count // SEG, scaling
    )
    sparse_q = sparse_rows(queries, RATE).astype(jnp.bfloat16)
    sparse_k = sparse_rows(key_rows, RATE).astype(jnp.bfloat16)
    sparse_v = sparse_rows(values, RATE).astype(jnp.bfloat16)
    near_count = sparse_k.shape[0]
    far_k, far_v = sent_together(
        (sparse_k.reshape(near_count, features), sparse_v.reshape(near_count, features)),
        "seq",
        0,
        1,
    )
    far_count = far_k.shape[0]
    far_k = far_k.reshape(far_count, HEADS, head_dim)
    far_v = far_v.reshape(far_count, HEADS, head_dim)
    sparse_pos = jnp.arange(far_count)[:, None] * RATE + (jnp.arange(HEADS) % RATE)[None, :]
    sparse_ok = sparse_pos < length
    remote = heads_map(head_forward, (sparse_q, far_k, far_v, sparse_ok), 1, scaling)
    output, log_total = merge_parts(local_part, remote, RATE)
    attended = (
        (output * valid_rows[:, None, None]).astype(jnp.bfloat16).reshape(row_count, features)
    )
    encoded = (embedded.astype(jnp.float32) + project(attended, w_out)).astype(jnp.bfloat16)
    upstream = (
        (project(upstream_in, w_out.T) * valid_rows[:, None])
        .astype(jnp.bfloat16)
        .reshape(row_count, HEADS, head_dim)
    )
    deltas = jnp.sum(upstream.astype(jnp.float32) * output, axis=-1)
    grad_outproj = jnp.einsum(
        "td,te->de", attended, upstream_in, preferred_element_type=jnp.float32
    )
    local_grads = heads_map(
        head_backward,
        (queries, key_rows, values, local_ok, log_total, upstream, deltas),
        row_count // SEG,
        scaling,
    )
    sparse_up = sparse_rows(upstream, RATE).astype(jnp.bfloat16)
    sparse_delta = sparse_rows(deltas[..., None], RATE)[..., 0]
    sparse_total = sparse_rows(log_total[..., None], RATE)[..., 0]
    remote_grads = heads_map(
        head_backward,
        (sparse_q, far_k, far_v, sparse_ok, sparse_total, sparse_up, sparse_delta),
        1,
        scaling,
    )
    key_back, value_back = side_by_side(
        (
            remote_grads[1].reshape(far_count, features),
            remote_grads[2].reshape(far_count, features),
        ),
        "seq",
        0,
        1,
    )
    key_back = key_back.reshape(near_count, HEADS, head_dim)
    value_back = value_back.reshape(near_count, HEADS, head_dim)
    query_far = remote_grads[0]
    query_grad = (
        (local_grads[0] + spread_rows(query_far, RATE, 0.0))
        .astype(jnp.bfloat16)
        .reshape(row_count, features)
    )
    key_grad = (
        (local_grads[1] + spread_rows(key_back, RATE, 0.0))
        .astype(jnp.bfloat16)
        .reshape(row_count, features)
    )
    value_grad = (
        (local_grads[2] + spread_rows(value_back, RATE, 0.0))
        .astype(jnp.bfloat16)
        .reshape(row_count, features)
    )
    embed_grad = upstream_in.astype(jnp.float32) + project(query_grad, w_query.T)
    embed_grad = embed_grad + project(key_grad, w_key.T)
    embed_grad = (embed_grad + project(value_grad, w_value.T)).astype(jnp.bfloat16)
    grad_query = jnp.einsum("td,te->de", embedded, query_grad, preferred_element_type=jnp.float32)
    grad_key = jnp.einsum("td,te->de", embedded, key_grad, preferred_element_type=jnp.float32)
    grad_value = jnp.einsum("td,te->de", embedded, value_grad, preferred_element_type=jnp.float32)
    summed = lax.psum((grad_query, grad_key, grad_value, grad_outproj), ("seq", "rep"))
    return (encoded[None], embed_grad[None], summed[0], summed[1], summed[2], summed[3])


def solution(mesh):
    return jax.shard_map(
        per_device,
        mesh=mesh,
        in_specs=(
            P("rep", "seq", None),
            P("rep", "seq"),
            P("rep"),
            P("rep", "seq", None),
            P(),
            P(),
            P(),
            P(),
        ),
        out_specs=(P("rep", "seq", None), P("rep", "seq", None), P(), P(), P(), P()),
        check_vma=False,
    )
```

profile of v0, /device:TPU:1, one launch (start us, length us, event | category | flops | bytes accessed | tf_op | source)
XLA Modules:
  0.0 927.7 jit_solution(13894790200978015584)
XLA Ops:
  12.4 4.5 gather_fusion
  16.9 13.8 %all_to_all.14 = s32[8,1,128]{2,1,0:T(1,128)S(1)} all-to-all(s32[8,1,128]{2,1,0:T(1,128)S(1)} %bitcast.386), channel_id=1, replica_groups=mesh['seq'=8,'rep'=16] {'seq'}, dimensions={0} | all-to-all | bytes 8192 | tf_op jit(solution)/shard_map/all_to_all | solution.py:137
  47.3 4.8 copy.100
  55.3 7.8 reshape.434
  65.1 6.4 scatter_custom_fusion
  76.8 7.8 reshape.431
  90.0 7.8 reshape.432
  105.1 7.8 reshape.433
  112.9 14.1 %select_reduce_fusion = (bf16[64,16,48]{2,1,0:T(8,128)(2,1)S(1)}, bf16[64,16,48]{2,1,0:T(8,128)(2,1)}, bf16[64,16,48]{2,1,0:T(8,128)(2,1)}, bf16[64,16,48]{2,1,0:T(8,128)(2,1)}) fusion(f32[64,16,16,48]{3,2,1,0:T(8,128)} %reshape.434, pred[16,16]{1,0:T(8,128)(4,1)} %copy-done.23, f32[64,16,16,48]{3,2,1,0:T(8,128)} %reshape.432, ...), kind=kLoop, calls=%fused_computation.133 | loop fusion | flops 6094848 | bytes 12976384 | tf_op jit(solution)/shard_map/reduce_sum | solution.py:40
  144.3 142.6 %while.56 = (s32[]{:T(128)}, f32[16,1024,48]{1,2,0:T(8,128)}, f32[16,1024]{1,0:T(8,128)S(1)}, f32[16,1024]{1,0:T(8,128)S(1)}, pred[16,1024]{1,0:T(8,128)(4,1)S(1...) while((s32[]{:T(128)}, f32[16,1024,48]{1,2,0:T(8,128)}, ...), condition=%wide.region_5.6_spmd, body=%wide.region_2.5_spmd.sunk | while | flops 212858880 | bytes 30383244 | solution.py:104
  287.0 7.9 copy.83
  301.3 42.2 %while.57 = (s32[]{:T(128)}, f32[16,64,48]{1,2,0:T(8,128)S(1)}, f32[16,64]{1,0:T(8,128)S(1)}, f32[16,64]{1,0:T(8,128)S(1)}, pred[16,512]{1,0:T(8,128)(4,1)S(1)},...) while((s32[]{:T(128)}, f32[16,64,48]{1,2,0:T(8,128)S(1)}, ...), condition=%wide.region_12.13_spmd, body=%wide.region_9.12_spmd.sunk | while | flops 6520706 | bytes 702321 | solution.py:104
  346.2 13.4 %multiply_convert_fusion.1 = (bf16[1024,16,48]{2,1,0:T(8,128)(2,1)}, f32[1024,16,48]{2,1,0:T(8,128)S(1)}) fusion(f32[1024]{0:T(1024)S(1)} %copy-done.25, f32[1024,16]{1,0:T(8,128)} %copy.97, f32[1024,16]{1,0:T(8,128)S(1)} %copy.96, f32[64,16,48]{2,1,0:T(8,128)S(1)} %copy.95, pred[1024,16]{1,0:T(8,128)(4,1)S(1)} %copy.94, f32[1024,16]{1,0:T(8,128)S(1)} %copy.93, ...), kind=kLoop, calls=%fused_computation.135 | loop fusion | flops 5505024 | bytes 8278016 | tf_op jit(solution)/shard_map/convert_element_type | solution.py:174
  362.9 103.9 %while.59 = (s32[]{:T(128)}, f32[16,64,48]{1,2,0:T(8,128)S(1)}, f32[16,512,48]{1,2,0:T(8,128)}, f32[16,512,48]{1,2,0:T(8,128)}, pred[16,512]{1,0:T(8,128)(4,1)S(...) while((s32[]{:T(128)}, f32[16,64,48]{1,2,0:T(8,128)S(1)}, ...), condition=%wide.region_20.21_spmd, body=%wide.region_19.20_spmd.sunk | while | flops 15985666 | bytes 1278077 | solution.py:104
  481.0 181.1 %while.58 = (s32[]{:T(128)}, f32[16,1024,48]{1,2,0:T(8,128)}, f32[16,1024,48]{1,2,0:T(8,128)}, f32[16,1024,48]{1,2,0:T(8,128)}, pred[16,1024]{1,0:T(8,128)(4,1)S...) while((s32[]{:T(128)}, f32[16,1024,48]{1,2,0:T(8,128)}, ...), condition=%wide.region_15.16_spmd, body=%wide.region_14.15_spmd.sunk | while | flops 513900544 | bytes 21337212 | solution.py:104
  662.5 7.9 copy.102
  670.3 7.8 copy.112
  678.2 7.8 copy.115
  686.0 5.5 copy.98
  699.3 15.1 %fusion.110 = (bf16[1024,16,48]{2,1,0:T(8,128)(2,1)}, bf16[1024,16,48]{2,1,0:T(8,128)(2,1)}, bf16[1024,16,48]{2,1,0:T(8,128)(2,1)}) fusion(f32[16,1024,48]{2,0,1:T(8,128)} %copy.102, f32[64,16,48]{2,1,0:T(8,128)S(1)} %copy.110, pred[1024,16]{1,0:T(8,128)(4,1)} %copy-done.14, f32[64,16,48]{2,1,0:T(8,128)S(1)} %copy.113, f32[16,1024,48]{2,0,1:T(8,128)} %copy.112, ...), kind=kLoop, calls=%fused_computation.127 | loop fusion | flops 7077888 | bytes 14761984 | tf_op jit(solution)/shard_map/convert_element_type | solution.py:215
  714.4 5.5 copy.111
  724.2 5.5 copy.114
  742.7 5.0 fusion.117
  753.6 157.5 %all-reduce.3.cloned.1.call-done = (f32[768,768]{1,0:T(8,128)}, f32[768,768]{1,0:T(8,128)}, f32[768,768]{1,0:T(8,128)}, f32[768,768]{1,0:T(8,128)}) async-done(((f32[768,768]{1,0:T(8,128)}, f32[768,768]{1,0:T(8,128)}, f32[768,768]{1,0:T(8,128)}, f32[768,768]{1,0:T(8,128)}), (f32[768,768]{1,0:T(8,128)}, f32[768,768]{1,0:T(8,128)}, f32[768,768]{1,0:T(8,128)}, ...) | async-done | bytes 9437200 | tf_op jit(solution)/shard_map/psum | solution.py:234
  (605 shorter events, 596.5 us)
Async XLA Ops:
  7.2 23.6 %copy-start = (bf16[1,1024,768]{2,1,0:T(8,128)(2,1)S(1)}, bf16[1,1024,768]{2,1,0:T(8,128)(2,1)}, u32[]{:S(2)}) copy-start(bf16[1,1024,768]{2,1,0:T(8,128)(2,1)} %param.16) | copy-start | bytes 4718596
  36.1 6.4 copy-start.8
  36.1 29.0 %all-to-all-start.1 = ((bf16[8,128,768]{2,1,0:T(8,128)(2,1)}), bf16[8,128,768]{2,1,0:T(8,128)(2,1)}, u32[]{:S(2)}, u32[]{:S(2)}) async-start(bf16[8,128,768]{2,1,0:T(8,128)(2,1)} %broadcast_select_fusion), calls=%async_computation.1 | async-start | bytes 3145728 | tf_op jit(solution)/shard_map/all_to_all | solution.py:139
  40.5 255.1 %all-gather.2.cloned.1.call-start = ((), (), s32[]{:S(2)}) async-start(), calls=%async_computation.3 | async-start | bytes 1769472 | tf_op jit(solution)/shard_map/all_gather | solution.py:16
  64.4 281.8 %copy-start.14 = (pred[1024,16]{1,0:T(8,128)(4,1)}, pred[1024,16]{1,0:T(8,128)(4,1)S(1)}, u32[]{:S(2)}) copy-start(pred[1024,16]{1,0:T(8,128)(4,1)S(1)} %copy.94) | copy-start | bytes 49156
  71.5 3.3 copy-start.10
  132.4 563.3 %reduce-scatter.4.cloned.1.call-start = ((), (), s32[]{:S(2)}) async-start(), calls=%async_computation.4 | async-start | bytes 3538944
  135.9 3.2 copy-start.4
  139.0 3.2 copy-start.28
  139.0 5.3 copy-start.19
  139.0 5.3 copy-start.20
  144.3 142.7 %copy-start.16 = (bf16[64,16,48]{2,1,0:T(8,128)(2,1)S(1)}, bf16[64,16,48]{2,1,0:T(8,128)(2,1)}, u32[]{:S(2)}) copy-start(bf16[64,16,48]{2,1,0:T(8,128)(2,1)} %get-tuple-element.310) | copy-start | bytes 294916
  343.4 2.7 copy-start.25
  346.2 13.4 %copy-start.3 = (bf16[1024,16,48]{2,1,0:T(8,128)(2,1)S(1)}, bf16[1024,16,48]{2,1,0:T(8,128)(2,1)}, u32[]{:S(2)}) copy-start(bf16[1024,16,48]{2,1,0:T(8,128)(2,1)} %copy.100) | copy-start | bytes 4718596
  359.6 3.0 copy-start.22
  474.7 436.5 %all-reduce.3.cloned.1.call-start = ((), (), s32[]{:S(2)}) async-start(), calls=%async_computation.5 | async-start | bytes 18874368 | tf_op jit(solution)/shard_map/psum | solution.py:234
  686.0 5.5 copy-start.9
  714.4 5.5 copy-start.11
  742.7 5.0 copy-start.12
  742.7 5.0 copy-start.29
  911.1 3.4 copy-start.7
  914.5 2.5 copy-start.6
  917.0 2.5 copy-start.5
  917.0 3.9 copy-start.1
  (26 other events, 46.8 us)
Sparse Core Ops, SparseCore 0:
  132.6 52.8 all-gather.1
  474.8 81.6 reduce-scatter.3
  742.8 168.2 all-reduce.2
where the time goes:
time: 942 us; the launch traced here: 928 us
  matrix products  454 us (48%)
  local copies, waits for them, and re-layouts  204 us (22%)
  waiting for transfers between devices  158 us (17%)
  other arithmetic  76.5 us (8%)
  between operations  15.1 us (2%)
  blocking collectives  13.8 us (1%)
    dot_general x224, matrix products, product(): jnp.einsum(pattern, left_side, right_side, preferred_element_type=jnp.flo...  413 us
    psum x1, waiting for transfers between devices, per_device(): lax.psum((grad_query, grad_key, grad_value, grad_outproj), ('seq', 'rep'))  158 us
    while x9, local copies, waits for them, and re-layouts, heads_map(): lax.map(lambda members: function(*members, pieces, scaling), transposed)  35.9 us
    while x32, local copies, waits for them, and re-layouts  30.8 us
    convert_element_type x6, local copies, waits for them, and re-layouts, sparse_rows(): dense.astype(jnp.float32)  30.7 us
    dot_general x8, matrix products, project(): return jnp.dot(left_side, right_side, preferred_element_type=jnp.float32)  24 us
  transfers between devices with their start and end apart: 4, of which 1 were waited for; matrix products, arithmetic and copies ran while one was open for 41% of the time, Pallas kernels for 0%

commit v1 on v0

v1 whole, which is shorter than its diff:
```python
import functools

import jax
import jax.numpy as jnp
from jax import lax
from jax.experimental import pallas as pl
from jax.experimental.pallas import tpu as pltpu
from jax.sharding import PartitionSpec as P

HEADS=16; RATE=16; HD=48; D=768; T=1024; FAR=512
BF=jnp.bfloat16; F32=jnp.float32
LOG2E=1.4426950408889634
NEG=-1e30
QC=512

def nn(a,b): return lax.dot_general(a,b,(((1,),(0,)),((),())),preferred_element_type=F32)
def nt(a,b): return lax.dot_general(a,b,(((1,),(1,)),((),())),preferred_element_type=F32)

def attn_kernel(len_ref, k_ref, v_ref, qT_ref, kT_ref, vT_ref, gT_ref, kf_ref, vf_ref, kfT_ref, vfT_ref,
                attT_ref, dqT_ref, dkT_ref, dvT_ref, dkfT_ref, dvfT_ref,
                qpad, gpad, kb, kfb, m2s, l2s, u2s, w2s, des, dqs, e2s):
    h = pl.program_id(0)
    n = len_ref[0]
    nfull = len_ref[1]
    scale = HD ** -0.5
    c = scale * LOG2E
    hh = lax.rem(h, 8)
    w0 = pl.multiple_of((h // 8) * 384 + jnp.where(hh >= 5, 128, 0), 128)
    off = h * HD - w0
    r = pl.multiple_of(h * HD, 16)
    row = lax.broadcasted_iota(jnp.int32, (256, T), 0)
    inside = (row >= off) & (row < off + HD)
    free = jnp.where(off >= 48, 0, 255)
    qw = qT_ref[pl.ds(w0, 256), :]
    gw = gT_ref[pl.ds(w0, 256), :]
    one = jnp.where(row == free, 1.0, 0.0).astype(BF)
    qpad[...] = jnp.where(inside, qw, one)
    gpad[...] = jnp.where(inside, gw, jnp.zeros_like(gw))
    ki = lax.broadcasted_iota(jnp.int32, (T, 1), 0)
    kpos = lax.rem(ki, 64) * RATE + ki // 64
    kbias = jnp.where(kpos < n, 0.0, NEG).astype(BF)
    lane = lax.broadcasted_iota(jnp.int32, (T, 256), 1)
    kb[...] = jnp.where(lane == free, kbias, k_ref[:, pl.ds(w0, 256)])
    fi = lax.broadcasted_iota(jnp.int32, (FAR, 1), 0)
    fbias = jnp.where(fi * RATE + h < nfull, 0.0, NEG).astype(BF)
    flane = lax.broadcasted_iota(jnp.int32, (FAR, 256), 1)
    kfb[...] = jnp.where(flane == free, fbias, kf_ref[:, pl.ds(w0, 256)])
    wq = pl.multiple_of((h // 2) * 128, 128)
    qlane = lax.broadcasted_iota(jnp.int32, (1, 128), 1)
    mine = (qlane // 64) == lax.rem(h, 2)
    S2 = nn(kfb[...], qpad[:, pl.ds(wq, 128)])
    x2 = jnp.max(S2, axis=0, keepdims=True)
    e2 = jnp.exp2(S2 * c - x2 * c)
    e2s[...] = e2
    l2 = jnp.sum(e2, axis=0, keepdims=True)
    u2 = nn(vfT_ref[pl.ds(r, HD), :], e2.astype(BF))
    m2s[...] = jnp.full_like(m2s, NEG)
    l2s[...] = jnp.zeros_like(l2s)
    u2s[...] = jnp.zeros_like(u2s)
    m2s[:, pl.ds(wq, 128)] = jnp.where(mine, x2 * scale, NEG)
    l2s[:, pl.ds(wq, 128)] = jnp.where(mine, l2, 0.0)
    u2s[:, pl.ds(wq, 128)] = jnp.where(mine, u2, 0.0)
    vwin = v_ref[:, pl.ds(w0, 256)]
    vTh = vT_ref[pl.ds(r, HD), :]
    kTh = kT_ref[pl.ds(r, HD), :]
    dv = jnp.zeros((HD, T), F32)
    dk = jnp.zeros((HD, T), F32)
    for ci in range(T // QC):
        sl = slice(ci * QC, (ci + 1) * QC)
        S = nn(kb[...], qpad[:, sl])
        x1 = jnp.max(S, axis=0, keepdims=True)
        e = jnp.exp2(S * c - x1 * c)
        l1 = jnp.sum(e, axis=0, keepdims=True)
        u1 = nn(vTh, e.astype(BF))
        m1 = x1 * scale
        m2 = m2s[:, sl]; l2c = l2s[:, sl]
        M = jnp.maximum(m1, m2)
        a1 = jnp.exp(m1 - M); a2 = jnp.exp(m2 - M)
        inv = 1.0 / (a1 * l1 + a2 * l2c)
        w1 = a1 * inv; w2 = a2 * inv
        o = u1 * w1 + u2s[:, sl] * w2
        qi = lax.broadcasted_iota(jnp.int32, (1, QC), 1) + ci * QC
        ok = (lax.rem(qi, 64) * RATE + qi // 64) < n
        attT_ref[pl.ds(r, HD), sl] = jnp.where(ok, o, 0.0).astype(BF)
        gTh = gT_ref[pl.ds(r, HD), sl]
        delta = jnp.sum(gTh.astype(F32) * o, axis=0, keepdims=True)
        w2s[:, sl] = w2
        des[:, sl] = delta
        dP = nn(vwin, gpad[:, sl])
        P = e * w1
        dS = (P * (dP - delta)).astype(BF)
        dqs[:, sl] = nn(kTh, dS)
        dv += nt(gTh, P.astype(BF))
        dk += nt(qT_ref[pl.ds(r, HD), sl], dS)
    dvT_ref[pl.ds(r, HD), :] = dv
    dkT_ref[pl.ds(r, HD), :] = dk * scale
    P2 = e2s[...] * jnp.where(mine, w2s[:, pl.ds(wq, 128)], 0.0)
    dP2 = nn(vf_ref[:, pl.ds(w0, 256)], gpad[:, pl.ds(wq, 128)])
    dS2 = (P2 * (dP2 - des[:, pl.ds(wq, 128)])).astype(BF)
    dvfT_ref[pl.ds(r, HD), :] = nt(gT_ref[pl.ds(r, HD), pl.ds(wq, 128)], P2.astype(BF))
    dkfT_ref[pl.ds(r, HD), :] = nt(qT_ref[pl.ds(r, HD), pl.ds(wq, 128)], dS2) * scale
    dqs[:, pl.ds(wq, 128)] += nn(kfT_ref[pl.ds(r, HD), :], dS2)
    dqT_ref[pl.ds(r, HD), :] = (dqs[...] * scale).astype(BF)

def attn(lens, *arrs):
    vm = pl.BlockSpec(memory_space=pltpu.VMEM)
    return pl.pallas_call(
        attn_kernel, grid=(HEADS,),
        in_specs=[pl.BlockSpec(memory_space=pltpu.SMEM)] + [vm]*10,
        out_specs=[vm]*6,
        out_shape=[jax.ShapeDtypeStruct((D,T),BF), jax.ShapeDtypeStruct((D,T),BF), jax.ShapeDtypeStruct((D,T),F32), jax.ShapeDtypeStruct((D,T),F32),
                   jax.ShapeDtypeStruct((D,FAR),F32), jax.ShapeDtypeStruct((D,FAR),F32)],
        scratch_shapes=[pltpu.VMEM((256,T),BF), pltpu.VMEM((256,T),BF), pltpu.VMEM((T,256),BF), pltpu.VMEM((FAR,256),BF),
                        pltpu.VMEM((1,T),F32), pltpu.VMEM((1,T),F32), pltpu.VMEM((HD,T),F32), pltpu.VMEM((1,T),F32), pltpu.VMEM((1,T),F32),
                        pltpu.VMEM((HD,T),F32), pltpu.VMEM((FAR,128),F32)],
        compiler_params=pltpu.CompilerParams(vmem_limit_bytes=60<<20),
    )(lens, *arrs)


def vm():
    return pl.BlockSpec(memory_space=pltpu.VMEM)


def sm():
    return pl.BlockSpec(memory_space=pltpu.SMEM)


def project_kernel(len_ref, x_ref, go_ref, wq_ref, wk_ref, wv_ref, wo_ref,
                   k_ref, v_ref, qT_ref, kT_ref, vT_ref, gT_ref, far_ref):
    n = len_ref[0]
    x = x_ref[...]
    k = nn(x, wk_ref[...]).astype(BF)
    v = nn(x, wv_ref[...]).astype(BF)
    k_ref[...] = k
    v_ref[...] = v
    qT_ref[...] = nn(x, wq_ref[...]).astype(BF).T
    kT_ref[...] = k.T
    vT_ref[...] = v.T
    qi = lax.broadcasted_iota(jnp.int32, (1, T), 1)
    ok = (lax.rem(qi, 64) * RATE + qi // 64) < n
    gT_ref[...] = jnp.where(ok, nt(wo_ref[...], go_ref[...]), 0.0).astype(BF)
    col = lax.broadcasted_iota(jnp.int32, (64, D), 1) // HD
    fk = jnp.zeros((64, D), BF)
    fv = jnp.zeros((64, D), BF)
    for h in range(HEADS):
        fk = jnp.where(col == h, k_ref[h * 64:(h + 1) * 64, :], fk)
        fv = jnp.where(col == h, v_ref[h * 64:(h + 1) * 64, :], fv)
    far_ref[:, :D] = fk
    far_ref[:, D:] = fv


def project_all(lens, x, go, wq, wk, wv, wo):
    s = jax.ShapeDtypeStruct
    return pl.pallas_call(
        project_kernel,
        in_specs=[sm()] + [vm()] * 6,
        out_specs=[vm()] * 7,
        out_shape=[s((T, D), BF)] * 2 + [s((D, T), BF)] * 4 + [s((64, 2 * D), BF)],
        compiler_params=pltpu.CompilerParams(vmem_limit_bytes=60 << 20),
        cost_estimate=pl.CostEstimate(flops=8 * T * D * D, bytes_accessed=20 << 20, transcendentals=0),
    )(lens, x, go, wq, wk, wv, wo)


def outer_kernel(x_ref, go_ref, attT_ref, dqT_ref, wo_ref, enc_ref, gq_ref, go_out_ref):
    x = x_ref[...]
    att = attT_ref[...].T
    enc_ref[...] = (x.astype(F32) + nn(att, wo_ref[...])).astype(BF)
    go_out_ref[...] = nn(attT_ref[...], go_ref[...])
    gq_ref[...] = nt(x.T, dqT_ref[...])


def outer_all(x, go, attT, dqT, wo):
    s = jax.ShapeDtypeStruct
    return pl.pallas_call(
        outer_kernel,
        in_specs=[vm()] * 5,
        out_specs=[vm()] * 3,
        out_shape=[s((T, D), BF), s((D, D), F32), s((D, D), F32)],
        compiler_params=pltpu.CompilerParams(vmem_limit_bytes=60 << 20),
        cost_estimate=pl.CostEstimate(flops=6 * T * D * D, bytes_accessed=12 << 20, transcendentals=0),
    )(x, go, attT, dqT, wo)


def final_kernel(x_ref, go_ref, dqT_ref, dkT_ref, dvT_ref, back_ref, wq_ref, wk_ref, wv_ref,
                 emb_ref, gk_ref, gv_ref, dkT_s, dvT_s):
    bT = back_ref[...].T
    dkT_s[...] = dkT_ref[...]
    dvT_s[...] = dvT_ref[...]
    zero = jnp.zeros((HD, 64), F32)
    for h in range(HEADS):
        r = slice(h * HD, (h + 1) * HD)
        w = slice((h // 2) * 128, (h // 2) * 128 + 128)
        bk = bT[h * HD:(h + 1) * HD, :]
        bv = bT[D + h * HD:D + (h + 1) * HD, :]
        pk = [bk, zero] if h % 2 == 0 else [zero, bk]
        pv = [bv, zero] if h % 2 == 0 else [zero, bv]
        dkT_s[r, w] += jnp.concatenate(pk, axis=1)
        dvT_s[r, w] += jnp.concatenate(pv, axis=1)
    dk = dkT_s[...].astype(BF)
    dv = dvT_s[...].astype(BF)
    e = nn(wq_ref[...], dqT_ref[...]) + nn(wk_ref[...], dk) + nn(wv_ref[...], dv)
    emb_ref[...] = (go_ref[...].astype(F32) + e.T).astype(BF)
    xT = x_ref[...].T
    gk_ref[...] = nt(xT, dk)
    gv_ref[...] = nt(xT, dv)


def final_all(x, go, dqT, dkT, dvT, back, wq, wk, wv):
    s = jax.ShapeDtypeStruct
    return pl.pallas_call(
        final_kernel,
        in_specs=[vm()] * 9,
        out_specs=[vm()] * 3,
        out_shape=[s((T, D), BF), s((D, D), F32), s((D, D), F32)],
        scratch_shapes=[pltpu.VMEM((D, T), F32)] * 2,
        compiler_params=pltpu.CompilerParams(vmem_limit_bytes=60 << 20),
        cost_estimate=pl.CostEstimate(flops=10 * T * D * D, bytes_accessed=20 << 20, transcendentals=0),
    )(x, go, dqT, dkT, dvT, back, wq, wk, wv)


def to_local(a):
    return a.reshape(64, RATE, -1).transpose(1, 0, 2).reshape(T, -1)


def from_local(a):
    return a.reshape(RATE, 64, -1).transpose(1, 0, 2).reshape(T, -1)


def per_device(tile_embed, tile_source, slide_len, grad_out, w_query, w_key, w_value, w_out):
    owned_rows = tile_embed[0]
    source = to_local(tile_source[0]).reshape(-1)
    row_count, features = owned_rows.shape
    stripes = lax.axis_size("seq")
    stripe = lax.axis_index("seq")
    portion = row_count // stripes
    owner_dev = source // row_count
    ordering = jnp.argsort(owner_dev, stable=True)
    wanted = (source % row_count)[ordering].reshape(stripes, portion)
    requested = lax.all_to_all(wanted, "seq", split_axis=0, concat_axis=0, tiled=True)
    picked = jnp.take(owned_rows, requested.reshape(-1), axis=0).reshape(stripes, portion, features)
    arrived = lax.all_to_all(picked, "seq", split_axis=0, concat_axis=0, tiled=True).reshape(
        row_count, features
    )
    x = jnp.zeros_like(arrived).at[ordering].set(arrived)
    length = slide_len[0]
    lens = jnp.stack([length - stripe * row_count, length]).astype(jnp.int32)
    go = to_local(grad_out[0])
    k, v, qT, kT, vT, gT, far = project_all(lens, x, go, w_query, w_key, w_value, w_out)
    farall = lax.all_gather(far, "seq", axis=0, tiled=True)
    kf = farall[:, :D]
    vf = farall[:, D:]
    attT, dqT, dkT, dvT, dkfT, dvfT = attn(lens, k, v, qT, kT, vT, gT, kf, vf, kf.T, vf.T)
    back = lax.psum_scatter(
        jnp.concatenate([dkfT.T, dvfT.T], axis=1), "seq", scatter_dimension=0, tiled=True
    )
    enc, gq, gout = outer_all(x, go, attT, dqT, w_out)
    emb, gk, gv = final_all(x, go, dqT, dkT, dvT, back, w_query, w_key, w_value)
    summed = lax.psum((gq, gk, gv, gout), ("seq", "rep"))
    return (from_local(enc)[None], from_local(emb)[None], summed[0], summed[1], summed[2], summed[3])


def solution(mesh):
    return jax.shard_map(
        per_device,
        mesh=mesh,
        in_specs=(
            P("rep", "seq", None),
            P("rep", "seq"),
            P("rep"),
            P("rep", "seq", None),
            P(),
            P(),
            P(),
            P(),
        ),
        out_specs=(P("rep", "seq", None), P("rep", "seq", None), P(), P(), P(), P()),
        check_vma=False,
    )
```

time: 942 us -> 496 us (0.53); the launches traced: 928 us -> 495 us
  matrix products: 454 us -> 0 us
  local copies, waits for them, and re-layouts: 204 us -> 40.3 us
  waiting for transfers between devices: 158 us -> 295 us
  Pallas kernels: 0 us -> 118 us
  other arithmetic: 76.5 us -> 9.89 us
    dot_general x236 -> x0, matrix products: 454 us -> none  [the longest x224 413 us: product(): jnp.einsum(pattern, left_side, right_side, preferred_element_type=jnp.flo...]
    pallas_call x0 -> x4, Pallas kernels: none -> 118 us  [the longest x1 85.2 us: attn(): pl.pallas_call(attn_kernel, grid=(HEADS,), in_specs=[pl.BlockSpec(memory_...]
    reduce_scatter x0 -> x1, waiting for transfers between devices: none -> 67.8 us  [per_device(): lax.psum_scatter(jnp.concatenate([dkfT.T, dvfT.T], axis=1), 'seq', scatte...]
    while x41 -> x0, local copies, waits for them, and re-layouts: 66.7 us -> none  [the longest x9 35.9 us: heads_map(): lax.map(lambda members: function(*members, pieces, scaling), transposed)]
    convert_element_type x14 -> x0, local copies, waits for them, and re-layouts: 65.3 us -> none  [the longest x6 30.7 us: sparse_rows(): dense.astype(jnp.float32)]
    all_gather x1, waiting for transfers between devices: 0.01 us -> 49.7 us  [per_device(): farall = lax.all_gather(far, 'seq', axis=0, tiled=True)]
    reduce_sum x35 -> x0, other arithmetic: 34.5 us -> none  [the longest x32 17.8 us: head_forward(): totals = jnp.sum(weights, axis=-1)]
    convert_element_type x2 -> x0, other arithmetic: 28.5 us -> none  [the longest x1 15.1 us: per_device(): query_grad = (local_grads[0] + spread_rows(query_far, RATE, 0.0)).astype(...]
  transfers between devices with their start and end apart: 4 -> 4, of which waited for: 1 -> 4; matrix products, arithmetic and copies ran while one was open for 41% -> 1% of each run, Pallas kernels for 0% -> 2%
where the time goes in v1:
time: 496 us; the launch traced here: 495 us
  waiting for transfers between devices  295 us (59%)
  Pallas kernels  118 us (24%)
  local copies, waits for them, and re-layouts  40.3 us (8%)
  between operations  14.5 us (3%)
  blocking collectives  13.8 us (3%)
  other arithmetic  9.89 us (2%)
    psum x1, waiting for transfers between devices, per_device(): summed = lax.psum((gq, gk, gv, gout), ('seq', 'rep'))  160 us
    pallas_call x1, Pallas kernels, attn(): pl.pallas_call(attn_kernel, grid=(HEADS,), in_specs=[pl.BlockSpec(memory_...  85.2 us
    reduce_scatter x1, waiting for transfers between devices, per_device(): lax.psum_scatter(jnp.concatenate([dkfT.T, dvfT.T], axis=1), 'seq', scatte...  67.8 us
    all_gather x1, waiting for transfers between devices, per_device(): farall = lax.all_gather(far, 'seq', axis=0, tiled=True)  49.7 us
    all_to_all x1, waiting for transfers between devices, per_device(): lax.all_to_all(picked, 'seq', split_axis=0, concat_axis=0, tiled=True)  17.5 us
    unnamed x27, local copies, waits for them, and re-layouts  14.3 us
    all_to_all x1, blocking collectives, per_device(): lax.all_to_all(wanted, 'seq', split_axis=0, concat_axis=0, tiled=True)  13.8 us
    pallas_call x1, Pallas kernels, final_all(): pl.pallas_call(final_kernel, in_specs=[vm()] * 9, out_specs=[vm()] * 3, o...  13.6 us
  transfers between devices with their start and end apart: 4, of which 4 were waited for; matrix products, arithmetic and copies ran while one was open for 1% of the time, Pallas kernels for 2%

profile of v1, /device:TPU:1, one launch (start us, length us, event | category | flops | bytes accessed | tf_op | source)
XLA Modules:
  0.0 495.4 jit_solution(5727290922688396632)
XLA Ops:
  9.3 4.4 sort.17
  13.7 4.5 gather_fusion
  18.2 13.8 %all_to_all.14 = s32[8,1,128]{2,1,0:T(1,128)S(1)} all-to-all(s32[8,1,128]{2,1,0:T(1,128)S(1)} %bitcast.49), channel_id=1, replica_groups=mesh['seq'=8,'rep'=16] {'seq'}, dimensions={0} | all-to-all | bytes 8192 | tf_op jit(solution)/shard_map/all_to_all | solution.py:239
  32.0 4.0 gather_fusion.1
  37.4 3.7 all-to-all-start.1
  41.8 1.6 copy.32
  44.0 17.5 %all-to-all-done.1 = bf16[8,128,768]{2,1,0:T(8,128)(2,1)S(1)} async-done(((bf16[8,128,768]{2,1,0:T(8,128)(2,1)}), bf16[8,128,768]{2,1,0:T(8,128)(2,1)S(1)}, u32[]{:S(2)}, u32[]{:S(2)}) %all-to-all-start.1) | async-done | bytes 1572896 | tf_op jit(solution)/shard_map/all_to_all | solution.py:241
  61.5 6.4 %scatter_custom_fusion.x_ref = bf16[1024,768]{1,0:T(8,128)(2,1)} fusion(s32[1024]{0:T(1024)S(1)} %get-tuple-element.53, bf16[1024,768]{1,0:T(8,128)(2,1)S(1)} %bitcast.41, bf16[]{:T(256)} %constant.41.clone.1), kind=kCustom, calls=%fused_computation.5 | custom fusion | bytes 1572866 | tf_op jit(solution)/shard_map/scatter | solution.py:244
  68.0 10.1 %shard_map.127 = (bf16[1024,768]{1,0:T(8,128)(2,1)}, bf16[1024,768]{1,0:T(8,128)(2,1)}, bf16[768,1024]{1,0:T(8,128)(2,1)}, bf16[768,1024]{1,0:T(8,128)(2,1)}, bf...) custom-call(s32[2]{0:T(128)} %pad_add_fusion.len_ref, ...), custom_call_target="tpu_custom_call" | custom-call | flops 4831838208 | bytes 20971520 | tf_op jit(solution)/shard_map/pallas_call | solution.py:154
  78.3 49.7 %all-gather.2.cloned.1.call-done = bf16[512,1536]{1,0:T(8,128)(2,1)} async-done(((bf16[64,1536]{1,0:T(8,128)(2,1)}), bf16[512,1536]{1,0:T(8,128)(2,1)}) %all-gather.2.cloned.1.call-update) | async-done | bytes 1572880 | tf_op jit(solution)/shard_map/all_gather | solution.py:249
  128.0 1.5 fusion.4
  132.1 85.2 %shard_map.128 = (bf16[768,1024]{1,0:T(8,128)(2,1)}, bf16[768,1024]{1,0:T(8,128)(2,1)}, f32[768,1024]{1,0:T(8,128)}, f32[768,1024]{1,0:T(8,128)}, f32[768,512]{1,0:T(8,128)}, /*index=5*/f32[768,512]{1,0:T(8,128)}) custom-call(s32[2]{0:T(128)} %pad_add_fusion.len_ref, bf16[1024,768]{1,0:T(8,128)(2,1)} %get-tuple-element.27.k_ref, ...), custom_call_target="tpu_custom_call" | custom-call | tf_op jit(solution)/shard_map/pallas_call | solution.py:107
  217.2 1.9 copy.38
  219.1 1.9 copy.39
  221.0 2.2 pad_maximum_fusion
  223.5 9.2 %shard_map.129 = (bf16[1024,768]{1,0:T(8,128)(2,1)}, f32[768,768]{1,0:T(8,128)}, f32[768,768]{1,0:T(8,128)}) custom-call(bf16[1024,768]{1,0:T(8,128)(2,1)} %scatter_custom_fusion.x_ref, bf16[1024,768]{1,0:T(8,128)(2,1)} %bitcast.39, bf16[768,1024]{1,0:T(8,128)(2,1)} %get-tuple-element.34.attT_ref, bf16[768,1024]{1,0:T(8,128)(2,1)} %get-tuple-element.35.dqT_ref, ...), custom_call_target="tpu_custom_call" | custom-call | flops 3623878656 | bytes 12582912 | tf_op jit(solution)/shard_map/pallas_call | solution.py:174
  232.7 67.8 %reduce-scatter.2.cloned.1.call-done.back_ref = f32[64,1536]{1,0:T(8,128)} async-done(((f32[512,1536]{1,0:T(8,128)}), f32[64,1536]{1,0:T(8,128)}) %reduce-scatter.2.cloned.1.call-update) | async-done | bytes 393232 | tf_op jit(solution)/shard_map/reduce_scatter | solution.py:253
  300.5 13.6 %shard_map.130 = (bf16[1024,768]{1,0:T(8,128)(2,1)}, f32[768,768]{1,0:T(8,128)}, f32[768,768]{1,0:T(8,128)}) custom-call(bf16[1024,768]{1,0:T(8,128)(2,1)} %scatter_custom_fusion.x_ref, bf16[1024,768]{1,0:T(8,128)(2,1)} %bitcast.40, bf16[768,1024]{1,0:T(8,128)(2,1)} %get-tuple-element.35.dqT_ref, f32[768,1024]{1,0:T(8,128)} %get-tuple-element.37.dkT_ref, ...), custom_call_target="tpu_custom_call" | custom-call | flops 6039797760 | bytes 20971520 | tf_op jit(solution)/shard_map/pallas_call | solution.py:210
  315.5 2.0 copy.37
  317.5 2.0 copy.40
  319.5 159.5 %all-reduce.3.cloned.1.call-done = (f32[768,768]{1,0:T(8,128)}, f32[768,768]{1,0:T(8,128)}, f32[768,768]{1,0:T(8,128)}, f32[768,768]{1,0:T(8,128)}) async-done(((f32[768,768]{1,0:T(8,128)}, f32[768,768]{1,0:T(8,128)}, f32[768,768]{1,0:T(8,128)}, f32[768,768]{1,0:T(8,128)}), (f32[768,768]{1,0:T(8,128)}, f32[768,768]{1,0:T(8,128)}, f32[768,768]{1,0:T(8,128)}, ...) | async-done | bytes 9437200 | tf_op jit(solution)/shard_map/psum | solution.py:258
  479.0 3.4 copy.48
  482.4 1.4 copy.49
  484.9 1.4 copy.50
  (42 shorter events, 12.2 us)
Async XLA Ops:
  7.2 24.8 %copy-start = (bf16[1,1024,768]{2,1,0:T(8,128)(2,1)S(1)}, bf16[1,1024,768]{2,1,0:T(8,128)(2,1)}, u32[]{:S(2)}) copy-start(bf16[1,1024,768]{2,1,0:T(8,128)(2,1)} %param.8) | copy-start | bytes 4718596
  37.4 4.4 copy-start.7
  37.4 24.1 %all-to-all-start.1 = ((bf16[8,128,768]{2,1,0:T(8,128)(2,1)}), bf16[8,128,768]{2,1,0:T(8,128)(2,1)S(1)}, u32[]{:S(2)}, u32[]{:S(2)}) async-start(bf16[8,128,768]{2,1,0:T(8,128)(2,1)} %broadcast_select_fusion), calls=%async_computation.1 | async-start | bytes 3145728 | tf_op jit(solution)/shard_map/all_to_all | solution.py:241
  41.1 86.9 %all-gather.2.cloned.1.call-start = ((), (), s32[]{:S(2)}) async-start(), calls=%async_computation.3 | async-start | bytes 1769472 | tf_op jit(solution)/shard_map/all_gather | solution.py:249
  78.1 222.4 %reduce-scatter.2.cloned.1.call-start = ((), (), s32[]{:S(2)}) async-start(), calls=%async_computation.4 | async-start | bytes 3538944 | tf_op jit(solution)/shard_map/reduce_scatter | solution.py:253
  129.5 2.6 copy-start.2
  129.5 2.6 copy-start.3
  223.2 255.8 %all-reduce.3.cloned.1.call-start = ((), (), s32[]{:S(2)}) async-start(), calls=%async_computation.5 | async-start | bytes 18874368 | tf_op jit(solution)/shard_map/psum | solution.py:258
  314.1 1.4 copy-start.8
  315.5 2.0 copy-start.9
  479.0 3.4 copy-start.6
  482.4 2.5 copy-start.5
  484.9 2.5 copy-start.4
  484.9 3.9 copy-start.1
Sparse Core Ops, SparseCore 0:
  78.2 49.7 all-gather.1
  223.3 77.1 reduce-scatter.1
  314.2 164.7 all-reduce.2

commit v2 on v1

--- a/solution.py
+++ b/solution.py
@@ -218,6 +218,154 @@
     )(x, go, dqT, dkT, dvT, back, wq, wk, wv)
 
 
+MESHID = pl.DeviceIdType.MESH
+ORDERS = ((0, 1, 2), (1, 2, 0), (2, 0, 1))
+
+
+def coords():
+    s = lax.axis_index("seq")
+    r = lax.axis_index("rep")
+    return ((s % 2) * 2 + r // 8, s // 2, (r // 2) % 4), r % 2
+
+
+def device_at(xyz, core):
+    x, y, z = xyz
+    return (y * 2 + x // 2, ((x % 2) * 4 + z) * 2 + core)
+
+
+def along(xyz, axis, step):
+    moved = list(xyz)
+    moved[axis] = (xyz[axis] + step) % 4
+    return tuple(moved)
+
+
+def greet(peers):
+    barrier = pltpu.get_barrier_semaphore()
+    for peer in peers:
+        pl.semaphore_signal(barrier, inc=1, device_id=peer, device_id_type=MESHID)
+    pl.semaphore_wait(barrier, len(peers))
+
+
+def send(src, dst, ssem, rsem, peer):
+    copy = pltpu.make_async_remote_copy(
+        src_ref=src, dst_ref=dst, send_sem=ssem, recv_sem=rsem, device_id=peer, device_id_type=MESHID
+    )
+    copy.start()
+    return copy
+
+
+HALF = D // 2
+
+
+def sum_kernel(gq_ref, gk_ref, gv_ref, go_ref, out_ref, acc, crx, rx1, rx2, rx3, r2, r3,
+               cs, cr, ss, rs, gs, gr, hs, hr):
+    xyz, core = coords()
+    mate = device_at(xyz, 1 - core)
+    greet([mate] + [device_at(along(xyz, a, d), core) for a in range(3) for d in (1, 2, 3)])
+    mine = pl.ds(pl.multiple_of(core * HALF, 128), HALF)
+    theirs = pl.ds(pl.multiple_of((1 - core) * HALF, 128), HALF)
+    grads = (gq_ref, gk_ref, gv_ref, go_ref)
+    pair = [send(g.at[:, theirs], crx.at[i], cs.at[i], cr.at[i], mate) for i, g in enumerate(grads)]
+    for i, g in enumerate(grads):
+        pair[i].wait_recv()
+        acc[i] = g[:, mine] + crx[i]
+    out = []
+    waves = []
+    for p in range(3):
+        axis = ORDERS[p][0]
+        a = xyz[axis]
+        rows = pl.ds(p * 256, 256)
+        waves.append([send(acc.at[(a + d) % 4, rows], rx1.at[p, d - 1], ss.at[0, p, d - 1], rs.at[0, p, d - 1],
+                           device_at(along(xyz, axis, d), core)) for d in (1, 2, 3)])
+    out += waves
+    nxt = []
+    for p in range(3):
+        a = xyz[ORDERS[p][0]]
+        for c in waves[p]:
+            c.wait_recv()
+        r2[p] = acc[a, p * 256:(p + 1) * 256] + rx1[p, 0] + rx1[p, 1] + rx1[p, 2]
+        axis = ORDERS[p][1]
+        b = xyz[axis]
+        nxt.append([send(r2.at[p, pl.ds(pl.multiple_of(((b + d) % 4) * 64, 64), 64)], rx2.at[p, d - 1],
+                         ss.at[1, p, d - 1], rs.at[1, p, d - 1], device_at(along(xyz, axis, d), core))
+                    for d in (1, 2, 3)])
+    out += nxt
+    waves = nxt
+    nxt = []
+    for p in range(3):
+        b = xyz[ORDERS[p][1]]
+        for c in waves[p]:
+            c.wait_recv()
+        r3[p] = r2[p, pl.ds(pl.multiple_of(b * 64, 64), 64)] + rx2[p, 0] + rx2[p, 1] + rx2[p, 2]
+        axis = ORDERS[p][2]
+        e = xyz[axis]
+        nxt.append([send(r3.at[p, pl.ds(pl.multiple_of(((e + d) % 4) * 16, 16), 16)], rx3.at[p, d - 1],
+                         ss.at[2, p, d - 1], rs.at[2, p, d - 1], device_at(along(xyz, axis, d), core))
+                    for d in (1, 2, 3)])
+    out += nxt
+    waves = nxt
+    nxt = []
+
+    def region(p, level):
+        a, b, e = (xyz[ORDERS[p][i]] for i in range(3))
+        if level == 2:
+            return a, pl.ds(pl.multiple_of(p * 256 + b * 64 + e * 16, 16), 16)
+        if level == 1:
+            return a, pl.ds(pl.multiple_of(p * 256 + b * 64, 64), 64)
+        return a, pl.ds(p * 256, 256)
+
+    for level in (2, 1, 0):
+        for p in range(3):
+            for c in waves[p]:
+                c.wait_recv()
+            i, rows = region(p, level)
+            if level == 2:
+                e = xyz[ORDERS[p][2]]
+                total = r3[p, pl.ds(pl.multiple_of(e * 16, 16), 16)] + rx3[p, 0] + rx3[p, 1] + rx3[p, 2]
+                out_ref[i, rows, mine] = total.astype(BF)
+            axis = ORDERS[p][level]
+            here = out_ref.at[i, rows, mine]
+            nxt.append([send(here, here, gs.at[level, p, d - 1], gr.at[level, p, d - 1],
+                             device_at(along(xyz, axis, d), core)) for d in (1, 2, 3)])
+        out += nxt
+        waves = nxt
+        nxt = []
+    for p in range(3):
+        for c in waves[p]:
+            c.wait_recv()
+    last = []
+    for i in range(4):
+        here = out_ref.at[i, :, mine]
+        last.append(send(here, here, hs.at[i], hr.at[i], mate))
+    for c in pair:
+        c.wait_send()
+    for wave in out:
+        for c in wave:
+            c.wait_send()
+    for c in last:
+        c.wait()
+
+
+def sum_all(gq, gk, gv, go):
+    s = jax.ShapeDtypeStruct
+    dma = pltpu.SemaphoreType.DMA
+    return pl.pallas_call(
+        sum_kernel,
+        in_specs=[vm()] * 4,
+        out_specs=vm(),
+        out_shape=s((4, D, D), BF),
+        scratch_shapes=[
+            pltpu.VMEM((4, D, HALF), F32), pltpu.VMEM((4, D, HALF), F32),
+            pltpu.VMEM((3, 3, 256, HALF), F32), pltpu.VMEM((3, 3, 64, HALF), F32),
+            pltpu.VMEM((3, 3, 16, HALF), F32), pltpu.VMEM((3, 256, HALF), F32), pltpu.VMEM((3, 64, HALF), F32),
+            dma((4,)), dma((4,)), dma((3, 3, 3)), dma((3, 3, 3)), dma((3, 3, 3)), dma((3, 3, 3)), dma((4,)), dma((4,)),
+        ],
+        compiler_params=pltpu.CompilerParams(
+            vmem_limit_bytes=56 << 20, collective_id=1, has_side_effects=True),
+        cost_estimate=pl.CostEstimate(flops=1 << 24, bytes_accessed=20 << 20, transcendentals=0),
+    )(gq, gk, gv, go)
+
+
 def to_local(a):
     return a.reshape(64, RATE, -1).transpose(1, 0, 2).reshape(T, -1)
 
@@ -255,7 +403,8 @@
     )
     enc, gq, gout = outer_all(x, go, attT, dqT, w_out)
     emb, gk, gv = final_all(x, go, dqT, dkT, dvT, back, w_query, w_key, w_value)
-    summed = lax.psum((gq, gk, gv, gout), ("seq", "rep"))
+    total = sum_all(gq, gk, gv, gout)
+    summed = [total[i].astype(F32) for i in range(4)]
     return (from_local(enc)[None], from_local(emb)[None], summed[0], summed[1], summed[2], summed[3])
 
 

time: 496 us -> 401 us (0.81)
  waiting for transfers between devices: 295 us -> 132 us
  Pallas kernels: 118 us -> 188 us
  local copies, waits for them, and re-layouts: 40.3 us -> 31.9 us
  other arithmetic: 9.89 us -> 16.2 us
    psum x1 -> x0, waiting for transfers between devices: 160 us -> none  [per_device(): summed = lax.psum((gq, gk, gv, gout), ('seq', 'rep'))]
    pallas_call x0 -> x1, Pallas kernels: none -> 70.5 us  [sum_all(): pl.pallas_call(sum_kernel, in_specs=[vm()] * 4, out_specs=vm(), out_shape...]
    unnamed x27 -> x13, local copies, waits for them, and re-layouts: 14.3 us -> 3.08 us
    convert_element_type x0 -> x1, other arithmetic: none -> 6.3 us  [per_device(): summed = [total[i].astype(F32) for i in range(4)]]
  transfers between devices with their start and end apart: 4 -> 3, of which waited for: 4 -> 3; matrix products, arithmetic and copies ran while one was open for 1% -> 1% of each run, Pallas kernels for 2% -> 2%
where the time goes in v2:
time: 401 us
  Pallas kernels  188 us (47%)
  waiting for transfers between devices  132 us (33%)
  local copies, waits for them, and re-layouts  31.9 us (8%)
  other arithmetic  16.2 us (4%)
  between operations  14.8 us (4%)
  blocking collectives  13.8 us (3%)
    pallas_call x1, Pallas kernels, attn(): pl.pallas_call(attn_kernel, grid=(HEADS,), in_specs=[pl.BlockSpec(memory_...  85.2 us
    pallas_call x1, Pallas kernels, sum_all(): pl.pallas_call(sum_kernel, in_specs=[vm()] * 4, out_specs=vm(), out_shape...  70.5 us
    reduce_scatter x1, waiting for transfers between devices, per_device(): lax.psum_scatter(jnp.concatenate([dkfT.T, dvfT.T], axis=1), 'seq', scatte...  64.6 us
    all_gather x1, waiting for transfers between devices, per_device(): farall = lax.all_gather(far, 'seq', axis=0, tiled=True)  49.7 us
    all_to_all x1, waiting for transfers between devices, per_device(): lax.all_to_all(picked, 'seq', split_axis=0, concat_axis=0, tiled=True)  17.4 us
    all_to_all x1, blocking collectives, per_device(): lax.all_to_all(wanted, 'seq', split_axis=0, concat_axis=0, tiled=True)  13.8 us
    pallas_call x1, Pallas kernels, final_all(): pl.pallas_call(final_kernel, in_specs=[vm()] * 9, out_specs=[vm()] * 3, o...  13.6 us
    pallas_call x1, Pallas kernels, project_all(): pl.pallas_call(project_kernel, in_specs=[sm()] + [vm()] * 6, out_specs=[v...  10.1 us
  transfers between devices with their start and end apart: 3, of which 3 were waited for; matrix products, arithmetic and copies ran while one was open for 1% of the time, Pallas kernels for 2%

profile of v2, /device:TPU:1, one launch (start us, length us, event | category | flops | bytes accessed | tf_op | source)
XLA Modules:
  0.0 401.0 jit_solution(98563923418559732)
XLA Ops:
  9.3 4.4 %sort.17 = (s32[1024]{0:T(1024)}, s32[1024]{0:T(1024)S(1)}) sort(s32[1024]{0:T(1024)S(1)} %get-tuple-element.55, s32[1024]{0:T(1024)S(1)} %iota.4), dimensions={0}, to_apply=%region_0.1 | sort | flops 10240 | bytes 16384 | tf_op jit(solution)/shard_map/jit(argsort)/sort | solution.py:385
  13.7 4.5 %gather_fusion = s32[1024]{0:T(1024)S(1)} fusion(s32[1024]{0:T(1024)S(1)} %get-tuple-element.54, s32[1024]{0:T(1024)S(1)} %get-tuple-element.52), kind=kCustom, calls=%fused_computation | custom fusion | bytes 12288 | tf_op jit(solution)/shard_map/gather | solution.py:386
  18.2 13.8 %all_to_all.14 = s32[8,1,128]{2,1,0:T(1,128)S(1)} all-to-all(s32[8,1,128]{2,1,0:T(1,128)S(1)} %bitcast.61), channel_id=1, replica_groups=mesh['seq'=8,'rep'=16] {'seq'}, dimensions={0} | all-to-all | bytes 8192 | tf_op jit(solution)/shard_map/all_to_all | solution.py:387
  32.0 4.0 gather_fusion.1
  36.0 1.4 broadcast_select_fusion
  37.4 3.7 all-to-all-start.1
  41.8 1.6 copy.32
  44.1 17.4 %all-to-all-done.1 = bf16[8,128,768]{2,1,0:T(8,128)(2,1)S(1)} async-done(((bf16[8,128,768]{2,1,0:T(8,128)(2,1)}), bf16[8,128,768]{2,1,0:T(8,128)(2,1)S(1)}, u32[]{:S(2)}, u32[]{:S(2)}) %all-to-all-start.1) | async-done | bytes 1572896 | tf_op jit(solution)/shard_map/all_to_all | solution.py:389
  61.5 6.4 %scatter_custom_fusion.x_ref = bf16[1024,768]{1,0:T(8,128)(2,1)} fusion(s32[1024]{0:T(1024)S(1)} %get-tuple-element.53, bf16[1024,768]{1,0:T(8,128)(2,1)S(1)} %bitcast.54, bf16[]{:T(256)} %constant.41.clone.1), kind=kCustom, calls=%fused_computation.9 | custom fusion | bytes 1572866 | tf_op jit(solution)/shard_map/scatter | solution.py:392
  68.0 10.1 %shard_map.127 = (bf16[1024,768]{1,0:T(8,128)(2,1)}, bf16[1024,768]{1,0:T(8,128)(2,1)}, bf16[768,1024]{1,0:T(8,128)(2,1)}, bf16[768,1024]{1,0:T(8,128)(2,1)}, bf...) custom-call(s32[2]{0:T(128)} %pad_add_fusion.len_ref, ...), custom_call_target="tpu_custom_call" | custom-call | flops 4831838208 | bytes 20971520 | tf_op jit(solution)/shard_map/pallas_call | solution.py:154
  78.3 49.7 %all-gather.2.cloned.1.call-done = bf16[512,1536]{1,0:T(8,128)(2,1)} async-done(((bf16[64,1536]{1,0:T(8,128)(2,1)}), bf16[512,1536]{1,0:T(8,128)(2,1)}) %all-gather.2.cloned.1.call-update) | async-done | bytes 1572880 | tf_op jit(solution)/shard_map/all_gather | solution.py:397
  128.0 1.5 fusion.4
  129.5 1.4 copy.42
  132.0 85.2 %shard_map.128 = (bf16[768,1024]{1,0:T(8,128)(2,1)}, bf16[768,1024]{1,0:T(8,128)(2,1)}, f32[768,1024]{1,0:T(8,128)}, f32[768,1024]{1,0:T(8,128)}, f32[768,512]{1,0:T(8,128)}, /*index=5*/f32[768,512]{1,0:T(8,128)}) custom-call(s32[2]{0:T(128)} %pad_add_fusion.len_ref, bf16[1024,768]{1,0:T(8,128)(2,1)} %get-tuple-element.27.k_ref, ...), custom_call_target="tpu_custom_call" | custom-call | tf_op jit(solution)/shard_map/pallas_call | solution.py:107
  217.2 1.9 copy.38
  219.1 1.9 copy.39
  220.9 2.2 pad_maximum_fusion
  223.1 9.2 %shard_map.129 = (bf16[1024,768]{1,0:T(8,128)(2,1)}, f32[768,768]{1,0:T(8,128)}, f32[768,768]{1,0:T(8,128)}) custom-call(bf16[1024,768]{1,0:T(8,128)(2,1)} %scatter_custom_fusion.x_ref, bf16[1024,768]{1,0:T(8,128)(2,1)} %bitcast.51, bf16[768,1024]{1,0:T(8,128)(2,1)} %get-tuple-element.34.attT_ref, bf16[768,1024]{1,0:T(8,128)(2,1)} %get-tuple-element.35.dqT_ref, ...), custom_call_target="tpu_custom_call" | custom-call | flops 3623878656 | bytes 12582912 | tf_op jit(solution)/shard_map/pallas_call | solution.py:174
  232.3 3.4 copy.37
  235.8 64.6 %reduce-scatter.2.cloned.1.call-done.back_ref = f32[64,1536]{1,0:T(8,128)} async-done(((f32[512,1536]{1,0:T(8,128)}), f32[64,1536]{1,0:T(8,128)}) %reduce-scatter.2.cloned.1.call-update) | async-done | bytes 393232 | tf_op jit(solution)/shard_map/reduce_scatter | solution.py:401
  300.4 13.6 %shard_map.130 = (bf16[1024,768]{1,0:T(8,128)(2,1)}, f32[768,768]{1,0:T(8,128)}, f32[768,768]{1,0:T(8,128)}) custom-call(bf16[1024,768]{1,0:T(8,128)(2,1)} %scatter_custom_fusion.x_ref, bf16[1024,768]{1,0:T(8,128)(2,1)} %bitcast.52, bf16[768,1024]{1,0:T(8,128)(2,1)} %get-tuple-element.35.dqT_ref, f32[768,1024]{1,0:T(8,128)} %get-tuple-element.37.dkT_ref, ...), custom_call_target="tpu_custom_call" | custom-call | flops 6039797760 | bytes 20971520 | tf_op jit(solution)/shard_map/pallas_call | solution.py:210
  314.0 3.4 copy.40
  317.4 70.5 %shard_map.131 = bf16[4,768,768]{2,1,0:T(8,128)(2,1)} custom-call(f32[768,768]{1,0:T(8,128)} %get-tuple-element.42.gq_ref, f32[768,768]{1,0:T(8,128)} %get-tuple-element.43.gk_ref, f32[768,768]{1,0:T(8,128)} %get-tuple-element.44.gv_ref, f32[768,768]{1,0:T(8,128)} %get-tuple-element.45.go_ref), custom_call_target="tpu_custom_call" | custom-call | flops 16777216 | bytes 20971520 | tf_op jit(solution)/shard_map/pallas_call | solution.py:352
  387.9 6.3 %bitcast_convert_fusion = (f32[768,768]{1,0:T(8,128)}, f32[768,768]{1,0:T(8,128)}, f32[768,768]{1,0:T(8,128)}, f32[768,768]{1,0:T(8,128)}) fusion(bf16[4,768,768]{2,1,0:T(8,128)(2,1)} %shard_map.131), kind=kLoop, calls=%fused_computation.5 | loop fusion | flops 2359296 | bytes 14155776 | tf_op jit(solution)/shard_map/convert_element_type | solution.py:407
  (27 shorter events, 4.3 us)
Async XLA Ops:
  7.2 24.8 %copy-start = (bf16[1,1024,768]{2,1,0:T(8,128)(2,1)S(1)}, bf16[1,1024,768]{2,1,0:T(8,128)(2,1)}, u32[]{:S(2)}) copy-start(bf16[1,1024,768]{2,1,0:T(8,128)(2,1)} %param.8) | copy-start | bytes 4718596
  37.4 4.4 %copy-start.4 = (bf16[1,1024,768]{2,1,0:T(8,128)(2,1)S(1)}, bf16[1,1024,768]{2,1,0:T(8,128)(2,1)}, u32[]{:S(2)}) copy-start(bf16[1,1024,768]{2,1,0:T(8,128)(2,1)} %param.11) | copy-start | bytes 4718596
  37.4 24.1 %all-to-all-start.1 = ((bf16[8,128,768]{2,1,0:T(8,128)(2,1)}), bf16[8,128,768]{2,1,0:T(8,128)(2,1)S(1)}, u32[]{:S(2)}, u32[]{:S(2)}) async-start(bf16[8,128,768]{2,1,0:T(8,128)(2,1)} %broadcast_select_fusion), calls=%async_computation.1 | async-start | bytes 3145728 | tf_op jit(solution)/shard_map/all_to_all | solution.py:389
  41.1 86.8 %all-gather.2.cloned.1.call-start = ((), (), s32[]{:S(2)}) async-start(), calls=%async_computation.3 | async-start | bytes 1769472 | tf_op jit(solution)/shard_map/all_gather | solution.py:397
  78.0 222.4 %reduce-scatter.2.cloned.1.call-start = ((), (), s32[]{:S(2)}) async-start(), calls=%async_computation.4 | async-start | bytes 3538944 | tf_op jit(solution)/shard_map/reduce_scatter | solution.py:401
  129.4 2.6 copy-start.2
  129.5 2.6 copy-start.3
  387.9 6.3 %copy-start.1 = (bf16[1,1024,768]{2,1,0:T(8,128)(2,1)S(1)}, bf16[1,1024,768]{2,1,0:T(8,128)(2,1)}, u32[]{:S(2)}) copy-start(bf16[1,1024,768]{2,1,0:T(8,128)(2,1)} %param.8) | copy-start | bytes 4718596
Sparse Core Ops, SparseCore 0:
  78.2 49.7 all-gather.1
  223.2 77.1 reduce-scatter.1

commit v3 on v2

--- a/solution.py
+++ b/solution.py
@@ -16,7 +16,7 @@
 def nn(a,b): return lax.dot_general(a,b,(((1,),(0,)),((),())),preferred_element_type=F32)
 def nt(a,b): return lax.dot_general(a,b,(((1,),(1,)),((),())),preferred_element_type=F32)
 
-def attn_kernel(len_ref, k_ref, v_ref, qT_ref, kT_ref, vT_ref, gT_ref, kf_ref, vf_ref, kfT_ref, vfT_ref,
+def attn_kernel(len_ref, k_ref, v_ref, qT_ref, kT_ref, vT_ref, gT_ref, far_ref, kfT_ref, vfT_ref,
                 attT_ref, dqT_ref, dkT_ref, dvT_ref, dkfT_ref, dvfT_ref,
                 qpad, gpad, kb, kfb, m2s, l2s, u2s, w2s, des, dqs, e2s):
     h = pl.program_id(0)
@@ -44,7 +44,7 @@
     fi = lax.broadcasted_iota(jnp.int32, (FAR, 1), 0)
     fbias = jnp.where(fi * RATE + h < nfull, 0.0, NEG).astype(BF)
     flane = lax.broadcasted_iota(jnp.int32, (FAR, 256), 1)
-    kfb[...] = jnp.where(flane == free, fbias, kf_ref[:, pl.ds(w0, 256)])
+    kfb[...] = jnp.where(flane == free, fbias, far_ref[:, pl.ds(w0, 256)])
     wq = pl.multiple_of((h // 2) * 128, 128)
     qlane = lax.broadcasted_iota(jnp.int32, (1, 128), 1)
     mine = (qlane // 64) == lax.rem(h, 2)
@@ -95,10 +95,10 @@
     dvT_ref[pl.ds(r, HD), :] = dv
     dkT_ref[pl.ds(r, HD), :] = dk * scale
     P2 = e2s[...] * jnp.where(mine, w2s[:, pl.ds(wq, 128)], 0.0)
-    dP2 = nn(vf_ref[:, pl.ds(w0, 256)], gpad[:, pl.ds(wq, 128)])
+    dP2 = nn(far_ref[:, pl.ds(pl.multiple_of(w0 + D, 128), 256)], gpad[:, pl.ds(wq, 128)])
     dS2 = (P2 * (dP2 - des[:, pl.ds(wq, 128)])).astype(BF)
-    dvfT_ref[pl.ds(r, HD), :] = nt(gT_ref[pl.ds(r, HD), pl.ds(wq, 128)], P2.astype(BF))
-    dkfT_ref[pl.ds(r, HD), :] = nt(qT_ref[pl.ds(r, HD), pl.ds(wq, 128)], dS2) * scale
+    dvfT_ref[pl.ds(r, HD), :] = nt(gT_ref[pl.ds(r, HD), pl.ds(wq, 128)], P2.astype(BF)).astype(BF)
+    dkfT_ref[pl.ds(r, HD), :] = (nt(qT_ref[pl.ds(r, HD), pl.ds(wq, 128)], dS2) * scale).astype(BF)
     dqs[:, pl.ds(wq, 128)] += nn(kfT_ref[pl.ds(r, HD), :], dS2)
     dqT_ref[pl.ds(r, HD), :] = (dqs[...] * scale).astype(BF)
 
@@ -106,10 +106,10 @@
     vm = pl.BlockSpec(memory_space=pltpu.VMEM)
     return pl.pallas_call(
         attn_kernel, grid=(HEADS,),
-        in_specs=[pl.BlockSpec(memory_space=pltpu.SMEM)] + [vm]*10,
+        in_specs=[pl.BlockSpec(memory_space=pltpu.SMEM)] + [vm]*9,
         out_specs=[vm]*6,
         out_shape=[jax.ShapeDtypeStruct((D,T),BF), jax.ShapeDtypeStruct((D,T),BF), jax.ShapeDtypeStruct((D,T),F32), jax.ShapeDtypeStruct((D,T),F32),
-                   jax.ShapeDtypeStruct((D,FAR),F32), jax.ShapeDtypeStruct((D,FAR),F32)],
+                   jax.ShapeDtypeStruct((D,FAR),BF), jax.ShapeDtypeStruct((D,FAR),BF)],
         scratch_shapes=[pltpu.VMEM((256,T),BF), pltpu.VMEM((256,T),BF), pltpu.VMEM((T,256),BF), pltpu.VMEM((FAR,256),BF),
                         pltpu.VMEM((1,T),F32), pltpu.VMEM((1,T),F32), pltpu.VMEM((HD,T),F32), pltpu.VMEM((1,T),F32), pltpu.VMEM((1,T),F32),
                         pltpu.VMEM((HD,T),F32), pltpu.VMEM((FAR,128),F32)],
@@ -123,99 +123,6 @@
 
 def sm():
     return pl.BlockSpec(memory_space=pltpu.SMEM)
-
-
-def project_kernel(len_ref, x_ref, go_ref, wq_ref, wk_ref, wv_ref, wo_ref,
-                   k_ref, v_ref, qT_ref, kT_ref, vT_ref, gT_ref, far_ref):
-    n = len_ref[0]
-    x = x_ref[...]
-    k = nn(x, wk_ref[...]).astype(BF)
-    v = nn(x, wv_ref[...]).astype(BF)
-    k_ref[...] = k
-    v_ref[...] = v
-    qT_ref[...] = nn(x, wq_ref[...]).astype(BF).T
-    kT_ref[...] = k.T
-    vT_ref[...] = v.T
-    qi = lax.broadcasted_iota(jnp.int32, (1, T), 1)
-    ok = (lax.rem(qi, 64) * RATE + qi // 64) < n
-    gT_ref[...] = jnp.where(ok, nt(wo_ref[...], go_ref[...]), 0.0).astype(BF)
-    col = lax.broadcasted_iota(jnp.int32, (64, D), 1) // HD
-    fk = jnp.zeros((64, D), BF)
-    fv = jnp.zeros((64, D), BF)
-    for h in range(HEADS):
-        fk = jnp.where(col == h, k_ref[h * 64:(h + 1) * 64, :], fk)
-        fv = jnp.where(col == h, v_ref[h * 64:(h + 1) * 64, :], fv)
-    far_ref[:, :D] = fk
-    far_ref[:, D:] = fv
-
-
-def project_all(lens, x, go, wq, wk, wv, wo):
-    s = jax.ShapeDtypeStruct
-    return pl.pallas_call(
-        project_kernel,
-        in_specs=[sm()] + [vm()] * 6,
-        out_specs=[vm()] * 7,
-        out_shape=[s((T, D), BF)] * 2 + [s((D, T), BF)] * 4 + [s((64, 2 * D), BF)],
-        compiler_params=pltpu.CompilerParams(vmem_limit_bytes=60 << 20),
-        cost_estimate=pl.CostEstimate(flops=8 * T * D * D, bytes_accessed=20 << 20, transcendentals=0),
-    )(lens, x, go, wq, wk, wv, wo)
-
-
-def outer_kernel(x_ref, go_ref, attT_ref, dqT_ref, wo_ref, enc_ref, gq_ref, go_out_ref):
-    x = x_ref[...]
-    att = attT_ref[...].T
-    enc_ref[...] = (x.astype(F32) + nn(att, wo_ref[...])).astype(BF)
-    go_out_ref[...] = nn(attT_ref[...], go_ref[...])
-    gq_ref[...] = nt(x.T, dqT_ref[...])
-
-
-def outer_all(x, go, attT, dqT, wo):
-    s = jax.ShapeDtypeStruct
-    return pl.pallas_call(
-        outer_kernel,
-        in_specs=[vm()] * 5,
-        out_specs=[vm()] * 3,
-        out_shape=[s((T, D), BF), s((D, D), F32), s((D, D), F32)],
-        compiler_params=pltpu.CompilerParams(vmem_limit_bytes=60 << 20),
-        cost_estimate=pl.CostEstimate(flops=6 * T * D * D, bytes_accessed=12 << 20, transcendentals=0),
-    )(x, go, attT, dqT, wo)
-
-
-def final_kernel(x_ref, go_ref, dqT_ref, dkT_ref, dvT_ref, back_ref, wq_ref, wk_ref, wv_ref,
-                 emb_ref, gk_ref, gv_ref, dkT_s, dvT_s):
-    bT = back_ref[...].T
-    dkT_s[...] = dkT_ref[...]
-    dvT_s[...] = dvT_ref[...]
-    zero = jnp.zeros((HD, 64), F32)
-    for h in range(HEADS):
-        r = slice(h * HD, (h + 1) * HD)
-        w = slice((h // 2) * 128, (h // 2) * 128 + 128)
-        bk = bT[h * HD:(h + 1) * HD, :]
-        bv = bT[D + h * HD:D + (h + 1) * HD, :]
-        pk = [bk, zero] if h % 2 == 0 else [zero, bk]
-        pv = [bv, zero] if h % 2 == 0 else [zero, bv]
-        dkT_s[r, w] += jnp.concatenate(pk, axis=1)
-        dvT_s[r, w] += jnp.concatenate(pv, axis=1)
-    dk = dkT_s[...].astype(BF)
-    dv = dvT_s[...].astype(BF)
-    e = nn(wq_ref[...], dqT_ref[...]) + nn(wk_ref[...], dk) + nn(wv_ref[...], dv)
-    emb_ref[...] = (go_ref[...].astype(F32) + e.T).astype(BF)
-    xT = x_ref[...].T
-    gk_ref[...] = nt(xT, dk)
-    gv_ref[...] = nt(xT, dv)
-
-
-def final_all(x, go, dqT, dkT, dvT, back, wq, wk, wv):
-    s = jax.ShapeDtypeStruct
-    return pl.pallas_call(
-        final_kernel,
-        in_specs=[vm()] * 9,
-        out_specs=[vm()] * 3,
-        out_shape=[s((T, D), BF), s((D, D), F32), s((D, D), F32)],
-        scratch_shapes=[pltpu.VMEM((D, T), F32)] * 2,
-        compiler_params=pltpu.CompilerParams(vmem_limit_bytes=60 << 20),
-        cost_estimate=pl.CostEstimate(flops=10 * T * D * D, bytes_accessed=20 << 20, transcendentals=0),
-    )(x, go, dqT, dkT, dvT, back, wq, wk, wv)
 
 
 MESHID = pl.DeviceIdType.MESH
@@ -366,6 +273,154 @@
     )(gq, gk, gv, go)
 
 
+def seq_peer(s, d):
+    return (lax.rem(s + d, 8), lax.axis_index("rep"))
+
+
+def front_kernel(len_ref, src_ref, rows_ref, go_ref, wq_ref, wk_ref, wv_ref, wo_ref,
+                 x_ref, k_ref, v_ref, qT_ref, kT_ref, vT_ref, gT_ref, far_ref, kfT_ref, vfT_ref,
+                 ask, req, picked, arrived, perm, qs, qr, ps, pr, fs, fr):
+    n = len_ref[0]
+    s = lax.axis_index("seq")
+    peers = [seq_peer(s, d) for d in range(1, 8)]
+    greet(peers)
+    src = src_ref[...]
+    owner = src // T
+    line = src - owner * T
+    hot = (lax.broadcasted_iota(jnp.int32, (16, T), 0) == owner).astype(BF)
+    before = (lax.broadcasted_iota(jnp.int32, (T, T), 0) < lax.broadcasted_iota(jnp.int32, (T, T), 1)).astype(BF)
+    rank = jnp.sum(nn(hot, before) * hot.astype(F32), axis=0, keepdims=True)
+    slot = owner.astype(F32) * 128.0 + rank
+    where = lax.broadcasted_iota(jnp.int32, (T, T), 0).astype(F32)
+    permT = (where == slot).astype(BF)
+    high = line // 32
+    low = line - high * 32
+    eight = lax.broadcasted_iota(jnp.int32, (16, T), 0)
+    parts = jnp.where(eight == 0, high, jnp.where(eight == 1, low, 0)).astype(F32).astype(BF)
+    got = nt(parts, permT)
+    lines = got[0:1] * 32.0 + got[1:2]
+    for o in range(8):
+        ask[o] = jnp.broadcast_to(lines[:, o * 128:(o + 1) * 128], (8, 128))
+    asks = [send(ask.at[lax.rem(s + d, 8)], req.at[d - 1], qs.at[d - 1], qr.at[d - 1], peers[d - 1])
+            for d in range(1, 8)]
+    perm[...] = permT.T
+    qi = lax.broadcasted_iota(jnp.int32, (1, T), 1)
+    ok = (lax.rem(qi, 64) * RATE + qi // 64) < n
+    gT_ref[...] = jnp.where(ok, nt(wo_ref[...], go_ref[...]), 0.0).astype(BF)
+    cells = lax.broadcasted_iota(jnp.int32, (128, T), 1).astype(F32)
+    rows = rows_ref[...]
+    mine = pl.ds(pl.multiple_of(s * 128, 128), 128)
+    sends = []
+    for d in range(1, 8):
+        asks[d - 1].wait_recv()
+        pick = (cells == req[d - 1].T[:, 0:1]).astype(BF)
+        picked[d - 1] = nn(pick, rows).astype(BF)
+        sends.append(send(picked.at[d - 1], arrived.at[mine], ps.at[d - 1], pr.at[d - 1], seq_peer(s, 8 - d)))
+    pick = (cells == ask[s].T[:, 0:1]).astype(BF)
+    arrived[mine, :] = nn(pick, rows).astype(BF)
+    for c in sends:
+        c.wait_recv()
+    x = nn(perm[...], arrived[...]).astype(BF)
+    x_ref[...] = x
+    k = nn(x, wk_ref[...]).astype(BF)
+    v = nn(x, wv_ref[...]).astype(BF)
+    k_ref[...] = k
+    v_ref[...] = v
+    col = lax.broadcasted_iota(jnp.int32, (64, D), 1) // HD
+    fk = jnp.zeros((64, D), BF)
+    fv = jnp.zeros((64, D), BF)
+    for h in range(HEADS):
+        fk = jnp.where(col == h, k_ref[h * 64:(h + 1) * 64, :], fk)
+        fv = jnp.where(col == h, v_ref[h * 64:(h + 1) * 64, :], fv)
+    here = pl.ds(pl.multiple_of(s * 64, 64), 64)
+    far_ref[here, 0:D] = fk
+    far_ref[here, D:2 * D] = fv
+    fars = [send(far_ref.at[here], far_ref.at[here], fs.at[d - 1], fr.at[d - 1], peers[d - 1]) for d in range(1, 8)]
+    qT_ref[...] = nn(x, wq_ref[...]).astype(BF).T
+    kT_ref[...] = k.T
+    vT_ref[...] = v.T
+    for c in fars:
+        c.wait_recv()
+    kfT_ref[...] = far_ref[:, 0:D].T
+    vfT_ref[...] = far_ref[:, D:2 * D].T
+    for c in asks + sends + fars:
+        c.wait_send()
+
+
+def front_all(lens, src, rows, go, wq, wk, wv, wo):
+    s = jax.ShapeDtypeStruct
+    dma = pltpu.SemaphoreType.DMA
+    return pl.pallas_call(
+        front_kernel,
+        in_specs=[sm()] + [vm()] * 7,
+        out_specs=[vm()] * 10,
+        out_shape=[s((T, D), BF)] * 3 + [s((D, T), BF)] * 4 + [s((FAR, 2 * D), BF)] + [s((D, FAR), BF)] * 2,
+        scratch_shapes=[
+            pltpu.VMEM((8, 8, 128), F32), pltpu.VMEM((7, 8, 128), F32), pltpu.VMEM((7, 128, D), BF),
+            pltpu.VMEM((T, D), BF), pltpu.VMEM((T, T), BF),
+        ] + [dma((7,))] * 6,
+        compiler_params=pltpu.CompilerParams(
+            vmem_limit_bytes=60 << 20, collective_id=2, has_side_effects=True),
+        cost_estimate=pl.CostEstimate(flops=12 * T * D * D, bytes_accessed=20 << 20, transcendentals=0),
+    )(lens, src, rows, go, wq, wk, wv, wo)
+
+
+def tail_kernel(x_ref, go_ref, attT_ref, dqT_ref, dkT_ref, dvT_ref, dkfT_ref, dvfT_ref, wq_ref, wk_ref, wv_ref, wo_ref,
+                enc_ref, emb_ref, gq_ref, gk_ref, gv_ref, gout_ref, part, rx, dk_s, dv_s, ss, rs):
+    s = lax.axis_index("seq")
+    peers = [seq_peer(s, d) for d in range(1, 8)]
+    greet(peers)
+    part[:, 0:D] = dkfT_ref[...].T
+    part[:, D:2 * D] = dvfT_ref[...].T
+    backs = [send(part.at[pl.ds(pl.multiple_of(lax.rem(s + d, 8) * 64, 64), 64)], rx.at[d - 1],
+                  ss.at[d - 1], rs.at[d - 1], peers[d - 1]) for d in range(1, 8)]
+    xT = x_ref[...].T
+    gq_ref[...] = nt(xT, dqT_ref[...])
+    gout_ref[...] = nn(attT_ref[...], go_ref[...])
+    enc_ref[...] = (x_ref[...].astype(F32) + nn(attT_ref[...].T, wo_ref[...])).astype(BF)
+    back = part[pl.ds(pl.multiple_of(s * 64, 64), 64), :].astype(F32)
+    for d in range(1, 8):
+        backs[d - 1].wait_recv()
+        back = back + rx[d - 1].astype(F32)
+    bT = back.T
+    zero = jnp.zeros((HD, 64), F32)
+    for h in range(HEADS):
+        r = slice(h * HD, (h + 1) * HD)
+        w = slice((h // 2) * 128, (h // 2) * 128 + 128)
+        bk = bT[h * HD:(h + 1) * HD, :]
+        bv = bT[D + h * HD:D + (h + 1) * HD, :]
+        pk = [bk, zero] if h % 2 == 0 else [zero, bk]
+        pv = [bv, zero] if h % 2 == 0 else [zero, bv]
+        dk_s[r, :] = dkT_ref[r, :].astype(BF)
+        dv_s[r, :] = dvT_ref[r, :].astype(BF)
+        dk_s[r, w] = (dkT_ref[r, w] + jnp.concatenate(pk, axis=1)).astype(BF)
+        dv_s[r, w] = (dvT_ref[r, w] + jnp.concatenate(pv, axis=1)).astype(BF)
+    gk_ref[...] = nt(xT, dk_s[...])
+    gv_ref[...] = nt(xT, dv_s[...])
+    e = nn(wq_ref[...], dqT_ref[...]) + nn(wk_ref[...], dk_s[...]) + nn(wv_ref[...], dv_s[...])
+    emb_ref[...] = (go_ref[...].astype(F32) + e.T).astype(BF)
+    for c in backs:
+        c.wait_send()
+
+
+def tail_all(*args):
+    s = jax.ShapeDtypeStruct
+    dma = pltpu.SemaphoreType.DMA
+    return pl.pallas_call(
+        tail_kernel,
+        in_specs=[vm()] * 12,
+        out_specs=[vm()] * 6,
+        out_shape=[s((T, D), BF)] * 2 + [s((D, D), F32)] * 4,
+        scratch_shapes=[
+            pltpu.VMEM((FAR, 2 * D), BF), pltpu.VMEM((7, 64, 2 * D), BF),
+            pltpu.VMEM((D, T), BF), pltpu.VMEM((D, T), BF), dma((7,)), dma((7,)),
+        ],
+        compiler_params=pltpu.CompilerParams(
+            vmem_limit_bytes=60 << 20, collective_id=3, has_side_effects=True),
+        cost_estimate=pl.CostEstimate(flops=16 * T * D * D, bytes_accessed=30 << 20, transcendentals=0),
+    )(*args)
+
+
 def to_local(a):
     return a.reshape(64, RATE, -1).transpose(1, 0, 2).reshape(T, -1)
 
@@ -375,34 +430,17 @@
 
 
 def per_device(tile_embed, tile_source, slide_len, grad_out, w_query, w_key, w_value, w_out):
-    owned_rows = tile_embed[0]
-    source = to_local(tile_source[0]).reshape(-1)
-    row_count, features = owned_rows.shape
-    stripes = lax.axis_size("seq")
-    stripe = lax.axis_index("seq")
-    portion = row_count // stripes
-    owner_dev = source // row_count
-    ordering = jnp.argsort(owner_dev, stable=True)
-    wanted = (source % row_count)[ordering].reshape(stripes, portion)
-    requested = lax.all_to_all(wanted, "seq", split_axis=0, concat_axis=0, tiled=True)
-    picked = jnp.take(owned_rows, requested.reshape(-1), axis=0).reshape(stripes, portion, features)
-    arrived = lax.all_to_all(picked, "seq", split_axis=0, concat_axis=0, tiled=True).reshape(
-        row_count, features
+    source = to_local(tile_source[0]).reshape(1, T)
+    length = slide_len[0]
+    lens = jnp.stack([length - lax.axis_index("seq") * T, length]).astype(jnp.int32)
+    go = to_local(grad_out[0])
+    x, k, v, qT, kT, vT, gT, far, kfT, vfT = front_all(
+        lens, source, tile_embed[0], go, w_query, w_key, w_value, w_out
     )
-    x = jnp.zeros_like(arrived).at[ordering].set(arrived)
-    length = slide_len[0]
-    lens = jnp.stack([length - stripe * row_count, length]).astype(jnp.int32)
-    go = to_local(grad_out[0])
-    k, v, qT, kT, vT, gT, far = project_all(lens, x, go, w_query, w_key, w_value, w_out)
-    farall = lax.all_gather(far, "seq", axis=0, tiled=True)
-    kf = farall[:, :D]
-    vf = farall[:, D:]
-    attT, dqT, dkT, dvT, dkfT, dvfT = attn(lens, k, v, qT, kT, vT, gT, kf, vf, kf.T, vf.T)
-    back = lax.psum_scatter(
-        jnp.concatenate([dkfT.T, dvfT.T], axis=1), "seq", scatter_dimension=0, tiled=True
+    attT, dqT, dkT, dvT, dkfT, dvfT = attn(lens, k, v, qT, kT, vT, gT, far, kfT, vfT)
+    enc, emb, gq, gk, gv, gout = tail_all(
+        x, go, attT, dqT, dkT, dvT, dkfT, dvfT, w_query, w_key, w_value, w_out
     )
-    enc, gq, gout = outer_all(x, go, attT, dqT, w_out)
-    emb, gk, gv = final_all(x, go, dqT, dkT, dvT, back, w_query, w_key, w_value)
     total = sum_all(gq, gk, gv, gout)
     summed = [total[i].astype(F32) for i in range(4)]
     return (from_local(enc)[None], from_local(emb)[None], summed[0], summed[1], summed[2], summed[3])

time: 401 us -> 283 us (0.71)
  waiting for transfers between devices: 132 us -> 0 us
  Pallas kernels: 188 us -> 263 us
  local copies, waits for them, and re-layouts: 31.9 us -> 10.1 us
  blocking collectives: 13.8 us -> 0 us
  between operations: 14.8 us -> 1.32 us
  other arithmetic: 16.2 us -> 8.11 us
    pallas_call x3 -> x2, Pallas kernels: 32.9 us -> 107 us  [the longest x1 64.2 us: front_all(): pl.pallas_call(front_kernel, in_specs=[sm()] + [vm()] * 7, out_specs=[vm(...]
    reduce_scatter x1 -> x0, waiting for transfers between devices: 64.6 us -> none  [per_device(): lax.psum_scatter(jnp.concatenate([dkfT.T, dvfT.T], axis=1), 'seq', scatte...]
    all_gather x1 -> x0, waiting for transfers between devices: 49.7 us -> none  [per_device(): farall = lax.all_gather(far, 'seq', axis=0, tiled=True)]
    all_to_all x1 -> x0, waiting for transfers between devices: 17.4 us -> none  [per_device(): lax.all_to_all(picked, 'seq', split_axis=0, concat_axis=0, tiled=True)]
    all_to_all x1 -> x0, blocking collectives: 13.8 us -> none  [per_device(): lax.all_to_all(wanted, 'seq', split_axis=0, concat_axis=0, tiled=True)]
    gather x2 -> x0, local copies, waits for them, and re-layouts: 8.53 us -> none  [the longest x1 4.52 us: per_device(): wanted = (source % row_count)[ordering].reshape(stripes, portion)]
    scatter x1 -> x0, local copies, waits for them, and re-layouts: 6.44 us -> none  [per_device(): x = jnp.zeros_like(arrived).at[ordering].set(arrived)]
    sort x1 -> x0, other arithmetic: 4.37 us -> none  [per_device(): ordering = jnp.argsort(owner_dev, stable=True)]
  transfers between devices with their start and end apart: 3 -> 0, of which waited for: 3 -> 0; matrix products, arithmetic and copies ran while one was open for 1% -> 0% of each run, Pallas kernels for 2% -> 0%
where the time goes in v3:
time: 283 us; the launch traced here: 282 us
  Pallas kernels  263 us (93%)
  local copies, waits for them, and re-layouts  10.1 us (4%)
  other arithmetic  8.11 us (3%)
    pallas_call x1, Pallas kernels, attn(): pl.pallas_call(attn_kernel, grid=(HEADS,), in_specs=[pl.BlockSpec(memory_...  84.9 us
    pallas_call x1, Pallas kernels, sum_all(): pl.pallas_call(sum_kernel, in_specs=[vm()] * 4, out_specs=vm(), out_shape...  70.9 us
    pallas_call x1, Pallas kernels, front_all(): pl.pallas_call(front_kernel, in_specs=[sm()] + [vm()] * 7, out_specs=[vm(...  64.2 us
    pallas_call x1, Pallas kernels, tail_all(): pl.pallas_call(tail_kernel, in_specs=[vm()] * 12, out_specs=[vm()] * 6, o...  42.8 us
    convert_element_type x1, other arithmetic, per_device(): summed = [total[i].astype(F32) for i in range(4)]  6.18 us
    transpose x2, local copies, waits for them, and re-layouts, from_local(): return a.reshape(RATE, 64, -1).transpose(1, 0, 2).reshape(T, -1)  5.76 us

profile of v3, /device:TPU:1, one launch (start us, length us, event | category | flops | bytes accessed | tf_op | source)
XLA Modules:
  0.0 282.3 jit_solution(3782610163331524631)
XLA Ops:
  1.3 0.6 pad_add_fusion.len_ref
  1.9 0.5 broadcast.3
  2.4 1.3 reduce.3
  3.7 0.1 reshape_squeeze.6
  3.8 0.1 copy.18
  3.9 0.7 reshape_reshape.3.src_ref
  4.6 3.0 %copy.19 = bf16[64,16,768]{2,0,1:T(8,128)(2,1)} copy(bf16[64,16,768]{2,1,0:T(8,128)(2,1)} %bitcast.31) | data formatting | bytes 3145728 | tf_op jit(solution)/shard_map/reshape;squeeze | solution.py:425
  7.6 64.2 %shard_map.127 = (bf16[1024,768]{1,0:T(8,128)(2,1)}, bf16[1024,768]{1,0:T(8,128)(2,1)}, bf16[1024,768]{1,0:T(8,128)(2,1)}, bf16[768,1024]{1,0:T(8,128)(2,1)}, bf...) custom-call(s32[2]{0:T(128)} %pad_add_fusion.len_ref, ...), custom_call_target="tpu_custom_call" | custom-call | flops 7247757312 | bytes 20971520 | tf_op jit(solution)/shard_map/pallas_call | solution.py:353
  71.8 84.9 %shard_map.128 = (bf16[768,1024]{1,0:T(8,128)(2,1)}, bf16[768,1024]{1,0:T(8,128)(2,1)}, f32[768,1024]{1,0:T(8,128)}, f32[768,1024]{1,0:T(8,128)}, bf16[768,512]{1,0:T(8,128)(2,1)}, /*index=5*/bf16[768,512]{1,0:T(8,128)(2,1)}) custom-call(s32[2]{0:T(128)} %pad_add_fusion.len_ref, bf16[1024,768]{1,0:T(8,128)(2,1)} %get-tuple-element.29.k_ref, ...), custom_call_target="tpu_custom_call" | custom-call | tf_op jit(solution)/shard_map/pallas_call | solution.py:107
  156.7 42.8 %shard_map.129 = (bf16[1024,768]{1,0:T(8,128)(2,1)}, bf16[1024,768]{1,0:T(8,128)(2,1)}, f32[768,768]{1,0:T(8,128)}, f32[768,768]{1,0:T(8,128)}, f32[768,768]{1,0:T(8,128)}, /*index=5*/f32[768,768]{1,0:T(8,128)}) custom-call(bf16[1024,768]{1,0:T(8,128)(2,1)} %get-tuple-element.28.x_ref, bf16[1024,768]{1,0:T(8,128)(2,1)} %bitcast.33, ...), custom_call_target="tpu_custom_call" | custom-call | flops 9663676416 | bytes 31457280 | tf_op jit(solution)/shard_map/pallas_call | solution.py:409
  199.5 0.0 copy-start
  199.5 3.5 %copy.20 = bf16[64,16,768]{2,1,0:T(8,128)(2,1)} copy(bf16[64,16,768]{2,0,1:T(8,128)(2,1)} %bitcast.37) | data formatting | bytes 3145728 | tf_op jit(solution)/shard_map/transpose | solution.py:429
  203.0 0.0 copy-done
  203.0 2.2 copy.21
  205.2 70.9 %shard_map.130 = bf16[4,768,768]{2,1,0:T(8,128)(2,1)} custom-call(f32[768,768]{1,0:T(8,128)} %get-tuple-element.46.gq_ref, f32[768,768]{1,0:T(8,128)} %get-tuple-element.47.gk_ref, f32[768,768]{1,0:T(8,128)} %get-tuple-element.48.gv_ref, f32[768,768]{1,0:T(8,128)} %get-tuple-element.49.go_ref), custom_call_target="tpu_custom_call" | custom-call | flops 16777216 | bytes 20971520 | tf_op jit(solution)/shard_map/pallas_call | solution.py:259
  276.2 6.2 %bitcast_convert_fusion = (f32[768,768]{1,0:T(8,128)}, f32[768,768]{1,0:T(8,128)}, f32[768,768]{1,0:T(8,128)}, f32[768,768]{1,0:T(8,128)}) fusion(bf16[4,768,768]{2,1,0:T(8,128)(2,1)} %shard_map.130), kind=kLoop, calls=%fused_computation | loop fusion | flops 2359296 | bytes 14155776 | tf_op jit(solution)/shard_map/convert_element_type | solution.py:445
Async XLA Ops:
  199.5 3.5 %copy-start = (bf16[1024,768]{1,0:T(8,128)(2,1)S(1)}, bf16[1024,768]{1,0:T(8,128)(2,1)}, u32[]{:S(2)}) copy-start(bf16[1024,768]{1,0:T(8,128)(2,1)} %get-tuple-element.45) | copy-start | bytes 4718596

commit v4 on v3

--- a/solution.py
+++ b/solution.py
@@ -16,10 +16,49 @@
 def nn(a,b): return lax.dot_general(a,b,(((1,),(0,)),((),())),preferred_element_type=F32)
 def nt(a,b): return lax.dot_general(a,b,(((1,),(1,)),((),())),preferred_element_type=F32)
 
-def attn_kernel(len_ref, k_ref, v_ref, qT_ref, kT_ref, vT_ref, gT_ref, far_ref, kfT_ref, vfT_ref,
-                attT_ref, dqT_ref, dkT_ref, dvT_ref, dkfT_ref, dvfT_ref,
-                qpad, gpad, kb, kfb, m2s, l2s, u2s, w2s, des, dqs, e2s):
+def attn_kernel(len_ref, k_ref, v_ref, qT_ref, kT_ref, vT_ref, gT_ref, far_ref, kfT_ref, vfT_ref, x_ref, go_ref,
+                attT_ref, dqT_ref, dk0_ref, dv0_ref, dk32_ref, dv32_ref, dkf_ref, dvf_ref, fin_ref,
+                qpad, gpad, kb, kfb, m2s, l2s, u2s, w2s, des, dqs, e2s,
+                dk0s, dv0s, dkf0, dvf0, xT, part, rx, bs, br, *scratch):
+    red = Reduction(*scratch[:7], fin_ref, *scratch[7:])
     h = pl.program_id(0)
+
+    @pl.when(h == 0)
+    def _():
+        greet(all_peers())
+
+    @pl.when(h == 8)
+    def _():
+        part[:, 0:HALF] = dkf0[...].T
+        part[:, HALF:D] = dvf0[...].T
+        for c in back_copies(part, rx, bs, br):
+            c.start()
+        xT[...] = x_ref[...].T
+        red.columns(0, nt(xT[...], dqT_ref[0:HALF, :]))
+        red.pair(0).start()
+        red.rows(3, nn(attT_ref[0:HALF, :], go_ref[...]))
+        red.pair(3).start()
+
+    @pl.when(h == 10)
+    def _():
+        add_back(back_copies(part, rx, bs, br), part, rx, 0, dk0s, dv0s, dk0_ref, dv0_ref)
+        red.columns(1, nt(xT[...], dk0_ref[...]))
+        red.pair(1).start()
+        red.columns(2, nt(xT[...], dv0_ref[...]))
+        red.pair(2).start()
+
+    @pl.when(h == 11)
+    def _():
+        red.after_pair()
+
+    @pl.when(h == 13)
+    def _():
+        red.after_first()
+
+    @pl.when(h == 14)
+    def _():
+        red.after_second()
+
     n = len_ref[0]
     nfull = len_ref[1]
     scale = HD ** -0.5
@@ -92,28 +131,65 @@
         dqs[:, sl] = nn(kTh, dS)
         dv += nt(gTh, P.astype(BF))
         dk += nt(qT_ref[pl.ds(r, HD), sl], dS)
-    dvT_ref[pl.ds(r, HD), :] = dv
-    dkT_ref[pl.ds(r, HD), :] = dk * scale
+    r1 = pl.multiple_of(lax.rem(h, 8) * HD, 16)
+
+    @pl.when(h < 8)
+    def _():
+        dv0s[pl.ds(r1, HD), :] = dv
+        dk0s[pl.ds(r1, HD), :] = dk * scale
+
+    @pl.when(h >= 8)
+    def _():
+        dv32_ref[pl.ds(r1, HD), :] = dv
+        dk32_ref[pl.ds(r1, HD), :] = dk * scale
+
     P2 = e2s[...] * jnp.where(mine, w2s[:, pl.ds(wq, 128)], 0.0)
     dP2 = nn(far_ref[:, pl.ds(pl.multiple_of(w0 + D, 128), 256)], gpad[:, pl.ds(wq, 128)])
     dS2 = (P2 * (dP2 - des[:, pl.ds(wq, 128)])).astype(BF)
-    dvfT_ref[pl.ds(r, HD), :] = nt(gT_ref[pl.ds(r, HD), pl.ds(wq, 128)], P2.astype(BF)).astype(BF)
-    dkfT_ref[pl.ds(r, HD), :] = (nt(qT_ref[pl.ds(r, HD), pl.ds(wq, 128)], dS2) * scale).astype(BF)
+    dvf = nt(gT_ref[pl.ds(r, HD), pl.ds(wq, 128)], P2.astype(BF)).astype(BF)
+    dkf = (nt(qT_ref[pl.ds(r, HD), pl.ds(wq, 128)], dS2) * scale).astype(BF)
+
+    @pl.when(h < 8)
+    def _():
+        dvf0[pl.ds(r1, HD), :] = dvf
+        dkf0[pl.ds(r1, HD), :] = dkf
+
+    @pl.when(h >= 8)
+    def _():
+        dvf_ref[pl.ds(r1, HD), :] = dvf
+        dkf_ref[pl.ds(r1, HD), :] = dkf
+
     dqs[:, pl.ds(wq, 128)] += nn(kfT_ref[pl.ds(r, HD), :], dS2)
     dqT_ref[pl.ds(r, HD), :] = (dqs[...] * scale).astype(BF)
 
+    @pl.when(h == HEADS - 1)
+    def _():
+        red.after_third()
+        for c in back_copies(part, rx, bs, br):
+            c.wait_send()
+        red.finish()
+
 def attn(lens, *arrs):
-    vm = pl.BlockSpec(memory_space=pltpu.VMEM)
+    s = jax.ShapeDtypeStruct
+    dma = pltpu.SemaphoreType.DMA
     return pl.pallas_call(
-        attn_kernel, grid=(HEADS,),
-        in_specs=[pl.BlockSpec(memory_space=pltpu.SMEM)] + [vm]*9,
-        out_specs=[vm]*6,
-        out_shape=[jax.ShapeDtypeStruct((D,T),BF), jax.ShapeDtypeStruct((D,T),BF), jax.ShapeDtypeStruct((D,T),F32), jax.ShapeDtypeStruct((D,T),F32),
-                   jax.ShapeDtypeStruct((D,FAR),BF), jax.ShapeDtypeStruct((D,FAR),BF)],
-        scratch_shapes=[pltpu.VMEM((256,T),BF), pltpu.VMEM((256,T),BF), pltpu.VMEM((T,256),BF), pltpu.VMEM((FAR,256),BF),
-                        pltpu.VMEM((1,T),F32), pltpu.VMEM((1,T),F32), pltpu.VMEM((HD,T),F32), pltpu.VMEM((1,T),F32), pltpu.VMEM((1,T),F32),
-                        pltpu.VMEM((HD,T),F32), pltpu.VMEM((FAR,128),F32)],
-        compiler_params=pltpu.CompilerParams(vmem_limit_bytes=60<<20),
+        attn_kernel,
+        grid=(HEADS,),
+        in_specs=[sm()] + [vm()] * 11,
+        out_specs=[vm()] * 9,
+        out_shape=[s((D, T), BF)] * 2 + [s((HALF, T), BF)] * 2 + [s((HALF, T), F32)] * 2 + [s((HALF, FAR), BF)] * 2
+        + [s((3, 32, HALF), BF)],
+        scratch_shapes=[
+            pltpu.VMEM((256, T), BF), pltpu.VMEM((256, T), BF), pltpu.VMEM((T, 256), BF), pltpu.VMEM((FAR, 256), BF),
+            pltpu.VMEM((1, T), F32), pltpu.VMEM((1, T), F32), pltpu.VMEM((HD, T), F32), pltpu.VMEM((1, T), F32),
+            pltpu.VMEM((1, T), F32), pltpu.VMEM((HD, T), F32), pltpu.VMEM((FAR, 128), F32),
+            pltpu.VMEM((HALF, T), F32), pltpu.VMEM((HALF, T), F32), pltpu.VMEM((HALF, FAR), BF),
+            pltpu.VMEM((HALF, FAR), BF), pltpu.VMEM((D, T), BF), pltpu.VMEM((FAR, D), BF), pltpu.VMEM((7, 64, D), BF),
+            dma((7,)), dma((7,)),
+        ] + reduction_scratch(),
+        compiler_params=pltpu.CompilerParams(
+            vmem_limit_bytes=60 << 20, collective_id=4, has_side_effects=True),
+        cost_estimate=pl.CostEstimate(flops=100 * T * D * D, bytes_accessed=30 << 20, transcendentals=0),
     )(lens, *arrs)
 
 
@@ -159,118 +235,6 @@
     )
     copy.start()
     return copy
-
-
-HALF = D // 2
-
-
-def sum_kernel(gq_ref, gk_ref, gv_ref, go_ref, out_ref, acc, crx, rx1, rx2, rx3, r2, r3,
-               cs, cr, ss, rs, gs, gr, hs, hr):
-    xyz, core = coords()
-    mate = device_at(xyz, 1 - core)
-    greet([mate] + [device_at(along(xyz, a, d), core) for a in range(3) for d in (1, 2, 3)])
-    mine = pl.ds(pl.multiple_of(core * HALF, 128), HALF)
-    theirs = pl.ds(pl.multiple_of((1 - core) * HALF, 128), HALF)
-    grads = (gq_ref, gk_ref, gv_ref, go_ref)
-    pair = [send(g.at[:, theirs], crx.at[i], cs.at[i], cr.at[i], mate) for i, g in enumerate(grads)]
-    for i, g in enumerate(grads):
-        pair[i].wait_recv()
-        acc[i] = g[:, mine] + crx[i]
-    out = []
-    waves = []
-    for p in range(3):
-        axis = ORDERS[p][0]
-        a = xyz[axis]
-        rows = pl.ds(p * 256, 256)
-        waves.append([send(acc.at[(a + d) % 4, rows], rx1.at[p, d - 1], ss.at[0, p, d - 1], rs.at[0, p, d - 1],
-                           device_at(along(xyz, axis, d), core)) for d in (1, 2, 3)])
-    out += waves
-    nxt = []
-    for p in range(3):
-        a = xyz[ORDERS[p][0]]
-        for c in waves[p]:
-            c.wait_recv()
-        r2[p] = acc[a, p * 256:(p + 1) * 256] + rx1[p, 0] + rx1[p, 1] + rx1[p, 2]
-        axis = ORDERS[p][1]
-        b = xyz[axis]
-        nxt.append([send(r2.at[p, pl.ds(pl.multiple_of(((b + d) % 4) * 64, 64), 64)], rx2.at[p, d - 1],
-                         ss.at[1, p, d - 1], rs.at[1, p, d - 1], device_at(along(xyz, axis, d), core))
-                    for d in (1, 2, 3)])
-    out += nxt
-    waves = nxt
-    nxt = []
-    for p in range(3):
-        b = xyz[ORDERS[p][1]]
-        for c in waves[p]:
-            c.wait_recv()
-        r3[p] = r2[p, pl.ds(pl.multiple_of(b * 64, 64), 64)] + rx2[p, 0] + rx2[p, 1] + rx2[p, 2]
-        axis = ORDERS[p][2]
-        e = xyz[axis]
-        nxt.append([send(r3.at[p, pl.ds(pl.multiple_of(((e + d) % 4) * 16, 16), 16)], rx3.at[p, d - 1],
-                         ss.at[2, p, d - 1], rs.at[2, p, d - 1], device_at(along(xyz, axis, d), core))
-                    for d in (1, 2, 3)])
-    out += nxt
-    waves = nxt
-    nxt = []
-
-    def region(p, level):
-        a, b, e = (xyz[ORDERS[p][i]] for i in range(3))
-        if level == 2:
-            return a, pl.ds(pl.multiple_of(p * 256 + b * 64 + e * 16, 16), 16)
-        if level == 1:
-            return a, pl.ds(pl.multiple_of(p * 256 + b * 64, 64), 64)
-        return a, pl.ds(p * 256, 256)
-
-    for level in (2, 1, 0):
-        for p in range(3):
-            for c in waves[p]:
-                c.wait_recv()
-            i, rows = region(p, level)
-            if level == 2:
-                e = xyz[ORDERS[p][2]]
-                total = r3[p, pl.ds(pl.multiple_of(e * 16, 16), 16)] + rx3[p, 0] + rx3[p, 1] + rx3[p, 2]
-                out_ref[i, rows, mine] = total.astype(BF)
-            axis = ORDERS[p][level]
-            here = out_ref.at[i, rows, mine]
-            nxt.append([send(here, here, gs.at[level, p, d - 1], gr.at[level, p, d - 1],
-                             device_at(along(xyz, axis, d), core)) for d in (1, 2, 3)])
-        out += nxt
-        waves = nxt
-        nxt = []
-    for p in range(3):
-        for c in waves[p]:
-            c.wait_recv()
-    last = []
-    for i in range(4):
-        here = out_ref.at[i, :, mine]
-        last.append(send(here, here, hs.at[i], hr.at[i], mate))
-    for c in pair:
-        c.wait_send()
-    for wave in out:
-        for c in wave:
-            c.wait_send()
-    for c in last:
-        c.wait()
-
-
-def sum_all(gq, gk, gv, go):
-    s = jax.ShapeDtypeStruct
-    dma = pltpu.SemaphoreType.DMA
-    return pl.pallas_call(
-        sum_kernel,
-        in_specs=[vm()] * 4,
-        out_specs=vm(),
-        out_shape=s((4, D, D), BF),
-        scratch_shapes=[
-            pltpu.VMEM((4, D, HALF), F32), pltpu.VMEM((4, D, HALF), F32),
-            pltpu.VMEM((3, 3, 256, HALF), F32), pltpu.VMEM((3, 3, 64, HALF), F32),
-            pltpu.VMEM((3, 3, 16, HALF), F32), pltpu.VMEM((3, 256, HALF), F32), pltpu.VMEM((3, 64, HALF), F32),
-            dma((4,)), dma((4,)), dma((3, 3, 3)), dma((3, 3, 3)), dma((3, 3, 3)), dma((3, 3, 3)), dma((4,)), dma((4,)),
-        ],
-        compiler_params=pltpu.CompilerParams(
-            vmem_limit_bytes=56 << 20, collective_id=1, has_side_effects=True),
-        cost_estimate=pl.CostEstimate(flops=1 << 24, bytes_accessed=20 << 20, transcendentals=0),
-    )(gq, gk, gv, go)
 
 
 def seq_peer(s, d):
@@ -365,42 +329,230 @@
     )(lens, src, rows, go, wq, wk, wv, wo)
 
 
-def tail_kernel(x_ref, go_ref, attT_ref, dqT_ref, dkT_ref, dvT_ref, dkfT_ref, dvfT_ref, wq_ref, wk_ref, wv_ref, wo_ref,
-                enc_ref, emb_ref, gq_ref, gk_ref, gv_ref, gout_ref, part, rx, dk_s, dv_s, ss, rs):
+HALF = D // 2
+GH = HEADS // 2
+
+
+def copy_to(src, dst, ssem, rsem, peer):
+    return pltpu.make_async_remote_copy(
+        src_ref=src, dst_ref=dst, send_sem=ssem, recv_sem=rsem, device_id=peer, device_id_type=MESHID
+    )
+
+
+def all_peers():
+    xyz, core = coords()
     s = lax.axis_index("seq")
-    peers = [seq_peer(s, d) for d in range(1, 8)]
-    greet(peers)
-    part[:, 0:D] = dkfT_ref[...].T
-    part[:, D:2 * D] = dvfT_ref[...].T
-    backs = [send(part.at[pl.ds(pl.multiple_of(lax.rem(s + d, 8) * 64, 64), 64)], rx.at[d - 1],
-                  ss.at[d - 1], rs.at[d - 1], peers[d - 1]) for d in range(1, 8)]
-    xT = x_ref[...].T
-    gq_ref[...] = nt(xT, dqT_ref[...])
-    gout_ref[...] = nn(attT_ref[...], go_ref[...])
-    enc_ref[...] = (x_ref[...].astype(F32) + nn(attT_ref[...].T, wo_ref[...])).astype(BF)
+    near = [device_at(along(xyz, 0, d), core) for d in (1, 3)] + [device_at(along(xyz, 2, d), core) for d in (1, 2, 3)]
+    return [seq_peer(s, d) for d in range(1, 8)] + near + [device_at(xyz, 1 - core)]
+
+
+class Reduction:
+    def __init__(self, grads, crx, acc, rx1, rx2, rx3, r2, fin, cs, cr, ss, rs):
+        self.xyz, self.core = coords()
+        self.grads, self.crx, self.acc = grads, crx, acc
+        self.rx1, self.rx2, self.rx3, self.r2, self.fin = rx1, rx2, rx3, r2, fin
+        self.cs, self.cr, self.ss, self.rs = cs, cr, ss, rs
+
+    def at(self, p, level):
+        return self.xyz[ORDERS[p][level]]
+
+    def peer(self, p, level, d):
+        return device_at(along(self.xyz, ORDERS[p][level], d), self.core)
+
+    def pair(self, i):
+        return copy_to(self.grads.at[i, 1 - self.core], self.crx.at[i], self.cs.at[i], self.cr.at[i],
+                       device_at(self.xyz, 1 - self.core))
+
+    def wave(self, level, parts=(0, 1, 2)):
+        made = []
+        for p in parts:
+            for d in (1, 2, 3):
+                other = (self.at(p, level) + d) % 4
+                if level == 0:
+                    src, dst = self.acc.at[other, pl.ds(p * 128, 128)], self.rx1.at[p, d - 1]
+                elif level == 1:
+                    src, dst = self.r2.at[p, pl.ds(pl.multiple_of(other * 32, 32), 32)], self.rx2.at[p, d - 1]
+                else:
+                    own = self.rx3.at[p, self.at(p, 2)]
+                    src, dst = own, own
+                made.append(copy_to(src, dst, self.ss.at[level, p, d - 1], self.rs.at[level, p, d - 1],
+                                    self.peer(p, level, d)))
+        return made
+
+    def start(self, copies):
+        for c in copies:
+            c.start()
+
+    def columns(self, i, value):
+        self.grads[i, 0] = value[:HALF]
+        self.grads[i, 1] = value[HALF:]
+
+    def rows(self, i, value):
+        self.grads[i, 0] = value[:, :HALF]
+        self.grads[i, 1] = value[:, HALF:]
+
+    def after_pair(self):
+        for i in (0, 3, 1, 2):
+            self.pair(i).wait_recv()
+            self.acc[i] = self.grads[i, self.core] + self.crx[i]
+        self.start(self.wave(0))
+
+    def after_first(self):
+        copies = self.wave(0)
+        for p in range(3):
+            for c in copies[3 * p:3 * p + 3]:
+                c.wait_recv()
+            self.r2[p] = self.acc[self.at(p, 0), p * 128:(p + 1) * 128] + self.rx1[p, 0] + self.rx1[p, 1] + self.rx1[p, 2]
+            self.start(self.wave(1, (p,)))
+
+    def after_second(self):
+        copies = self.wave(1)
+        for p in range(3):
+            for c in copies[3 * p:3 * p + 3]:
+                c.wait_recv()
+            own = self.r2[p, pl.ds(pl.multiple_of(self.at(p, 1) * 32, 32), 32)]
+            self.rx3[p, self.at(p, 2)] = own + self.rx2[p, 0] + self.rx2[p, 1] + self.rx2[p, 2]
+            self.start(self.wave(2, (p,)))
+
+    def after_third(self):
+        copies = self.wave(2)
+        for p in range(3):
+            for c in copies[3 * p:3 * p + 3]:
+                c.wait_recv()
+            self.fin[p] = (self.rx3[p, 0] + self.rx3[p, 1] + self.rx3[p, 2] + self.rx3[p, 3]).astype(BF)
+
+    def finish(self):
+        for i in range(4):
+            self.pair(i).wait_send()
+        for level in range(3):
+            for c in self.wave(level):
+                c.wait_send()
+
+
+def reduction_scratch():
+    dma = pltpu.SemaphoreType.DMA
+    return [
+        pltpu.VMEM((4, 2, HALF, HALF), F32), pltpu.VMEM((4, HALF, HALF), F32), pltpu.VMEM((4, HALF, HALF), F32),
+        pltpu.VMEM((3, 3, 128, HALF), F32), pltpu.VMEM((3, 3, 32, HALF), F32), pltpu.VMEM((3, 4, 32, HALF), F32),
+        pltpu.VMEM((3, 128, HALF), F32), dma((4,)), dma((4,)), dma((3, 3, 3)), dma((3, 3, 3)),
+    ]
+
+
+class Spread:
+    def __init__(self, red, fin, out, gs, gr, hs, hr):
+        self.red, self.fin, self.out, self.gs, self.gr, self.hs, self.hr = red, fin, out, gs, gr, hs, hr
+
+    def wave(self, level, parts=(0, 1, 2)):
+        made = []
+        for p in parts:
+            a, b = self.red.at(p, 0), self.red.at(p, 1)
+            rows = pl.ds(pl.multiple_of(p * 128 + b * 32, 32), 32) if level == 1 else pl.ds(p * 128, 128)
+            here = self.out.at[self.red.core, a, rows]
+            for d in (1, 2, 3):
+                made.append(copy_to(here, here, self.gs.at[level, p, d - 1], self.gr.at[level, p, d - 1],
+                                    self.red.peer(p, level, d)))
+        return made
+
+    def mate(self):
+        here = self.out.at[self.red.core]
+        return copy_to(here, here, self.hs, self.hr, device_at(self.red.xyz, 1 - self.red.core))
+
+    def begin(self):
+        for p in range(3):
+            rows = pl.ds(pl.multiple_of(p * 128 + self.red.at(p, 1) * 32, 32), 32)
+            self.out[self.red.core, self.red.at(p, 0), rows] = self.fin[p]
+        for c in self.wave(1):
+            c.start()
+
+    def middle(self):
+        for p in range(3):
+            for c in self.wave(1, (p,)):
+                c.wait_recv()
+            for c in self.wave(0, (p,)):
+                c.start()
+
+    def end(self):
+        for c in self.wave(0):
+            c.wait_recv()
+        self.mate().start()
+
+    def finish(self):
+        for level in range(2):
+            for c in self.wave(level):
+                c.wait_send()
+        self.mate().wait()
+
+
+def back_copies(part, rx, ss, rs):
+    s = lax.axis_index("seq")
+    return [copy_to(part.at[pl.ds(pl.multiple_of(lax.rem(s + d, 8) * 64, 64), 64)], rx.at[d - 1],
+                    ss.at[d - 1], rs.at[d - 1], seq_peer(s, d)) for d in range(1, 8)]
+
+
+def add_back(copies, part, rx, group, dk32, dv32, dk, dv):
+    s = lax.axis_index("seq")
     back = part[pl.ds(pl.multiple_of(s * 64, 64), 64), :].astype(F32)
     for d in range(1, 8):
-        backs[d - 1].wait_recv()
+        copies[d - 1].wait_recv()
         back = back + rx[d - 1].astype(F32)
     bT = back.T
     zero = jnp.zeros((HD, 64), F32)
-    for h in range(HEADS):
-        r = slice(h * HD, (h + 1) * HD)
+    for i in range(GH):
+        h = group * GH + i
+        r = slice(i * HD, (i + 1) * HD)
         w = slice((h // 2) * 128, (h // 2) * 128 + 128)
-        bk = bT[h * HD:(h + 1) * HD, :]
-        bv = bT[D + h * HD:D + (h + 1) * HD, :]
+        bk = bT[i * HD:(i + 1) * HD, :]
+        bv = bT[HALF + i * HD:HALF + (i + 1) * HD, :]
         pk = [bk, zero] if h % 2 == 0 else [zero, bk]
         pv = [bv, zero] if h % 2 == 0 else [zero, bv]
-        dk_s[r, :] = dkT_ref[r, :].astype(BF)
-        dv_s[r, :] = dvT_ref[r, :].astype(BF)
-        dk_s[r, w] = (dkT_ref[r, w] + jnp.concatenate(pk, axis=1)).astype(BF)
-        dv_s[r, w] = (dvT_ref[r, w] + jnp.concatenate(pv, axis=1)).astype(BF)
-    gk_ref[...] = nt(xT, dk_s[...])
-    gv_ref[...] = nt(xT, dv_s[...])
-    e = nn(wq_ref[...], dqT_ref[...]) + nn(wk_ref[...], dk_s[...]) + nn(wv_ref[...], dv_s[...])
+        dk[r, :] = dk32[r, :].astype(BF)
+        dv[r, :] = dv32[r, :].astype(BF)
+        dk[r, w] = (dk32[r, w] + jnp.concatenate(pk, axis=1)).astype(BF)
+        dv[r, w] = (dv32[r, w] + jnp.concatenate(pv, axis=1)).astype(BF)
+
+
+def tail_kernel(x_ref, go_ref, attT_ref, dqT_ref, dk0_ref, dv0_ref, dk32_ref, dv32_ref, dkf_ref, dvf_ref, fin0_ref,
+                wq_ref, wk_ref, wv_ref, wo_ref, enc_ref, emb_ref, out0_ref, out1_ref,
+                part, rx, dk, dv, fin1, bs, br, g0s, g0r, h0s, h0r, g1s, g1r, h1s, h1r, *scratch):
+    greet(all_peers())
+    red = Reduction(*scratch[:7], fin1, *scratch[7:])
+    first = Spread(red, fin0_ref, out0_ref, g0s, g0r, h0s, h0r)
+    second = Spread(red, fin1, out1_ref, g1s, g1r, h1s, h1r)
+    part[:, 0:HALF] = dkf_ref[...].T
+    part[:, HALF:D] = dvf_ref[...].T
+    backs = back_copies(part, rx, bs, br)
+    for c in backs:
+        c.start()
+    first.begin()
+    xT = x_ref[...].T
+    red.columns(0, nt(xT, dqT_ref[HALF:, :]))
+    red.pair(0).start()
+    red.rows(3, nn(attT_ref[HALF:, :], go_ref[...]))
+    red.pair(3).start()
+    first.middle()
+    enc_ref[...] = (x_ref[...].astype(F32) + nn(attT_ref[...].T, wo_ref[...])).astype(BF)
+    add_back(backs, part, rx, 1, dk32_ref, dv32_ref, dk, dv)
+    red.columns(1, nt(xT, dk[...]))
+    red.pair(1).start()
+    red.columns(2, nt(xT, dv[...]))
+    red.pair(2).start()
+    first.end()
+    red.after_pair()
+    e = nn(wq_ref[...], dqT_ref[...])
+    e = e + nn(wk_ref[:, 0:HALF], dk0_ref[...]) + nn(wk_ref[:, HALF:D], dk[...])
+    e = e + nn(wv_ref[:, 0:HALF], dv0_ref[...]) + nn(wv_ref[:, HALF:D], dv[...])
     emb_ref[...] = (go_ref[...].astype(F32) + e.T).astype(BF)
+    red.after_first()
+    red.after_second()
+    red.after_third()
+    second.begin()
+    second.middle()
+    second.end()
     for c in backs:
         c.wait_send()
+    red.finish()
+    first.finish()
+    second.finish()
 
 
 def tail_all(*args):
@@ -408,13 +560,13 @@
     dma = pltpu.SemaphoreType.DMA
     return pl.pallas_call(
         tail_kernel,
-        in_specs=[vm()] * 12,
-        out_specs=[vm()] * 6,
-        out_shape=[s((T, D), BF)] * 2 + [s((D, D), F32)] * 4,
+        in_specs=[vm()] * 15,
+        out_specs=[vm()] * 4,
+        out_shape=[s((T, D), BF)] * 2 + [s((2, 4, HALF, HALF), BF)] * 2,
         scratch_shapes=[
-            pltpu.VMEM((FAR, 2 * D), BF), pltpu.VMEM((7, 64, 2 * D), BF),
-            pltpu.VMEM((D, T), BF), pltpu.VMEM((D, T), BF), dma((7,)), dma((7,)),
-        ],
+            pltpu.VMEM((FAR, D), BF), pltpu.VMEM((7, 64, D), BF),
+            pltpu.VMEM((HALF, T), BF), pltpu.VMEM((HALF, T), BF), pltpu.VMEM((3, 32, HALF), BF), dma((7,)), dma((7,)),
+        ] + [dma((2, 3, 3)), dma((2, 3, 3)), dma(()), dma(())] * 2 + reduction_scratch(),
         compiler_params=pltpu.CompilerParams(
             vmem_limit_bytes=60 << 20, collective_id=3, has_side_effects=True),
         cost_estimate=pl.CostEstimate(flops=16 * T * D * D, bytes_accessed=30 << 20, transcendentals=0),
@@ -437,12 +589,14 @@
     x, k, v, qT, kT, vT, gT, far, kfT, vfT = front_all(
         lens, source, tile_embed[0], go, w_query, w_key, w_value, w_out
     )
-    attT, dqT, dkT, dvT, dkfT, dvfT = attn(lens, k, v, qT, kT, vT, gT, far, kfT, vfT)
-    enc, emb, gq, gk, gv, gout = tail_all(
-        x, go, attT, dqT, dkT, dvT, dkfT, dvfT, w_query, w_key, w_value, w_out
+    attT, dqT, dk0, dv0, dk32, dv32, dkf, dvf, fin0 = attn(lens, k, v, qT, kT, vT, gT, far, kfT, vfT, x, go)
+    enc, emb, out0, out1 = tail_all(
+        x, go, attT, dqT, dk0, dv0, dk32, dv32, dkf, dvf, fin0, w_query, w_key, w_value, w_out
     )
-    total = sum_all(gq, gk, gv, gout)
-    summed = [total[i].astype(F32) for i in range(4)]
+    summed = []
+    for i in range(4):
+        along_rows = [jnp.concatenate([o[0, i], o[1, i]], axis=0 if i < 3 else 1) for o in (out0, out1)]
+        summed.append(jnp.concatenate(along_rows, axis=1 if i < 3 else 0).astype(F32))
     return (from_local(enc)[None], from_local(emb)[None], summed[0], summed[1], summed[2], summed[3])
 
 

time: 283 us -> 255 us (0.901)
  Pallas kernels: 263 us -> 234 us
    pallas_call x3 -> x2, Pallas kernels: 199 us -> 170 us  [the longest x1 102 us: attn(): pl.pallas_call(attn_kernel, grid=(HEADS,), in_specs=[sm()] + [vm()] * 11,...]
    convert_element_type x1 -> x4, other arithmetic: 6.18 us -> 6.27 us  [per_device(): jnp.concatenate(along_rows, axis=1 if i < 3 else 0).astype(F32)]
where the time goes in v4:
time: 255 us
  Pallas kernels  234 us (92%)
  local copies, waits for them, and re-layouts  10.9 us (4%)
  other arithmetic  8.2 us (3%)
    pallas_call x1, Pallas kernels, attn(): pl.pallas_call(attn_kernel, grid=(HEADS,), in_specs=[sm()] + [vm()] * 11,...  102 us
    pallas_call x1, Pallas kernels, tail_all(): pl.pallas_call(tail_kernel, in_specs=[vm()] * 15, out_specs=[vm()] * 4, o...  67.7 us
    pallas_call x1, Pallas kernels, front_all(): pl.pallas_call(front_kernel, in_specs=[sm()] + [vm()] * 7, out_specs=[vm(...  64.1 us
    convert_element_type x4, other arithmetic, per_device(): jnp.concatenate(along_rows, axis=1 if i < 3 else 0).astype(F32)  6.27 us
    transpose x2, local copies, waits for them, and re-layouts, from_local(): return a.reshape(RATE, 64, -1).transpose(1, 0, 2).reshape(T, -1)  5.83 us

profile of v4, /device:TPU:1, one launch (start us, length us, event | category | flops | bytes accessed | tf_op | source)
XLA Modules:
  0.0 254.6 jit_solution(2779337405608207026)
XLA Ops:
  1.3 0.6 pad_add_fusion.len_ref
  1.9 0.5 broadcast.3
  2.4 1.3 reduce.3
  3.7 0.1 reshape_squeeze.6
  3.8 0.1 copy.18
  3.9 0.7 reshape_reshape.3.src_ref
  4.6 3.0 %copy.19 = bf16[64,16,768]{2,0,1:T(8,128)(2,1)} copy(bf16[64,16,768]{2,1,0:T(8,128)(2,1)} %bitcast.51) | data formatting | bytes 3145728 | tf_op jit(solution)/shard_map/reshape;squeeze | solution.py:577
  7.6 64.1 %shard_map.127 = (bf16[1024,768]{1,0:T(8,128)(2,1)}, bf16[1024,768]{1,0:T(8,128)(2,1)}, bf16[1024,768]{1,0:T(8,128)(2,1)}, bf16[768,1024]{1,0:T(8,128)(2,1)}, bf...) custom-call(s32[2]{0:T(128)} %pad_add_fusion.len_ref, ...), custom_call_target="tpu_custom_call" | custom-call | flops 7247757312 | bytes 20971520 | tf_op jit(solution)/shard_map/pallas_call | solution.py:317
  71.7 102.3 %shard_map.128 = (bf16[768,1024]{1,0:T(8,128)(2,1)}, bf16[768,1024]{1,0:T(8,128)(2,1)}, bf16[384,1024]{1,0:T(8,128)(2,1)}, bf16[384,1024]{1,0:T(8,128)(2,1)}, f3...) custom-call(s32[2]{0:T(128)} %pad_add_fusion.len_ref, ...), custom_call_target="tpu_custom_call" | custom-call | flops 60397977600 | bytes 31457280 | tf_op jit(solution)/shard_map/pallas_call | solution.py:175
  174.0 67.7 %shard_map.129 = (bf16[1024,768]{1,0:T(8,128)(2,1)}, bf16[1024,768]{1,0:T(8,128)(2,1)}, bf16[2,4,384,384]{3,2,1,0:T(8,128)(2,1)}, bf16[2,4,384,384]{3,2,1,0:T(8,128)(2,1)}) custom-call(bf16[1024,768]{1,0:T(8,128)(2,1)} %get-tuple-element.29.x_ref, bf16[1024,768]{1,0:T(8,128)(2,1)} %bitcast.56, bf16[768,1024]{1,0:T(8,128)(2,1)} %get-tuple-element.39.attT_ref, ...), custom_call_target="tpu_custom_call" | custom-call | flops 9663676416 | bytes 31457280 | tf_op jit(solution)/shard_map/pallas_call | solution.py:561
  241.7 0.0 copy-start.2
  241.7 0.0 copy-start.1
  241.7 3.8 %copy.20 = bf16[64,16,768]{2,1,0:T(8,128)(2,1)} copy(bf16[64,16,768]{2,0,1:T(8,128)(2,1)} %bitcast.58) | data formatting | bytes 3145728 | tf_op jit(solution)/shard_map/transpose | solution.py:581
  245.6 0.0 copy-start
  245.6 0.0 copy-done.2
  245.6 2.0 copy.21
  247.6 0.0 copy-done.1
  247.6 0.0 copy-done
  247.6 0.7 slice_bitcast_fusion.1
  248.3 1.6 maximum_convert_fusion.3
  249.9 1.6 maximum_convert_fusion.2
  251.5 1.6 maximum_convert_fusion.1
  253.0 1.6 maximum_convert_fusion
Async XLA Ops:
  241.7 3.8 %copy-start.2 = (bf16[1024,768]{1,0:T(8,128)(2,1)S(1)}, bf16[1024,768]{1,0:T(8,128)(2,1)}, u32[]{:S(2)}) copy-start(bf16[1024,768]{1,0:T(8,128)(2,1)} %get-tuple-element.49) | copy-start | bytes 4718596
  241.7 5.8 %copy-start.1 = (bf16[2,4,384,384]{3,2,1,0:T(8,128)(2,1)S(1)}, bf16[2,4,384,384]{3,2,1,0:T(8,128)(2,1)}, u32[]{:S(2)}) copy-start(bf16[2,4,384,384]{3,2,1,0:T(8,128)(2,1)} %get-tuple-element.51) | copy-start | bytes 7077892
  245.6 2.0 copy-start

commit v5 on v4

--- a/solution.py
+++ b/solution.py
@@ -16,7 +16,7 @@
 def nn(a,b): return lax.dot_general(a,b,(((1,),(0,)),((),())),preferred_element_type=F32)
 def nt(a,b): return lax.dot_general(a,b,(((1,),(1,)),((),())),preferred_element_type=F32)
 
-def attn_kernel(len_ref, k_ref, v_ref, qT_ref, kT_ref, vT_ref, gT_ref, far_ref, kfT_ref, vfT_ref, x_ref, go_ref,
+def attn_kernel(len_ref, k_ref, v_ref, qT_ref, kT_ref, vT_ref, gT_ref, far_ref, kfT_ref, vfT_ref, top_ref, x_ref, go_ref,
                 attT_ref, dqT_ref, dk0_ref, dv0_ref, dk32_ref, dv32_ref, dkf_ref, dvf_ref, fin_ref,
                 qpad, gpad, kb, kfb, m2s, l2s, u2s, w2s, des, dqs, e2s,
                 dk0s, dv0s, dkf0, dvf0, xT, part, rx, bs, br, *scratch):
@@ -63,23 +63,13 @@
     nfull = len_ref[1]
     scale = HD ** -0.5
     c = scale * LOG2E
-    hh = lax.rem(h, 8)
-    w0 = pl.multiple_of((h // 8) * 384 + jnp.where(hh >= 5, 128, 0), 128)
-    off = h * HD - w0
+    w0, off, free = window(h)
     r = pl.multiple_of(h * HD, 16)
     row = lax.broadcasted_iota(jnp.int32, (256, T), 0)
-    inside = (row >= off) & (row < off + HD)
-    free = jnp.where(off >= 48, 0, 255)
-    qw = qT_ref[pl.ds(w0, 256), :]
-    gw = gT_ref[pl.ds(w0, 256), :]
-    one = jnp.where(row == free, 1.0, 0.0).astype(BF)
-    qpad[...] = jnp.where(inside, qw, one)
-    gpad[...] = jnp.where(inside, gw, jnp.zeros_like(gw))
-    ki = lax.broadcasted_iota(jnp.int32, (T, 1), 0)
-    kpos = lax.rem(ki, 64) * RATE + ki // 64
-    kbias = jnp.where(kpos < n, 0.0, NEG).astype(BF)
+    qpad[...] = pad_rows(qT_ref, w0, off, row, jnp.where(row == free, 1.0, 0.0).astype(BF))
+    gpad[...] = pad_rows(gT_ref, w0, off, row, jnp.zeros((256, T), BF))
     lane = lax.broadcasted_iota(jnp.int32, (T, 256), 1)
-    kb[...] = jnp.where(lane == free, kbias, k_ref[:, pl.ds(w0, 256)])
+    kb[...] = jnp.where(lane == free, key_bias(n), k_ref[:, pl.ds(w0, 256)])
     fi = lax.broadcasted_iota(jnp.int32, (FAR, 1), 0)
     fbias = jnp.where(fi * RATE + h < nfull, 0.0, NEG).astype(BF)
     flane = lax.broadcasted_iota(jnp.int32, (FAR, 256), 1)
@@ -107,7 +97,7 @@
     for ci in range(T // QC):
         sl = slice(ci * QC, (ci + 1) * QC)
         S = nn(kb[...], qpad[:, sl])
-        x1 = jnp.max(S, axis=0, keepdims=True)
+        x1 = top_ref[h, :, sl]
         e = jnp.exp2(S * c - x1 * c)
         l1 = jnp.sum(e, axis=0, keepdims=True)
         u1 = nn(vTh, e.astype(BF))
@@ -175,7 +165,7 @@
     return pl.pallas_call(
         attn_kernel,
         grid=(HEADS,),
-        in_specs=[sm()] + [vm()] * 11,
+        in_specs=[sm()] + [vm()] * 12,
         out_specs=[vm()] * 9,
         out_shape=[s((D, T), BF)] * 2 + [s((HALF, T), BF)] * 2 + [s((HALF, T), F32)] * 2 + [s((HALF, FAR), BF)] * 2
         + [s((3, 32, HALF), BF)],
@@ -241,27 +231,44 @@
     return (lax.rem(s + d, 8), lax.axis_index("rep"))
 
 
-def front_kernel(len_ref, src_ref, rows_ref, go_ref, wq_ref, wk_ref, wv_ref, wo_ref,
-                 x_ref, k_ref, v_ref, qT_ref, kT_ref, vT_ref, gT_ref, far_ref, kfT_ref, vfT_ref,
-                 ask, req, picked, arrived, perm, qs, qr, ps, pr, fs, fr):
+def window(h):
+    hh = lax.rem(h, 8)
+    w0 = pl.multiple_of((h // 8) * 384 + jnp.where(hh >= 5, 128, 0), 128)
+    off = h * HD - w0
+    return w0, off, jnp.where(off >= 48, 0, 255)
+
+
+def pad_rows(ref, w0, off, rows_in, filler):
+    return jnp.where((rows_in >= off) & (rows_in < off + HD), ref[pl.ds(w0, 256), :], filler)
+
+
+def key_bias(n):
+    ki = lax.broadcasted_iota(jnp.int32, (T, 1), 0)
+    return jnp.where(lax.rem(ki, 64) * RATE + ki // 64 < n, 0.0, NEG).astype(BF)
+
+
+def front_kernel(len_ref, src_ref, rows_ref, grad_ref, wq_ref, wk_ref, wv_ref, wo_ref,
+                 x_ref, go_ref, k_ref, v_ref, qT_ref, kT_ref, vT_ref, gT_ref, far_ref, kfT_ref, vfT_ref, top_ref,
+                 ask, req, picked, arrived, perm, qpad, kb, qs, qr, ps, pr, fs, fr):
     n = len_ref[0]
     s = lax.axis_index("seq")
     peers = [seq_peer(s, d) for d in range(1, 8)]
     greet(peers)
     src = src_ref[...]
-    owner = src // T
-    line = src - owner * T
+    sixteen = lax.broadcasted_iota(jnp.int32, (16, T), 0)
+    line = lax.rem(src, T)
+    parts = jnp.where(sixteen == 0, line // 32, jnp.where(sixteen == 1, lax.rem(line, 32), src // T))
+    spot = lax.broadcasted_iota(jnp.int32, (T, T), 0)
+    reorder = (lax.broadcasted_iota(jnp.int32, (T, T), 1) == lax.rem(spot, 64) * RATE + spot // 64).astype(BF)
+    parts = nt(parts.astype(F32).astype(BF), reorder)
+    owner = parts[2:3].astype(jnp.int32)
     hot = (lax.broadcasted_iota(jnp.int32, (16, T), 0) == owner).astype(BF)
     before = (lax.broadcasted_iota(jnp.int32, (T, T), 0) < lax.broadcasted_iota(jnp.int32, (T, T), 1)).astype(BF)
     rank = jnp.sum(nn(hot, before) * hot.astype(F32), axis=0, keepdims=True)
     slot = owner.astype(F32) * 128.0 + rank
     where = lax.broadcasted_iota(jnp.int32, (T, T), 0).astype(F32)
     permT = (where == slot).astype(BF)
-    high = line // 32
-    low = line - high * 32
-    eight = lax.broadcasted_iota(jnp.int32, (16, T), 0)
-    parts = jnp.where(eight == 0, high, jnp.where(eight == 1, low, 0)).astype(F32).astype(BF)
-    got = nt(parts, permT)
+    got = nt(parts.astype(BF), permT)
     lines = got[0:1] * 32.0 + got[1:2]
     for o in range(8):
         ask[o] = jnp.broadcast_to(lines[:, o * 128:(o + 1) * 128], (8, 128))
@@ -270,6 +277,7 @@
     perm[...] = permT.T
     qi = lax.broadcasted_iota(jnp.int32, (1, T), 1)
     ok = (lax.rem(qi, 64) * RATE + qi // 64) < n
+    go_ref[...] = nn(reorder, grad_ref[...]).astype(BF)
     gT_ref[...] = jnp.where(ok, nt(wo_ref[...], go_ref[...]), 0.0).astype(BF)
     cells = lax.broadcasted_iota(jnp.int32, (128, T), 1).astype(F32)
     rows = rows_ref[...]
@@ -303,6 +311,19 @@
     qT_ref[...] = nn(x, wq_ref[...]).astype(BF).T
     kT_ref[...] = k.T
     vT_ref[...] = v.T
+    rows_in = lax.broadcasted_iota(jnp.int32, (256, T), 0)
+    cols_in = lax.broadcasted_iota(jnp.int32, (T, 256), 1)
+    kbias = key_bias(n)
+
+    @pl.loop(0, HEADS)
+    def _(h):
+        w0, off, free = window(h)
+        qpad[...] = pad_rows(qT_ref, w0, off, rows_in, jnp.where(rows_in == free, 1.0, 0.0).astype(BF))
+        kb[...] = jnp.where(cols_in == free, kbias, k_ref[:, pl.ds(w0, 256)])
+        for ci in range(T // QC):
+            sl = slice(ci * QC, (ci + 1) * QC)
+            top_ref[h, :, sl] = jnp.max(nn(kb[...], qpad[:, sl]), axis=0, keepdims=True)
+
     for c in fars:
         c.wait_recv()
     kfT_ref[...] = far_ref[:, 0:D].T
@@ -317,11 +338,12 @@
     return pl.pallas_call(
         front_kernel,
         in_specs=[sm()] + [vm()] * 7,
-        out_specs=[vm()] * 10,
-        out_shape=[s((T, D), BF)] * 3 + [s((D, T), BF)] * 4 + [s((FAR, 2 * D), BF)] + [s((D, FAR), BF)] * 2,
+        out_specs=[vm()] * 12,
+        out_shape=[s((T, D), BF)] * 4 + [s((D, T), BF)] * 4 + [s((FAR, 2 * D), BF)] + [s((D, FAR), BF)] * 2
+        + [s((HEADS, 1, T), F32)],
         scratch_shapes=[
             pltpu.VMEM((8, 8, 128), F32), pltpu.VMEM((7, 8, 128), F32), pltpu.VMEM((7, 128, D), BF),
-            pltpu.VMEM((T, D), BF), pltpu.VMEM((T, T), BF),
+            pltpu.VMEM((T, D), BF), pltpu.VMEM((T, T), BF), pltpu.VMEM((256, T), BF), pltpu.VMEM((T, 256), BF),
         ] + [dma((7,))] * 6,
         compiler_params=pltpu.CompilerParams(
             vmem_limit_bytes=60 << 20, collective_id=2, has_side_effects=True),
@@ -513,7 +535,7 @@
 
 def tail_kernel(x_ref, go_ref, attT_ref, dqT_ref, dk0_ref, dv0_ref, dk32_ref, dv32_ref, dkf_ref, dvf_ref, fin0_ref,
                 wq_ref, wk_ref, wv_ref, wo_ref, enc_ref, emb_ref, out0_ref, out1_ref,
-                part, rx, dk, dv, fin1, bs, br, g0s, g0r, h0s, h0r, g1s, g1r, h1s, h1r, *scratch):
+                part, rx, dk, dv, fin1, home, bs, br, g0s, g0r, h0s, h0r, g1s, g1r, h1s, h1r, *scratch):
     greet(all_peers())
     red = Reduction(*scratch[:7], fin1, *scratch[7:])
     first = Spread(red, fin0_ref, out0_ref, g0s, g0r, h0s, h0r)
@@ -530,7 +552,10 @@
     red.rows(3, nn(attT_ref[HALF:, :], go_ref[...]))
     red.pair(3).start()
     first.middle()
-    enc_ref[...] = (x_ref[...].astype(F32) + nn(attT_ref[...].T, wo_ref[...])).astype(BF)
+    enc = (x_ref[...].astype(F32) + nn(attT_ref[...].T, wo_ref[...])).astype(BF)
+    spot = lax.broadcasted_iota(jnp.int32, (T, T), 0)
+    home[...] = (lax.broadcasted_iota(jnp.int32, (T, T), 1) == lax.rem(spot, RATE) * 64 + spot // RATE).astype(BF)
+    enc_ref[...] = nn(home[...], enc).astype(BF)
     add_back(backs, part, rx, 1, dk32_ref, dv32_ref, dk, dv)
     red.columns(1, nt(xT, dk[...]))
     red.pair(1).start()
@@ -541,7 +566,8 @@
     e = nn(wq_ref[...], dqT_ref[...])
     e = e + nn(wk_ref[:, 0:HALF], dk0_ref[...]) + nn(wk_ref[:, HALF:D], dk[...])
     e = e + nn(wv_ref[:, 0:HALF], dv0_ref[...]) + nn(wv_ref[:, HALF:D], dv[...])
-    emb_ref[...] = (go_ref[...].astype(F32) + e.T).astype(BF)
+    emb = (go_ref[...].astype(F32) + e.T).astype(BF)
+    emb_ref[...] = nn(home[...], emb).astype(BF)
     red.after_first()
     red.after_second()
     red.after_third()
@@ -565,7 +591,8 @@
         out_shape=[s((T, D), BF)] * 2 + [s((2, 4, HALF, HALF), BF)] * 2,
         scratch_shapes=[
             pltpu.VMEM((FAR, D), BF), pltpu.VMEM((7, 64, D), BF),
-            pltpu.VMEM((HALF, T), BF), pltpu.VMEM((HALF, T), BF), pltpu.VMEM((3, 32, HALF), BF), dma((7,)), dma((7,)),
+            pltpu.VMEM((HALF, T), BF), pltpu.VMEM((HALF, T), BF), pltpu.VMEM((3, 32, HALF), BF), pltpu.VMEM((T, T), BF),
+            dma((7,)), dma((7,)),
         ] + [dma((2, 3, 3)), dma((2, 3, 3)), dma(()), dma(())] * 2 + reduction_scratch(),
         compiler_params=pltpu.CompilerParams(
             vmem_limit_bytes=60 << 20, collective_id=3, has_side_effects=True),
@@ -573,23 +600,14 @@
     )(*args)
 
 
-def to_local(a):
-    return a.reshape(64, RATE, -1).transpose(1, 0, 2).reshape(T, -1)
-
-
-def from_local(a):
-    return a.reshape(RATE, 64, -1).transpose(1, 0, 2).reshape(T, -1)
-
-
 def per_device(tile_embed, tile_source, slide_len, grad_out, w_query, w_key, w_value, w_out):
-    source = to_local(tile_source[0]).reshape(1, T)
+    source = tile_source.reshape(1, T)
     length = slide_len[0]
     lens = jnp.stack([length - lax.axis_index("seq") * T, length]).astype(jnp.int32)
-    go = to_local(grad_out[0])
-    x, k, v, qT, kT, vT, gT, far, kfT, vfT = front_all(
-        lens, source, tile_embed[0], go, w_query, w_key, w_value, w_out
+    x, go, k, v, qT, kT, vT, gT, far, kfT, vfT, top = front_all(
+        lens, source, tile_embed[0], grad_out[0], w_query, w_key, w_value, w_out
     )
-    attT, dqT, dk0, dv0, dk32, dv32, dkf, dvf, fin0 = attn(lens, k, v, qT, kT, vT, gT, far, kfT, vfT, x, go)
+    attT, dqT, dk0, dv0, dk32, dv32, dkf, dvf, fin0 = attn(lens, k, v, qT, kT, vT, gT, far, kfT, vfT, top, x, go)
     enc, emb, out0, out1 = tail_all(
         x, go, attT, dqT, dk0, dv0, dk32, dv32, dkf, dvf, fin0, w_query, w_key, w_value, w_out
     )
@@ -597,7 +615,7 @@
     for i in range(4):
         along_rows = [jnp.concatenate([o[0, i], o[1, i]], axis=0 if i < 3 else 1) for o in (out0, out1)]
         summed.append(jnp.concatenate(along_rows, axis=1 if i < 3 else 0).astype(F32))
-    return (from_local(enc)[None], from_local(emb)[None], summed[0], summed[1], summed[2], summed[3])
+    return (enc[None], emb[None], summed[0], summed[1], summed[2], summed[3])
 
 
 def solution(mesh):

time: 255 us -> 240 us (0.941)
  Pallas kernels: 234 us -> 225 us
  local copies, waits for them, and re-layouts: 10.9 us -> 6.6 us
    pallas_call x1, Pallas kernels: 102 us -> 90.2 us  [attn(): pl.pallas_call(attn_kernel, grid=(HEADS,), in_specs=[sm()] + [vm()] * 12,...]
    transpose x3 -> x0, local copies, waits for them, and re-layouts: 5.89 us -> none  [the longest x2 5.83 us: from_local(): return a.reshape(RATE, 64, -1).transpose(1, 0, 2).reshape(T, -1)]
    another operation x3 -> x0, local copies, waits for them, and re-layouts: 3.78 us -> none  [the longest x2 3.09 us: to_local(): return a.reshape(64, RATE, -1).transpose(1, 0, 2).reshape(T, -1)]
    pallas_call x1, Pallas kernels: 64.1 us -> 67.4 us  [front_all(): pl.pallas_call(front_kernel, in_specs=[sm()] + [vm()] * 7, out_specs=[vm(...]
    unnamed x7 -> x6, local copies, waits for them, and re-layouts: 0.52 us -> 3.69 us
where the time goes in v5:
time: 240 us
  Pallas kernels  225 us (94%)
  other arithmetic  6.85 us (3%)
  local copies, waits for them, and re-layouts  6.6 us (3%)
    pallas_call x1, Pallas kernels, attn(): pl.pallas_call(attn_kernel, grid=(HEADS,), in_specs=[sm()] + [vm()] * 12,...  90.2 us
    pallas_call x1, Pallas kernels, front_all(): pl.pallas_call(front_kernel, in_specs=[sm()] + [vm()] * 7, out_specs=[vm(...  67.4 us
    pallas_call x1, Pallas kernels, tail_all(): pl.pallas_call(tail_kernel, in_specs=[vm()] * 15, out_specs=[vm()] * 4, o...  67.2 us
    convert_element_type x4, other arithmetic, per_device(): jnp.concatenate(along_rows, axis=1 if i < 3 else 0).astype(F32)  6.27 us

profile of v5, /device:TPU:1, one launch (start us, length us, event | category | flops | bytes accessed | tf_op | source)
XLA Modules:
  0.0 239.6 jit_solution(12301739790323393810)
XLA Ops:
  1.3 0.6 pad_add_fusion.len_ref
  1.9 67.4 %shard_map.127 = (bf16[1024,768]{1,0:T(8,128)(2,1)}, bf16[1024,768]{1,0:T(8,128)(2,1)}, bf16[1024,768]{1,0:T(8,128)(2,1)}, bf16[1024,768]{1,0:T(8,128)(2,1)}, bf...) custom-call(s32[2]{0:T(128)} %pad_add_fusion.len_ref, ...), custom_call_target="tpu_custom_call" | custom-call | flops 7247757312 | bytes 20971520 | tf_op jit(solution)/shard_map/pallas_call | solution.py:338
  69.3 90.2 %shard_map.128 = (bf16[768,1024]{1,0:T(8,128)(2,1)}, bf16[768,1024]{1,0:T(8,128)(2,1)}, bf16[384,1024]{1,0:T(8,128)(2,1)}, bf16[384,1024]{1,0:T(8,128)(2,1)}, f3...) custom-call(s32[2]{0:T(128)} %pad_add_fusion.len_ref, ...), custom_call_target="tpu_custom_call" | custom-call | flops 60397977600 | bytes 31457280 | tf_op jit(solution)/shard_map/pallas_call | solution.py:165
  159.5 67.2 %shard_map.129 = (bf16[1024,768]{1,0:T(8,128)(2,1)}, bf16[1024,768]{1,0:T(8,128)(2,1)}, bf16[2,4,384,384]{3,2,1,0:T(8,128)(2,1)}, bf16[2,4,384,384]{3,2,1,0:T(8,128)(2,1)}) custom-call(bf16[1024,768]{1,0:T(8,128)(2,1)} %get-tuple-element.31.x_ref, bf16[1024,768]{1,0:T(8,128)(2,1)} %get-tuple-element.32.go_ref, bf16[768,1024]{1,0:T(8,128)(2,1)} %get-tuple-element.43.attT_ref, ...), custom_call_target="tpu_custom_call" | custom-call | flops 9663676416 | bytes 31457280 | tf_op jit(solution)/shard_map/pallas_call | solution.py:587
  226.7 2.9 %slice_bitcast_fusion.1 = (bf16[384,384]{1,0:T(8,128)(2,1)S(1)}, bf16[384,384]{1,0:T(8,128)(2,1)S(1)}, bf16[384,384]{1,0:T(8,128)(2,1)S(1)}, bf16[384,384]{1,0:T...) fusion(bf16[2,4,384,384]{3,2,1,0:T(8,128)(2,1)} %get-tuple-elem, ...), kind=kLoop, calls=%fused_computation.5 | loop fusion | bytes 9437184 | tf_op jit(solution)/shard_map/squeeze | solution.py:616
  229.6 1.6 maximum_convert_fusion.3
  231.2 1.6 maximum_convert_fusion.2
  232.8 1.6 maximum_convert_fusion.1
  234.3 0.0 copy-start.1
  234.3 1.6 maximum_convert_fusion
  235.9 0.6 copy-done.1
  236.5 0.0 copy-start
  236.5 1.1 copy.17
  237.6 0.8 copy-done
  238.5 1.1 copy.18
Async XLA Ops:
  234.3 2.1 copy-start.1
  236.5 2.0 copy-start

commit v6 on v5

--- a/solution.py
+++ b/solution.py
@@ -17,47 +17,79 @@
 def nt(a,b): return lax.dot_general(a,b,(((1,),(1,)),((),())),preferred_element_type=F32)
 
 def attn_kernel(len_ref, k_ref, v_ref, qT_ref, kT_ref, vT_ref, gT_ref, far_ref, kfT_ref, vfT_ref, top_ref, x_ref, go_ref,
-                attT_ref, dqT_ref, dk0_ref, dv0_ref, dk32_ref, dv32_ref, dkf_ref, dvf_ref, fin_ref,
+                attT_ref, dqT_ref, dk_ref, dv_ref, dk32_ref, dv32_ref, dkvf_ref, fin_ref, out_ref,
                 qpad, gpad, kb, kfb, m2s, l2s, u2s, w2s, des, dqs, e2s,
-                dk0s, dv0s, dkf0, dvf0, xT, part, rx, bs, br, *scratch):
-    red = Reduction(*scratch[:7], fin_ref, *scratch[7:])
+                dk32, dv32, dkvf, xT, part, rx, sums, bs, br, gs, gr, hs, hr, *scratch):
     h = pl.program_id(0)
+    step = lax.rem(h, 4)
+
+    def reduction(g):
+        return Reduction(scratch[0], *[ref.at[g] for ref in scratch[1:7]], fin_ref.at[g],
+                         *[sem.at[g] for sem in scratch[7:]])
+
+    def spread(g):
+        return Spread(reduction(g), fin_ref.at[g], sums.at[g], gs.at[g], gr.at[g], hs.at[g], hr.at[g])
+
+    def backs(g):
+        return back_copies(part, rx.at[g], bs.at[g], br.at[g])
+
+    now = jnp.maximum(h // 4 - 1, 0)
+    before = jnp.maximum(h // 4 - 2, 0)
+    low = pl.ds(pl.multiple_of(now * GR, 64), GR)
 
     @pl.when(h == 0)
     def _():
         greet(all_peers())
 
-    @pl.when(h == 8)
-    def _():
-        part[:, 0:HALF] = dkf0[...].T
-        part[:, HALF:D] = dvf0[...].T
-        for c in back_copies(part, rx, bs, br):
+    @pl.when(h == 4)
+    def _():
+        xT[...] = x_ref[...].T
+
+    @pl.when((step == 0) & (h >= 4))
+    def _():
+        part[...] = dkvf[lax.rem(now, 2)].T
+        for c in backs(now):
             c.start()
-        xT[...] = x_ref[...].T
-        red.columns(0, nt(xT[...], dqT_ref[0:HALF, :]))
+        red = reduction(now)
+        red.rows(0, nt(dqT_ref[low, :], xT[...]))
         red.pair(0).start()
-        red.rows(3, nn(attT_ref[0:HALF, :], go_ref[...]))
+        red.rows(3, nn(attT_ref[low, :], go_ref[...]))
         red.pair(3).start()
 
-    @pl.when(h == 10)
-    def _():
-        add_back(back_copies(part, rx, bs, br), part, rx, 0, dk0s, dv0s, dk0_ref, dv0_ref)
-        red.columns(1, nt(xT[...], dk0_ref[...]))
+    @pl.when((step == 0) & (h >= 8))
+    def _():
+        reduction(before).after_second()
+
+    @pl.when((step == 1) & (h >= 4))
+    def _():
+        slot = lax.rem(now, 2)
+        add_back(backs(now), part, rx.at[now], now, dk32.at[slot], dv32.at[slot], dk_ref.at[low], dv_ref.at[low])
+        red = reduction(now)
+        red.rows(1, nt(dk_ref[low, :], xT[...]))
         red.pair(1).start()
-        red.columns(2, nt(xT[...], dv0_ref[...]))
+        red.rows(2, nt(dv_ref[low, :], xT[...]))
         red.pair(2).start()
 
-    @pl.when(h == 11)
-    def _():
-        red.after_pair()
-
-    @pl.when(h == 13)
-    def _():
-        red.after_first()
-
-    @pl.when(h == 14)
-    def _():
-        red.after_second()
+    @pl.when((step == 1) & (h >= 8))
+    def _():
+        reduction(before).after_third()
+        spread(before).begin()
+
+    @pl.when((step == 2) & (h >= 4))
+    def _():
+        reduction(now).after_pair()
+
+    @pl.when((step == 2) & (h >= 8))
+    def _():
+        spread(before).middle()
+
+    @pl.when((step == 3) & (h >= 4))
+    def _():
+        reduction(now).after_first()
+
+    @pl.when((step == 3) & (h >= 8))
+    def _():
+        spread(before).end()
 
     n = len_ref[0]
     nfull = len_ref[1]
@@ -121,43 +153,34 @@
         dqs[:, sl] = nn(kTh, dS)
         dv += nt(gTh, P.astype(BF))
         dk += nt(qT_ref[pl.ds(r, HD), sl], dS)
-    r1 = pl.multiple_of(lax.rem(h, 8) * HD, 16)
-
-    @pl.when(h < 8)
-    def _():
-        dv0s[pl.ds(r1, HD), :] = dv
-        dk0s[pl.ds(r1, HD), :] = dk * scale
-
-    @pl.when(h >= 8)
-    def _():
-        dv32_ref[pl.ds(r1, HD), :] = dv
-        dk32_ref[pl.ds(r1, HD), :] = dk * scale
-
+    r1 = pl.multiple_of(step * HD, 16)
+    slot = lax.rem(h // 4, 2)
+    dv32[slot, pl.ds(r1, HD), :] = dv
+    dk32[slot, pl.ds(r1, HD), :] = dk * scale
     P2 = e2s[...] * jnp.where(mine, w2s[:, pl.ds(wq, 128)], 0.0)
     dP2 = nn(far_ref[:, pl.ds(pl.multiple_of(w0 + D, 128), 256)], gpad[:, pl.ds(wq, 128)])
     dS2 = (P2 * (dP2 - des[:, pl.ds(wq, 128)])).astype(BF)
     dvf = nt(gT_ref[pl.ds(r, HD), pl.ds(wq, 128)], P2.astype(BF)).astype(BF)
     dkf = (nt(qT_ref[pl.ds(r, HD), pl.ds(wq, 128)], dS2) * scale).astype(BF)
 
-    @pl.when(h < 8)
-    def _():
-        dvf0[pl.ds(r1, HD), :] = dvf
-        dkf0[pl.ds(r1, HD), :] = dkf
-
-    @pl.when(h >= 8)
-    def _():
-        dvf_ref[pl.ds(r1, HD), :] = dvf
-        dkf_ref[pl.ds(r1, HD), :] = dkf
-
+    dkvf[slot, pl.ds(r1, HD), :] = dkf
+    dkvf[slot, pl.ds(pl.multiple_of(r1 + GR, 16), HD), :] = dvf
     dqs[:, pl.ds(wq, 128)] += nn(kfT_ref[pl.ds(r, HD), :], dS2)
     dqT_ref[pl.ds(r, HD), :] = (dqs[...] * scale).astype(BF)
 
     @pl.when(h == HEADS - 1)
     def _():
-        red.after_third()
-        for c in back_copies(part, rx, bs, br):
-            c.wait_send()
-        red.finish()
+        reduction(2).after_second()
+        dk32_ref[...] = dk32[1]
+        dv32_ref[...] = dv32[1]
+        dkvf_ref[...] = dkvf[1]
+        reduction(2).after_third()
+        for g in range(3):
+            reduction(g).finish()
+        for g in range(2):
+            spread(g).finish()
+        out_ref[...] = sums[...]
+
 
 def attn(lens, *arrs):
     s = jax.ShapeDtypeStruct
@@ -167,16 +190,16 @@
         grid=(HEADS,),
         in_specs=[sm()] + [vm()] * 12,
         out_specs=[vm()] * 9,
-        out_shape=[s((D, T), BF)] * 2 + [s((HALF, T), BF)] * 2 + [s((HALF, T), F32)] * 2 + [s((HALF, FAR), BF)] * 2
-        + [s((3, 32, HALF), BF)],
+        out_shape=[s((D, T), BF)] * 2 + [s((3 * GR, T), BF)] * 2 + [s((GR, T), F32)] * 2 + [s((2 * GR, FAR), BF)]
+        + [s((3, 3, 16, HALF), BF), s((2, 2, 4, GR, HALF), BF)],
         scratch_shapes=[
             pltpu.VMEM((256, T), BF), pltpu.VMEM((256, T), BF), pltpu.VMEM((T, 256), BF), pltpu.VMEM((FAR, 256), BF),
             pltpu.VMEM((1, T), F32), pltpu.VMEM((1, T), F32), pltpu.VMEM((HD, T), F32), pltpu.VMEM((1, T), F32),
             pltpu.VMEM((1, T), F32), pltpu.VMEM((HD, T), F32), pltpu.VMEM((FAR, 128), F32),
-            pltpu.VMEM((HALF, T), F32), pltpu.VMEM((HALF, T), F32), pltpu.VMEM((HALF, FAR), BF),
-            pltpu.VMEM((HALF, FAR), BF), pltpu.VMEM((D, T), BF), pltpu.VMEM((FAR, D), BF), pltpu.VMEM((7, 64, D), BF),
-            dma((7,)), dma((7,)),
-        ] + reduction_scratch(),
+            pltpu.VMEM((2, GR, T), F32), pltpu.VMEM((2, GR, T), F32), pltpu.VMEM((2, 2 * GR, FAR), BF),
+            pltpu.VMEM((D, T), BF), pltpu.VMEM((FAR, 2 * GR), BF), pltpu.VMEM((3, 7, 64, 2 * GR), BF),
+            pltpu.VMEM((2, 2, 4, GR, HALF), BF), dma((3, 7)), dma((3, 7)), dma((2, 2, 3, 3)), dma((2, 2, 3, 3)), dma((2,)), dma((2,)),
+        ] + reduction_scratch(3),
         compiler_params=pltpu.CompilerParams(
             vmem_limit_bytes=60 << 20, collective_id=4, has_side_effects=True),
         cost_estimate=pl.CostEstimate(flops=100 * T * D * D, bytes_accessed=30 << 20, transcendentals=0),
@@ -352,7 +375,8 @@
 
 
 HALF = D // 2
-GH = HEADS // 2
+GH = HEADS // 4
+GR = GH * HD
 
 
 def copy_to(src, dst, ssem, rsem, peer):
@@ -391,9 +415,9 @@
             for d in (1, 2, 3):
                 other = (self.at(p, level) + d) % 4
                 if level == 0:
-                    src, dst = self.acc.at[other, pl.ds(p * 128, 128)], self.rx1.at[p, d - 1]
+                    src, dst = self.acc.at[other, pl.ds(p * 64, 64)], self.rx1.at[p, d - 1]
                 elif level == 1:
-                    src, dst = self.r2.at[p, pl.ds(pl.multiple_of(other * 32, 32), 32)], self.rx2.at[p, d - 1]
+                    src, dst = self.r2.at[p, pl.ds(pl.multiple_of(other * 16, 16), 16)], self.rx2.at[p, d - 1]
                 else:
                     own = self.rx3.at[p, self.at(p, 2)]
                     src, dst = own, own
@@ -405,10 +429,6 @@
         for c in copies:
             c.start()
 
-    def columns(self, i, value):
-        self.grads[i, 0] = value[:HALF]
-        self.grads[i, 1] = value[HALF:]
-
     def rows(self, i, value):
         self.grads[i, 0] = value[:, :HALF]
         self.grads[i, 1] = value[:, HALF:]
@@ -417,6 +437,8 @@
         for i in (0, 3, 1, 2):
             self.pair(i).wait_recv()
             self.acc[i] = self.grads[i, self.core] + self.crx[i]
+        for i in range(4):
+            self.pair(i).wait_send()
         self.start(self.wave(0))
 
     def after_first(self):
@@ -424,7 +446,7 @@
         for p in range(3):
             for c in copies[3 * p:3 * p + 3]:
                 c.wait_recv()
-            self.r2[p] = self.acc[self.at(p, 0), p * 128:(p + 1) * 128] + self.rx1[p, 0] + self.rx1[p, 1] + self.rx1[p, 2]
+            self.r2[p] = self.acc[self.at(p, 0), p * 64:(p + 1) * 64] + self.rx1[p, 0] + self.rx1[p, 1] + self.rx1[p, 2]
             self.start(self.wave(1, (p,)))
 
     def after_second(self):
@@ -432,7 +454,7 @@
         for p in range(3):
             for c in copies[3 * p:3 * p + 3]:
                 c.wait_recv()
-            own = self.r2[p, pl.ds(pl.multiple_of(self.at(p, 1) * 32, 32), 32)]
+            own = self.r2[p, pl.ds(pl.multiple_of(self.at(p, 1) * 16, 16), 16)]
             self.rx3[p, self.at(p, 2)] = own + self.rx2[p, 0] + self.rx2[p, 1] + self.rx2[p, 2]
             self.start(self.wave(2, (p,)))
 
@@ -444,19 +466,19 @@
             self.fin[p] = (self.rx3[p, 0] + self.rx3[p, 1] + self.rx3[p, 2] + self.rx3[p, 3]).astype(BF)
 
     def finish(self):
-        for i in range(4):
-            self.pair(i).wait_send()
         for level in range(3):
             for c in self.wave(level):
                 c.wait_send()
 
 
-def reduction_scratch():
+def reduction_scratch(*groups):
     dma = pltpu.SemaphoreType.DMA
     return [
-        pltpu.VMEM((4, 2, HALF, HALF), F32), pltpu.VMEM((4, HALF, HALF), F32), pltpu.VMEM((4, HALF, HALF), F32),
-        pltpu.VMEM((3, 3, 128, HALF), F32), pltpu.VMEM((3, 3, 32, HALF), F32), pltpu.VMEM((3, 4, 32, HALF), F32),
-        pltpu.VMEM((3, 128, HALF), F32), dma((4,)), dma((4,)), dma((3, 3, 3)), dma((3, 3, 3)),
+        pltpu.VMEM((4, 2, GR, HALF), F32), pltpu.VMEM(groups + (4, GR, HALF), F32),
+        pltpu.VMEM(groups + (4, GR, HALF), F32), pltpu.VMEM(groups + (3, 3, 64, HALF), F32),
+        pltpu.VMEM(groups + (3, 3, 16, HALF), F32), pltpu.VMEM(groups + (3, 4, 16, HALF), F32),
+        pltpu.VMEM(groups + (3, 64, HALF), F32), dma(groups + (4,)), dma(groups + (4,)),
+        dma(groups + (3, 3, 3)), dma(groups + (3, 3, 3)),
     ]
 
 
@@ -468,7 +490,7 @@
         made = []
         for p in parts:
             a, b = self.red.at(p, 0), self.red.at(p, 1)
-            rows = pl.ds(pl.multiple_of(p * 128 + b * 32, 32), 32) if level == 1 else pl.ds(p * 128, 128)
+            rows = pl.ds(pl.multiple_of(p * 64 + b * 16, 16), 16) if level == 1 else pl.ds(p * 64, 64)
             here = self.out.at[self.red.core, a, rows]
             for d in (1, 2, 3):
                 made.append(copy_to(here, here, self.gs.at[level, p, d - 1], self.gr.at[level, p, d - 1],
@@ -481,7 +503,7 @@
 
     def begin(self):
         for p in range(3):
-            rows = pl.ds(pl.multiple_of(p * 128 + self.red.at(p, 1) * 32, 32), 32)
+            rows = pl.ds(pl.multiple_of(p * 64 + self.red.at(p, 1) * 16, 16), 16)
             self.out[self.red.core, self.red.at(p, 0), rows] = self.fin[p]
         for c in self.wave(1):
             c.start()
@@ -517,65 +539,65 @@
     for d in range(1, 8):
         copies[d - 1].wait_recv()
         back = back + rx[d - 1].astype(F32)
+    for c in copies:
+        c.wait_send()
     bT = back.T
     zero = jnp.zeros((HD, 64), F32)
     for i in range(GH):
-        h = group * GH + i
         r = slice(i * HD, (i + 1) * HD)
-        w = slice((h // 2) * 128, (h // 2) * 128 + 128)
+        w = pl.ds(pl.multiple_of((group * 2 + i // 2) * 128, 128), 128)
         bk = bT[i * HD:(i + 1) * HD, :]
-        bv = bT[HALF + i * HD:HALF + (i + 1) * HD, :]
-        pk = [bk, zero] if h % 2 == 0 else [zero, bk]
-        pv = [bv, zero] if h % 2 == 0 else [zero, bv]
+        bv = bT[GR + i * HD:GR + (i + 1) * HD, :]
+        pk = [bk, zero] if i % 2 == 0 else [zero, bk]
+        pv = [bv, zero] if i % 2 == 0 else [zero, bv]
         dk[r, :] = dk32[r, :].astype(BF)
         dv[r, :] = dv32[r, :].astype(BF)
         dk[r, w] = (dk32[r, w] + jnp.concatenate(pk, axis=1)).astype(BF)
         dv[r, w] = (dv32[r, w] + jnp.concatenate(pv, axis=1)).astype(BF)
 
 
-def tail_kernel(x_ref, go_ref, attT_ref, dqT_ref, dk0_ref, dv0_ref, dk32_ref, dv32_ref, dkf_ref, dvf_ref, fin0_ref,
-                wq_ref, wk_ref, wv_ref, wo_ref, enc_ref, emb_ref, out0_ref, out1_ref,
-                part, rx, dk, dv, fin1, home, bs, br, g0s, g0r, h0s, h0r, g1s, g1r, h1s, h1r, *scratch):
+def tail_kernel(x_ref, go_ref, attT_ref, dqT_ref, dk_ref, dv_ref, dk32_ref, dv32_ref, dkvf_ref, fin_ref,
+                wq_ref, wk_ref, wv_ref, wo_ref, enc_ref, emb_ref, out2_ref, out3_ref,
+                part, rx, dk, dv, fin3, home, bs, br, g2s, g2r, h2s, h2r, g3s, g3r, h3s, h3r, *scratch):
     greet(all_peers())
-    red = Reduction(*scratch[:7], fin1, *scratch[7:])
-    first = Spread(red, fin0_ref, out0_ref, g0s, g0r, h0s, h0r)
-    second = Spread(red, fin1, out1_ref, g1s, g1r, h1s, h1r)
-    part[:, 0:HALF] = dkf_ref[...].T
-    part[:, HALF:D] = dvf_ref[...].T
+    red = Reduction(*scratch[:7], fin3, *scratch[7:])
+    first = Spread(red, fin_ref.at[2], out2_ref, g2s, g2r, h2s, h2r)
+    second = Spread(red, fin3, out3_ref, g3s, g3r, h3s, h3r)
+    part[...] = dkvf_ref[...].T
     backs = back_copies(part, rx, bs, br)
     for c in backs:
         c.start()
     first.begin()
+    last = 3 * GR
     xT = x_ref[...].T
-    red.columns(0, nt(xT, dqT_ref[HALF:, :]))
+    red.rows(0, nt(dqT_ref[last:, :], xT))
     red.pair(0).start()
-    red.rows(3, nn(attT_ref[HALF:, :], go_ref[...]))
+    red.rows(3, nn(attT_ref[last:, :], go_ref[...]))
     red.pair(3).start()
     first.middle()
+    dk[0:last, :] = dk_ref[...]
+    dv[0:last, :] = dv_ref[...]
+    add_back(backs, part, rx, 3, dk32_ref, dv32_ref, dk.at[last:D], dv.at[last:D])
+    red.rows(1, nt(dk[last:D, :], xT))
+    red.pair(1).start()
+    red.rows(2, nt(dv[last:D, :], xT))
+    red.pair(2).start()
+    first.end()
+    red.after_pair()
     enc = (x_ref[...].astype(F32) + nn(attT_ref[...].T, wo_ref[...])).astype(BF)
     spot = lax.broadcasted_iota(jnp.int32, (T, T), 0)
     home[...] = (lax.broadcasted_iota(jnp.int32, (T, T), 1) == lax.rem(spot, RATE) * 64 + spot // RATE).astype(BF)
     enc_ref[...] = nn(home[...], enc).astype(BF)
-    add_back(backs, part, rx, 1, dk32_ref, dv32_ref, dk, dv)
-    red.columns(1, nt(xT, dk[...]))
-    red.pair(1).start()
-    red.columns(2, nt(xT, dv[...]))
-    red.pair(2).start()
-    first.end()
-    red.after_pair()
-    e = nn(wq_ref[...], dqT_ref[...])
-    e = e + nn(wk_ref[:, 0:HALF], dk0_ref[...]) + nn(wk_ref[:, HALF:D], dk[...])
-    e = e + nn(wv_ref[:, 0:HALF], dv0_ref[...]) + nn(wv_ref[:, HALF:D], dv[...])
+    red.after_first()
+    e = nn(wq_ref[...], dqT_ref[...]) + nn(wk_ref[...], dk[...])
+    red.after_second()
+    e = e + nn(wv_ref[...], dv[...])
     emb = (go_ref[...].astype(F32) + e.T).astype(BF)
-    emb_ref[...] = nn(home[...], emb).astype(BF)
-    red.after_first()
-    red.after_second()
     red.after_third()
     second.begin()
+    emb_ref[...] = nn(home[...], emb).astype(BF)
     second.middle()
     second.end()
-    for c in backs:
-        c.wait_send()
     red.finish()
     first.finish()
     second.finish()
@@ -586,18 +608,50 @@
     dma = pltpu.SemaphoreType.DMA
     return pl.pallas_call(
         tail_kernel,
-        in_specs=[vm()] * 15,
+        in_specs=[vm()] * 14,
         out_specs=[vm()] * 4,
-        out_shape=[s((T, D), BF)] * 2 + [s((2, 4, HALF, HALF), BF)] * 2,
+        out_shape=[s((T, D), BF)] * 2 + [s((2, 4, GR, HALF), BF)] * 2,
         scratch_shapes=[
-            pltpu.VMEM((FAR, D), BF), pltpu.VMEM((7, 64, D), BF),
-            pltpu.VMEM((HALF, T), BF), pltpu.VMEM((HALF, T), BF), pltpu.VMEM((3, 32, HALF), BF), pltpu.VMEM((T, T), BF),
+            pltpu.VMEM((FAR, 2 * GR), BF), pltpu.VMEM((7, 64, 2 * GR), BF),
+            pltpu.VMEM((D, T), BF), pltpu.VMEM((D, T), BF), pltpu.VMEM((3, 16, HALF), BF), pltpu.VMEM((T, T), BF),
             dma((7,)), dma((7,)),
         ] + [dma((2, 3, 3)), dma((2, 3, 3)), dma(()), dma(())] * 2 + reduction_scratch(),
         compiler_params=pltpu.CompilerParams(
             vmem_limit_bytes=60 << 20, collective_id=3, has_side_effects=True),
         cost_estimate=pl.CostEstimate(flops=16 * T * D * D, bytes_accessed=30 << 20, transcendentals=0),
     )(*args)
+
+
+def lay_kernel(out01_ref, out2_ref, out3_ref, gq_ref, gk_ref, gv_ref, gout_ref, stage, sems):
+    copies = []
+    for i, to in enumerate((gq_ref, gk_ref, gv_ref, gout_ref)):
+        blocks = [out01_ref.at[0], out01_ref.at[1], out2_ref, out3_ref]
+        for g, block in enumerate(blocks):
+            whole = jnp.concatenate([block[0, i], block[1, i]], axis=1)
+            rows = slice(g * GR, (g + 1) * GR)
+            if i < 3:
+                stage[4, rows, :] = whole.astype(F32)
+            else:
+                stage[i, rows, :] = whole.astype(F32)
+        if i < 3:
+            stage[i] = stage[4].T
+        copies.append(pltpu.make_async_copy(stage.at[i], to, sems.at[i]))
+        copies[-1].start()
+    for c in copies:
+        c.wait()
+
+
+def lay_all(out01, out2, out3):
+    s = jax.ShapeDtypeStruct
+    return pl.pallas_call(
+        lay_kernel,
+        in_specs=[vm()] * 3,
+        out_specs=[pl.BlockSpec(memory_space=pl.ANY)] * 4,
+        out_shape=[s((D, D), F32)] * 4,
+        scratch_shapes=[pltpu.VMEM((5, D, D), F32), pltpu.SemaphoreType.DMA((4,))],
+        compiler_params=pltpu.CompilerParams(vmem_limit_bytes=40 << 20),
+        cost_estimate=pl.CostEstimate(flops=4 * D * D, bytes_accessed=24 * D * D, transcendentals=0),
+    )(out01, out2, out3)
 
 
 def per_device(tile_embed, tile_source, slide_len, grad_out, w_query, w_key, w_value, w_out):
@@ -607,14 +661,13 @@
     x, go, k, v, qT, kT, vT, gT, far, kfT, vfT, top = front_all(
         lens, source, tile_embed[0], grad_out[0], w_query, w_key, w_value, w_out
     )
-    attT, dqT, dk0, dv0, dk32, dv32, dkf, dvf, fin0 = attn(lens, k, v, qT, kT, vT, gT, far, kfT, vfT, top, x, go)
-    enc, emb, out0, out1 = tail_all(
-        x, go, attT, dqT, dk0, dv0, dk32, dv32, dkf, dvf, fin0, w_query, w_key, w_value, w_out
+    attT, dqT, dk, dv, dk32, dv32, dkvf, fin, out01 = attn(
+        lens, k, v, qT, kT, vT, gT, far, kfT, vfT, top, x, go
     )
-    summed = []
-    for i in range(4):
-        along_rows = [jnp.concatenate([o[0, i], o[1, i]], axis=0 if i < 3 else 1) for o in (out0, out1)]
-        summed.append(jnp.concatenate(along_rows, axis=1 if i < 3 else 0).astype(F32))
+    enc, emb, out2, out3 = tail_all(
+        x, go, attT, dqT, dk, dv, dk32, dv32, dkvf, fin, w_query, w_key, w_value, w_out
+    )
+    summed = lay_all(out01, out2, out3)
     return (enc[None], emb[None], summed[0], summed[1], summed[2], summed[3])
 
 

time: 240 us -> 238 us (level)
  other arithmetic: 6.85 us -> 0.59 us
  Pallas kernels: 225 us -> 230 us
    pallas_call x1, Pallas kernels: 90.2 us -> 105 us  [attn(): pl.pallas_call(attn_kernel, grid=(HEADS,), in_specs=[sm()] + [vm()] * 12,...]
    pallas_call x1 -> x2, Pallas kernels: 67.2 us -> 57.2 us  [the longest x1 53.1 us: tail_all(): pl.pallas_call(tail_kernel, in_specs=[vm()] * 14, out_specs=[vm()] * 4, o...]
    convert_element_type x4 -> x0, other arithmetic: 6.27 us -> none  [per_device(): jnp.concatenate(along_rows, axis=1 if i < 3 else 0).astype(F32)]
    squeeze x1 -> x0, local copies, waits for them, and re-layouts: 2.91 us -> none  [per_device(): o[0, i]]
    unnamed x6 -> x12, local copies, waits for them, and re-layouts: 3.69 us -> 5.65 us
where the time goes in v6:
time: 238 us
  Pallas kernels  230 us (97%)
  local copies, waits for them, and re-layouts  5.65 us (2%)
    pallas_call x1, Pallas kernels, attn(): pl.pallas_call(attn_kernel, grid=(HEADS,), in_specs=[sm()] + [vm()] * 12,...  105 us
    pallas_call x1, Pallas kernels, front_all(): pl.pallas_call(front_kernel, in_specs=[sm()] + [vm()] * 7, out_specs=[vm(...  67.5 us
    pallas_call x1, Pallas kernels, tail_all(): pl.pallas_call(tail_kernel, in_specs=[vm()] * 14, out_specs=[vm()] * 4, o...  53.1 us
    unnamed x12, local copies, waits for them, and re-layouts  5.65 us

profile of v6, /device:TPU:1, one launch (start us, length us, event | category | flops | bytes accessed | tf_op | source)
XLA Modules:
  0.0 237.7 jit_solution(7944458563446313147)
XLA Ops:
  1.3 0.6 pad_add_fusion.len_ref
  1.9 67.5 %shard_map.127 = (bf16[1024,768]{1,0:T(8,128)(2,1)}, bf16[1024,768]{1,0:T(8,128)(2,1)}, bf16[1024,768]{1,0:T(8,128)(2,1)}, bf16[1024,768]{1,0:T(8,128)(2,1)}, bf...) custom-call(s32[2]{0:T(128)} %pad_add_fusion.len_ref, ...), custom_call_target="tpu_custom_call" | custom-call | flops 7247757312 | bytes 20971520 | tf_op jit(solution)/shard_map/pallas_call | solution.py:361
  69.3 105.5 %shard_map.128 = (bf16[768,1024]{1,0:T(8,128)(2,1)}, bf16[768,1024]{1,0:T(8,128)(2,1)}, bf16[576,1024]{1,0:T(8,128)(2,1)}, bf16[576,1024]{1,0:T(8,128)(2,1)}, f3...) custom-call(s32[2]{0:T(128)} %pad_add_fusion.len_ref, ...), custom_call_target="tpu_custom_call" | custom-call | flops 60397977600 | bytes 31457280 | tf_op jit(solution)/shard_map/pallas_call | solution.py:188
  174.8 0.0 copy-start
  174.8 53.1 %shard_map.129 = (bf16[1024,768]{1,0:T(8,128)(2,1)}, bf16[1024,768]{1,0:T(8,128)(2,1)}, bf16[2,4,192,384]{3,2,1,0:T(8,128)(2,1)}, bf16[2,4,192,384]{3,2,1,0:T(8,128)(2,1)}) custom-call(bf16[1024,768]{1,0:T(8,128)(2,1)} %get-tuple-element.35.x_ref, bf16[1024,768]{1,0:T(8,128)(2,1)} %get-tuple-element.36.go_ref, bf16[768,1024]{1,0:T(8,128)(2,1)} %get-tuple-element.47.attT_ref, ...), custom_call_target="tpu_custom_call" | custom-call | flops 9663676416 | bytes 31457280 | tf_op jit(solution)/shard_map/pallas_call | solution.py:609
  227.9 0.0 copy-done
  227.9 0.0 copy-start.1
  228.0 1.3 copy-done.1
  229.2 0.0 copy-start.2
  229.2 1.3 copy-done.2
  230.5 0.0 copy-start.4
  230.5 4.1 %shard_map.130 = (f32[768,768]{1,0:T(8,128)}, f32[768,768]{1,0:T(8,128)}, f32[768,768]{1,0:T(8,128)}, f32[768,768]{1,0:T(8,128)}) custom-call(bf16[2,2,4,192,384]{4,3,2,1,0:T(8,128)(2,1)S(1)} %copy-done, bf16[2,4,192,384]{3,2,1,0:T(8,128)(2,1)S(1)} %copy-done.1, bf16[2,4,192,384]{3,2,1,0:T(8,128)(2,1)S(1)} %copy-done.2), custom_call_target="tpu_custom_call" | custom-call | flops 2359296 | bytes 14155776 | tf_op jit(solution)/shard_map/pallas_call | solution.py:646
  234.6 0.0 copy-done.4
  234.6 0.0 copy-start.3
  234.6 1.1 copy.17
  235.8 0.8 copy-done.3
  236.6 1.1 copy.18
Async XLA Ops:
  174.8 53.1 %copy-start = (bf16[2,2,4,192,384]{4,3,2,1,0:T(8,128)(2,1)S(1)}, bf16[2,2,4,192,384]{4,3,2,1,0:T(8,128)(2,1)}, u32[]{:S(2)}) copy-start(bf16[2,2,4,192,384]{4,3,2,1,0:T(8,128)(2,1)} %get-tuple-element.57.out01_ref) | copy-start | bytes 7077892
  227.9 1.3 copy-start.1
  229.2 1.3 copy-start.2
  230.5 4.1 %copy-start.4 = (bf16[1024,768]{1,0:T(8,128)(2,1)S(1)}, bf16[1024,768]{1,0:T(8,128)(2,1)}, u32[]{:S(2)}) copy-start(bf16[1024,768]{1,0:T(8,128)(2,1)} %get-tuple-element.55) | copy-start | bytes 4718596
  234.6 2.0 copy-start.3

commit v7 on v6

--- a/solution.py
+++ b/solution.py
@@ -17,7 +17,7 @@
 def nt(a,b): return lax.dot_general(a,b,(((1,),(1,)),((),())),preferred_element_type=F32)
 
 def attn_kernel(len_ref, k_ref, v_ref, qT_ref, kT_ref, vT_ref, gT_ref, far_ref, kfT_ref, vfT_ref, top_ref, x_ref, go_ref,
-                attT_ref, dqT_ref, dk_ref, dv_ref, dk32_ref, dv32_ref, dkvf_ref, fin_ref, out_ref,
+                attT_ref, dqT_ref, dk_ref, dv_ref, dk32_ref, dv32_ref, dkvf_ref, fin_ref, acc_ref, out_ref,
                 qpad, gpad, kb, kfb, m2s, l2s, u2s, w2s, des, dqs, e2s,
                 dk32, dv32, dkvf, xT, part, rx, sums, bs, br, gs, gr, hs, hr, *scratch):
     h = pl.program_id(0)
@@ -28,7 +28,7 @@
                          *[sem.at[g] for sem in scratch[7:]])
 
     def spread(g):
-        return Spread(reduction(g), fin_ref.at[g], sums.at[g], gs.at[g], gr.at[g], hs.at[g], hr.at[g])
+        return Spread(reduction(g), fin_ref.at[g], sums, gs, gr, hs, hr)
 
     def backs(g):
         return back_copies(part, rx.at[g], bs.at[g], br.at[g])
@@ -56,11 +56,7 @@
         red.rows(3, nn(attT_ref[low, :], go_ref[...]))
         red.pair(3).start()
 
-    @pl.when((step == 0) & (h >= 8))
-    def _():
-        reduction(before).after_second()
-
-    @pl.when((step == 1) & (h >= 4))
+    @pl.when((step == 2) & (h >= 4))
     def _():
         slot = lax.rem(now, 2)
         add_back(backs(now), part, rx.at[now], now, dk32.at[slot], dv32.at[slot], dk_ref.at[low], dv_ref.at[low])
@@ -72,24 +68,36 @@
 
     @pl.when((step == 1) & (h >= 8))
     def _():
+        reduction(before).after_first()
+
+    @pl.when((step == 2) & (h >= 8))
+    def _():
+        reduction(before).after_second()
+
+    @pl.when((step == 3) & (h >= 8))
+    def _():
         reduction(before).after_third()
-        spread(before).begin()
-
-    @pl.when((step == 2) & (h >= 4))
-    def _():
-        reduction(now).after_pair()
-
-    @pl.when((step == 2) & (h >= 8))
-    def _():
-        spread(before).middle()
 
     @pl.when((step == 3) & (h >= 4))
     def _():
-        reduction(now).after_first()
-
-    @pl.when((step == 3) & (h >= 8))
-    def _():
-        spread(before).end()
+        reduction(now).add_pairs()
+
+    @pl.when((step == 3) & (h >= 4) & (h < 12))
+    def _():
+        red = reduction(now)
+        red.start(red.wave(0))
+
+    @pl.when(h == 11)
+    def _():
+        spread(0).begin()
+
+    @pl.when(h == 13)
+    def _():
+        spread(0).middle()
+
+    @pl.when(h == 14)
+    def _():
+        spread(0).end()
 
     n = len_ref[0]
     nfull = len_ref[1]
@@ -170,15 +178,13 @@
 
     @pl.when(h == HEADS - 1)
     def _():
-        reduction(2).after_second()
         dk32_ref[...] = dk32[1]
         dv32_ref[...] = dv32[1]
         dkvf_ref[...] = dkvf[1]
-        reduction(2).after_third()
-        for g in range(3):
+        acc_ref[...] = scratch[2][2]
+        for g in range(2):
             reduction(g).finish()
-        for g in range(2):
-            spread(g).finish()
+        spread(0).finish()
         out_ref[...] = sums[...]
 
 
@@ -189,16 +195,16 @@
         attn_kernel,
         grid=(HEADS,),
         in_specs=[sm()] + [vm()] * 12,
-        out_specs=[vm()] * 9,
+        out_specs=[vm()] * 10,
         out_shape=[s((D, T), BF)] * 2 + [s((3 * GR, T), BF)] * 2 + [s((GR, T), F32)] * 2 + [s((2 * GR, FAR), BF)]
-        + [s((3, 3, 16, HALF), BF), s((2, 2, 4, GR, HALF), BF)],
+        + [s((2, 3, 16, HALF), BF), s((4, GR, HALF), F32), s((2, 4, GR, HALF), BF)],
         scratch_shapes=[
             pltpu.VMEM((256, T), BF), pltpu.VMEM((256, T), BF), pltpu.VMEM((T, 256), BF), pltpu.VMEM((FAR, 256), BF),
             pltpu.VMEM((1, T), F32), pltpu.VMEM((1, T), F32), pltpu.VMEM((HD, T), F32), pltpu.VMEM((1, T), F32),
             pltpu.VMEM((1, T), F32), pltpu.VMEM((HD, T), F32), pltpu.VMEM((FAR, 128), F32),
             pltpu.VMEM((2, GR, T), F32), pltpu.VMEM((2, GR, T), F32), pltpu.VMEM((2, 2 * GR, FAR), BF),
             pltpu.VMEM((D, T), BF), pltpu.VMEM((FAR, 2 * GR), BF), pltpu.VMEM((3, 7, 64, 2 * GR), BF),
-            pltpu.VMEM((2, 2, 4, GR, HALF), BF), dma((3, 7)), dma((3, 7)), dma((2, 2, 3, 3)), dma((2, 2, 3, 3)), dma((2,)), dma((2,)),
+            pltpu.VMEM((2, 4, GR, HALF), BF), dma((3, 7)), dma((3, 7)), dma((2, 3, 3)), dma((2, 3, 3)), dma(()), dma(()),
         ] + reduction_scratch(3),
         compiler_params=pltpu.CompilerParams(
             vmem_limit_bytes=60 << 20, collective_id=4, has_side_effects=True),
@@ -433,13 +439,12 @@
         self.grads[i, 0] = value[:, :HALF]
         self.grads[i, 1] = value[:, HALF:]
 
-    def after_pair(self):
+    def add_pairs(self):
         for i in (0, 3, 1, 2):
             self.pair(i).wait_recv()
             self.acc[i] = self.grads[i, self.core] + self.crx[i]
         for i in range(4):
             self.pair(i).wait_send()
-        self.start(self.wave(0))
 
     def after_first(self):
         copies = self.wave(0)
@@ -556,76 +561,89 @@
         dv[r, w] = (dv32[r, w] + jnp.concatenate(pv, axis=1)).astype(BF)
 
 
-def tail_kernel(x_ref, go_ref, attT_ref, dqT_ref, dk_ref, dv_ref, dk32_ref, dv32_ref, dkvf_ref, fin_ref,
-                wq_ref, wk_ref, wv_ref, wo_ref, enc_ref, emb_ref, out2_ref, out3_ref,
-                part, rx, dk, dv, fin3, home, bs, br, g2s, g2r, h2s, h2r, g3s, g3r, h3s, h3r, *scratch):
+def tail_kernel(x_ref, go_ref, attT_ref, dqT_ref, dk_ref, dv_ref, dk32_ref, dv32_ref, dkvf_ref, fin_ref, acc_ref,
+                wq_ref, wk_ref, wv_ref, wo_ref, enc_ref, emb_ref, out1_ref, out2_ref, out3_ref,
+                part, rx, dk, dv, fin2, fin3, home, bs, br, *scratch):
     greet(all_peers())
-    red = Reduction(*scratch[:7], fin3, *scratch[7:])
-    first = Spread(red, fin_ref.at[2], out2_ref, g2s, g2r, h2s, h2r)
-    second = Spread(red, fin3, out3_ref, g3s, g3r, h3s, h3r)
+    sems, older, newer = scratch[:12], scratch[12:18], scratch[18:]
+    red2 = Reduction(None, None, acc_ref, *older[:4], fin2, None, None, *older[4:])
+    red3 = Reduction(*newer[:7], fin3, *newer[7:])
+    spread1 = Spread(red2, fin_ref.at[1], out1_ref, *sems[0:4])
+    spread2 = Spread(red2, fin2, out2_ref, *sems[4:8])
+    spread3 = Spread(red3, fin3, out3_ref, *sems[8:12])
     part[...] = dkvf_ref[...].T
     backs = back_copies(part, rx, bs, br)
     for c in backs:
         c.start()
-    first.begin()
+    spread1.begin()
+    red2.start(red2.wave(0))
     last = 3 * GR
     xT = x_ref[...].T
-    red.rows(0, nt(dqT_ref[last:, :], xT))
-    red.pair(0).start()
-    red.rows(3, nn(attT_ref[last:, :], go_ref[...]))
-    red.pair(3).start()
-    first.middle()
+    red3.rows(0, nt(dqT_ref[last:, :], xT))
+    red3.pair(0).start()
+    red3.rows(3, nn(attT_ref[last:, :], go_ref[...]))
+    red3.pair(3).start()
+    spread1.middle()
     dk[0:last, :] = dk_ref[...]
     dv[0:last, :] = dv_ref[...]
-    add_back(backs, part, rx, 3, dk32_ref, dv32_ref, dk.at[last:D], dv.at[last:D])
-    red.rows(1, nt(dk[last:D, :], xT))
-    red.pair(1).start()
-    red.rows(2, nt(dv[last:D, :], xT))
-    red.pair(2).start()
-    first.end()
-    red.after_pair()
-    enc = (x_ref[...].astype(F32) + nn(attT_ref[...].T, wo_ref[...])).astype(BF)
     spot = lax.broadcasted_iota(jnp.int32, (T, T), 0)
     home[...] = (lax.broadcasted_iota(jnp.int32, (T, T), 1) == lax.rem(spot, RATE) * 64 + spot // RATE).astype(BF)
+    red2.after_first()
+    add_back(backs, part, rx, 3, dk32_ref, dv32_ref, dk.at[last:D], dv.at[last:D])
+    red3.rows(1, nt(dk[last:D, :], xT))
+    red3.pair(1).start()
+    red3.rows(2, nt(dv[last:D, :], xT))
+    red3.pair(2).start()
+    spread1.end()
+    red2.after_second()
+    red3.add_pairs()
+    red3.start(red3.wave(0))
+    enc = (x_ref[...].astype(F32) + nn(attT_ref[...].T, wo_ref[...])).astype(BF)
+    red2.after_third()
+    spread2.begin()
     enc_ref[...] = nn(home[...], enc).astype(BF)
-    red.after_first()
+    red3.after_first()
+    spread2.middle()
     e = nn(wq_ref[...], dqT_ref[...]) + nn(wk_ref[...], dk[...])
-    red.after_second()
+    red3.after_second()
+    spread2.end()
     e = e + nn(wv_ref[...], dv[...])
+    red3.after_third()
+    spread3.begin()
     emb = (go_ref[...].astype(F32) + e.T).astype(BF)
-    red.after_third()
-    second.begin()
+    spread3.middle()
     emb_ref[...] = nn(home[...], emb).astype(BF)
-    second.middle()
-    second.end()
-    red.finish()
-    first.finish()
-    second.finish()
+    spread3.end()
+    red2.finish()
+    red3.finish()
+    for spread in (spread1, spread2, spread3):
+        spread.finish()
 
 
 def tail_all(*args):
     s = jax.ShapeDtypeStruct
     dma = pltpu.SemaphoreType.DMA
+    older = reduction_scratch()
     return pl.pallas_call(
         tail_kernel,
-        in_specs=[vm()] * 14,
-        out_specs=[vm()] * 4,
-        out_shape=[s((T, D), BF)] * 2 + [s((2, 4, GR, HALF), BF)] * 2,
+        in_specs=[vm()] * 15,
+        out_specs=[vm()] * 5,
+        out_shape=[s((T, D), BF)] * 2 + [s((2, 4, GR, HALF), BF)] * 3,
         scratch_shapes=[
             pltpu.VMEM((FAR, 2 * GR), BF), pltpu.VMEM((7, 64, 2 * GR), BF),
-            pltpu.VMEM((D, T), BF), pltpu.VMEM((D, T), BF), pltpu.VMEM((3, 16, HALF), BF), pltpu.VMEM((T, T), BF),
-            dma((7,)), dma((7,)),
-        ] + [dma((2, 3, 3)), dma((2, 3, 3)), dma(()), dma(())] * 2 + reduction_scratch(),
+            pltpu.VMEM((D, T), BF), pltpu.VMEM((D, T), BF), pltpu.VMEM((3, 16, HALF), BF),
+            pltpu.VMEM((3, 16, HALF), BF), pltpu.VMEM((T, T), BF), dma((7,)), dma((7,)),
+        ] + [dma((2, 3, 3)), dma((2, 3, 3)), dma(()), dma(())] * 3 + older[3:7] + older[9:] + reduction_scratch(),
         compiler_params=pltpu.CompilerParams(
             vmem_limit_bytes=60 << 20, collective_id=3, has_side_effects=True),
         cost_estimate=pl.CostEstimate(flops=16 * T * D * D, bytes_accessed=30 << 20, transcendentals=0),
     )(*args)
 
 
-def lay_kernel(out01_ref, out2_ref, out3_ref, gq_ref, gk_ref, gv_ref, gout_ref, stage, sems):
+def lay_kernel(out0_ref, out1_ref, out2_ref, out3_ref, gq_ref, gk_ref, gv_ref, gout_ref, stage, sems):
     copies = []
     for i, to in enumerate((gq_ref, gk_ref, gv_ref, gout_ref)):
-        blocks = [out01_ref.at[0], out01_ref.at[1], out2_ref, out3_ref]
+        blocks = [out0_ref, out1_ref, out2_ref, out3_ref]
         for g, block in enumerate(blocks):
             whole = jnp.concatenate([block[0, i], block[1, i]], axis=1)
             rows = slice(g * GR, (g + 1) * GR)
@@ -641,17 +659,17 @@
         c.wait()
 
 
-def lay_all(out01, out2, out3):
+def lay_all(out0, out1, out2, out3):
     s = jax.ShapeDtypeStruct
     return pl.pallas_call(
         lay_kernel,
-        in_specs=[vm()] * 3,
+        in_specs=[vm()] * 4,
         out_specs=[pl.BlockSpec(memory_space=pl.ANY)] * 4,
         out_shape=[s((D, D), F32)] * 4,
         scratch_shapes=[pltpu.VMEM((5, D, D), F32), pltpu.SemaphoreType.DMA((4,))],
         compiler_params=pltpu.CompilerParams(vmem_limit_bytes=40 << 20),
         cost_estimate=pl.CostEstimate(flops=4 * D * D, bytes_accessed=24 * D * D, transcendentals=0),
-    )(out01, out2, out3)
+    )(out0, out1, out2, out3)
 
 
 def per_device(tile_embed, tile_source, slide_len, grad_out, w_query, w_key, w_value, w_out):
@@ -661,13 +679,13 @@
     x, go, k, v, qT, kT, vT, gT, far, kfT, vfT, top = front_all(
         lens, source, tile_embed[0], grad_out[0], w_query, w_key, w_value, w_out
     )
-    attT, dqT, dk, dv, dk32, dv32, dkvf, fin, out01 = attn(
+    attT, dqT, dk, dv, dk32, dv32, dkvf, fin, acc, out0 = attn(
         lens, k, v, qT, kT, vT, gT, far, kfT, vfT, top, x, go
     )
-    enc, emb, out2, out3 = tail_all(
-        x, go, attT, dqT, dk, dv, dk32, dv32, dkvf, fin, w_query, w_key, w_value, w_out
+    enc, emb, out1, out2, out3 = tail_all(
+        x, go, attT, dqT, dk, dv, dk32, dv32, dkvf, fin, acc, w_query, w_key, w_value, w_out
     )
-    summed = lay_all(out01, out2, out3)
+    summed = lay_all(out0, out1, out2, out3)
     return (enc[None], emb[None], summed[0], summed[1], summed[2], summed[3])
 
 

time: 238 us -> 233 us (0.979)
  Pallas kernels: 230 us -> 224 us
    pallas_call x1, Pallas kernels: 105 us -> 93.9 us  [attn(): pl.pallas_call(attn_kernel, grid=(HEADS,), in_specs=[sm()] + [vm()] * 12,...]
    pallas_call x2, Pallas kernels: 57.2 us -> 62.9 us  [the longest x1 58.8 us: tail_all(): pl.pallas_call(tail_kernel, in_specs=[vm()] * 15, out_specs=[vm()] * 5, o...]
    unnamed x12 -> x14, local copies, waits for them, and re-layouts: 5.65 us -> 6.92 us
where the time goes in v7:
time: 233 us
  Pallas kernels  224 us (96%)
  local copies, waits for them, and re-layouts  6.92 us (3%)
    pallas_call x1, Pallas kernels, attn(): pl.pallas_call(attn_kernel, grid=(HEADS,), in_specs=[sm()] + [vm()] * 12,...  93.9 us
    pallas_call x1, Pallas kernels, front_all(): pl.pallas_call(front_kernel, in_specs=[sm()] + [vm()] * 7, out_specs=[vm(...  67.4 us
    pallas_call x1, Pallas kernels, tail_all(): pl.pallas_call(tail_kernel, in_specs=[vm()] * 15, out_specs=[vm()] * 5, o...  58.8 us
    unnamed x14, local copies, waits for them, and re-layouts  6.92 us

profile of v7, /device:TPU:1, one launch (start us, length us, event | category | flops | bytes accessed | tf_op | source)
XLA Modules:
  0.0 233.2 jit_solution(1106142800469789810)
XLA Ops:
  1.3 0.6 pad_add_fusion.len_ref
  1.9 67.4 %shard_map.127 = (bf16[1024,768]{1,0:T(8,128)(2,1)}, bf16[1024,768]{1,0:T(8,128)(2,1)}, bf16[1024,768]{1,0:T(8,128)(2,1)}, bf16[1024,768]{1,0:T(8,128)(2,1)}, bf...) custom-call(s32[2]{0:T(128)} %pad_add_fusion.len_ref, ...), custom_call_target="tpu_custom_call" | custom-call | flops 7247757312 | bytes 20971520 | tf_op jit(solution)/shard_map/pallas_call | solution.py:367
  69.3 93.9 %shard_map.128 = (bf16[768,1024]{1,0:T(8,128)(2,1)}, bf16[768,1024]{1,0:T(8,128)(2,1)}, bf16[576,1024]{1,0:T(8,128)(2,1)}, bf16[576,1024]{1,0:T(8,128)(2,1)}, f3...) custom-call(s32[2]{0:T(128)} %pad_add_fusion.len_ref, ...), custom_call_target="tpu_custom_call" | custom-call | flops 60397977600 | bytes 31457280 | tf_op jit(solution)/shard_map/pallas_call | solution.py:194
  163.2 0.0 copy-start
  163.3 58.8 %shard_map.129 = (bf16[1024,768]{1,0:T(8,128)(2,1)}, bf16[1024,768]{1,0:T(8,128)(2,1)}, bf16[2,4,192,384]{3,2,1,0:T(8,128)(2,1)}, bf16[2,4,192,384]{3,2,1,0:T(8,128)(2,1)}, bf16[2,4,192,384]{3,2,1,0:T(8,128)(2,1)}) custom-call(bf16[1024,768]{1,0:T(8,128)(2,1)} %get-tuple-element.37.x_ref, bf16[1024,768]{1,0:T(8,128)(2,1)} %get-tuple-element.38.go_ref, ...), custom_call_target="tpu_custom_call" | custom-call | flops 9663676416 | bytes 31457280 | tf_op jit(solution)/shard_map/pallas_call | solution.py:627
  222.1 0.0 copy-done
  222.1 0.0 copy-start.1
  222.1 1.3 copy-done.1
  223.4 0.0 copy-start.2
  223.4 1.3 copy-done.2
  224.7 0.0 copy-start.3
  224.7 1.3 copy-done.3
  225.9 0.0 copy-start.5
  225.9 4.1 %shard_map.130 = (f32[768,768]{1,0:T(8,128)}, f32[768,768]{1,0:T(8,128)}, f32[768,768]{1,0:T(8,128)}, f32[768,768]{1,0:T(8,128)}) custom-call(bf16[2,4,192,384]{3,2,1,0:T(8,128)(2,1)S(1)} %copy-done, bf16[2,4,192,384]{3,2,1,0:T(8,128)(2,1)S(1)} %copy-done.1, bf16[2,4,192,384]{3,2,1,0:T(8,128)(2,1)S(1)} %copy-done.2, bf16[2,4,192,384]{3,2,1,0:T(8,128)(2,1)S(1)} %copy-done.3), custom_call_target="tpu_custom_call" | custom-call | flops 2359296 | bytes 14155776 | tf_op jit(solution)/shard_map/pallas_call | solution.py:664
  230.0 0.0 copy-done.5
  230.1 0.0 copy-start.4
  230.1 1.1 copy.17
  231.2 0.8 copy-done.4
  232.0 1.1 copy.18
Async XLA Ops:
  163.2 58.9 %copy-start = (bf16[2,4,192,384]{3,2,1,0:T(8,128)(2,1)S(1)}, bf16[2,4,192,384]{3,2,1,0:T(8,128)(2,1)}, u32[]{:S(2)}) copy-start(bf16[2,4,192,384]{3,2,1,0:T(8,128)(2,1)} %get-tuple-element.60.out0_ref) | copy-start | bytes 3538948
  222.1 1.3 copy-start.1
  223.4 1.3 copy-start.2
  224.7 1.3 copy-start.3
  225.9 4.1 %copy-start.5 = (bf16[1024,768]{1,0:T(8,128)(2,1)S(1)}, bf16[1024,768]{1,0:T(8,128)(2,1)}, u32[]{:S(2)}) copy-start(bf16[1024,768]{1,0:T(8,128)(2,1)} %get-tuple-element.58) | copy-start | bytes 4718596
  230.1 2.0 copy-start.4

commit v8 on v7

--- a/solution.py
+++ b/solution.py
@@ -16,9 +16,9 @@
 def nn(a,b): return lax.dot_general(a,b,(((1,),(0,)),((),())),preferred_element_type=F32)
 def nt(a,b): return lax.dot_general(a,b,(((1,),(1,)),((),())),preferred_element_type=F32)
 
-def attn_kernel(len_ref, k_ref, v_ref, qT_ref, kT_ref, vT_ref, gT_ref, far_ref, kfT_ref, vfT_ref, top_ref, x_ref, go_ref,
+def attn_kernel(len_ref, k_ref, v_ref, qT_ref, kT_ref, vT_ref, gT_ref, far_ref, kfT_ref, vfT_ref, top_ref, x_hbm, go_hbm,
                 attT_ref, dqT_ref, dk_ref, dv_ref, dk32_ref, dv32_ref, dkvf_ref, fin_ref, acc_ref, out_ref,
-                qpad, gpad, kb, kfb, m2s, l2s, u2s, w2s, des, dqs, e2s,
+                x_ref, go_ref, ins, qpad, gpad, kb, kfb, m2s, l2s, u2s, w2s, des, dqs, e2s,
                 dk32, dv32, dkvf, xT, part, rx, sums, bs, br, gs, gr, hs, hr, *scratch):
     h = pl.program_id(0)
     step = lax.rem(h, 4)
@@ -37,12 +37,18 @@
     before = jnp.maximum(h // 4 - 2, 0)
     low = pl.ds(pl.multiple_of(now * GR, 64), GR)
 
+    fetch = [pltpu.make_async_copy(x_hbm, x_ref, ins.at[0]), pltpu.make_async_copy(go_hbm, go_ref, ins.at[1])]
+
     @pl.when(h == 0)
     def _():
+        for c in fetch:
+            c.start()
         greet(all_peers())
 
     @pl.when(h == 4)
     def _():
+        for c in fetch:
+            c.wait()
         xT[...] = x_ref[...].T
 
     @pl.when((step == 0) & (h >= 4))
@@ -194,11 +200,12 @@
     return pl.pallas_call(
         attn_kernel,
         grid=(HEADS,),
-        in_specs=[sm()] + [vm()] * 12,
+        in_specs=[sm()] + [vm()] * 10 + [hbm()] * 2,
         out_specs=[vm()] * 10,
         out_shape=[s((D, T), BF)] * 2 + [s((3 * GR, T), BF)] * 2 + [s((GR, T), F32)] * 2 + [s((2 * GR, FAR), BF)]
         + [s((2, 3, 16, HALF), BF), s((4, GR, HALF), F32), s((2, 4, GR, HALF), BF)],
         scratch_shapes=[
+            pltpu.VMEM((T, D), BF), pltpu.VMEM((T, D), BF), dma((2,)),
             pltpu.VMEM((256, T), BF), pltpu.VMEM((256, T), BF), pltpu.VMEM((T, 256), BF), pltpu.VMEM((FAR, 256), BF),
             pltpu.VMEM((1, T), F32), pltpu.VMEM((1, T), F32), pltpu.VMEM((HD, T), F32), pltpu.VMEM((1, T), F32),
             pltpu.VMEM((1, T), F32), pltpu.VMEM((HD, T), F32), pltpu.VMEM((FAR, 128), F32),
@@ -216,6 +223,10 @@
     return pl.BlockSpec(memory_space=pltpu.VMEM)
 
 
+def hbm():
+    return pl.BlockSpec(memory_space=pl.ANY)
+
+
 def sm():
     return pl.BlockSpec(memory_space=pltpu.SMEM)
 
@@ -276,10 +287,20 @@
     return jnp.where(lax.rem(ki, 64) * RATE + ki // 64 < n, 0.0, NEG).astype(BF)
 
 
-def front_kernel(len_ref, src_ref, rows_ref, grad_ref, wq_ref, wk_ref, wv_ref, wo_ref,
+def front_kernel(len_ref, src_ref, rows_ref, grad_hbm, wq_hbm, wk_hbm, wv_hbm, wo_hbm,
+                 x_out, go_out, k_out, v_out, qT_out, kT_out, vT_out, gT_out, far_out, kfT_out, vfT_out, top_out,
                  x_ref, go_ref, k_ref, v_ref, qT_ref, kT_ref, vT_ref, gT_ref, far_ref, kfT_ref, vfT_ref, top_ref,
-                 ask, req, picked, arrived, perm, qpad, kb, qs, qr, ps, pr, fs, fr):
+                 grad_ref, wq_ref, wk_ref, wv_ref, wo_ref,
+                 ask, req, picked, arrived, perm, qpad, kb, ins, outs, qs, qr, ps, pr, fs, fr):
     n = len_ref[0]
+    fetch = [pltpu.make_async_copy(a, b, ins.at[i]) for i, (a, b) in enumerate((
+        (grad_hbm, grad_ref), (wo_hbm, wo_ref), (wk_hbm, wk_ref), (wv_hbm, wv_ref), (wq_hbm, wq_ref)))]
+    for c in fetch:
+        c.start()
+    store = [pltpu.make_async_copy(a, b, outs.at[i]) for i, (a, b) in enumerate((
+        (x_ref, x_out), (go_ref, go_out), (k_ref, k_out), (v_ref, v_out), (qT_ref, qT_out), (kT_ref, kT_out),
+        (vT_ref, vT_out), (gT_ref, gT_out), (far_ref, far_out), (kfT_ref, kfT_out), (vfT_ref, vfT_out),
+        (top_ref, top_out)))]
     s = lax.axis_index("seq")
     peers = [seq_peer(s, d) for d in range(1, 8)]
     greet(peers)
@@ -306,8 +327,12 @@
     perm[...] = permT.T
     qi = lax.broadcasted_iota(jnp.int32, (1, T), 1)
     ok = (lax.rem(qi, 64) * RATE + qi // 64) < n
+    fetch[0].wait()
+    fetch[1].wait()
     go_ref[...] = nn(reorder, grad_ref[...]).astype(BF)
+    store[1].start()
     gT_ref[...] = jnp.where(ok, nt(wo_ref[...], go_ref[...]), 0.0).astype(BF)
+    store[7].start()
     cells = lax.broadcasted_iota(jnp.int32, (128, T), 1).astype(F32)
     rows = rows_ref[...]
     mine = pl.ds(pl.multiple_of(s * 128, 128), 128)
@@ -323,10 +348,15 @@
         c.wait_recv()
     x = nn(perm[...], arrived[...]).astype(BF)
     x_ref[...] = x
+    store[0].start()
+    fetch[2].wait()
+    fetch[3].wait()
     k = nn(x, wk_ref[...]).astype(BF)
     v = nn(x, wv_ref[...]).astype(BF)
     k_ref[...] = k
     v_ref[...] = v
+    store[2].start()
+    store[3].start()
     col = lax.broadcasted_iota(jnp.int32, (64, D), 1) // HD
     fk = jnp.zeros((64, D), BF)
     fv = jnp.zeros((64, D), BF)
@@ -337,9 +367,13 @@
     far_ref[here, 0:D] = fk
     far_ref[here, D:2 * D] = fv
     fars = [send(far_ref.at[here], far_ref.at[here], fs.at[d - 1], fr.at[d - 1], peers[d - 1]) for d in range(1, 8)]
+    fetch[4].wait()
     qT_ref[...] = nn(x, wq_ref[...]).astype(BF).T
+    store[4].start()
     kT_ref[...] = k.T
+    store[5].start()
     vT_ref[...] = v.T
+    store[6].start()
     rows_in = lax.broadcasted_iota(jnp.int32, (256, T), 0)
     cols_in = lax.broadcasted_iota(jnp.int32, (T, 256), 1)
     kbias = key_bias(n)
@@ -353,10 +387,16 @@
             sl = slice(ci * QC, (ci + 1) * QC)
             top_ref[h, :, sl] = jnp.max(nn(kb[...], qpad[:, sl]), axis=0, keepdims=True)
 
+    store[11].start()
     for c in fars:
         c.wait_recv()
+    store[8].start()
     kfT_ref[...] = far_ref[:, 0:D].T
     vfT_ref[...] = far_ref[:, D:2 * D].T
+    store[9].start()
+    store[10].start()
+    for c in store:
+        c.wait()
     for c in asks + sends + fars:
         c.wait_send()
 
@@ -366,13 +406,17 @@
     dma = pltpu.SemaphoreType.DMA
     return pl.pallas_call(
         front_kernel,
-        in_specs=[sm()] + [vm()] * 7,
-        out_specs=[vm()] * 12,
+        in_specs=[sm()] + [vm()] * 2 + [hbm()] * 5,
+        out_specs=[hbm()] * 12,
         out_shape=[s((T, D), BF)] * 4 + [s((D, T), BF)] * 4 + [s((FAR, 2 * D), BF)] + [s((D, FAR), BF)] * 2
         + [s((HEADS, 1, T), F32)],
-        scratch_shapes=[
+        scratch_shapes=[pltpu.VMEM((T, D), BF)] * 4 + [pltpu.VMEM((D, T), BF)] * 4 + [
+            pltpu.VMEM((FAR, 2 * D), BF), pltpu.VMEM((D, FAR), BF), pltpu.VMEM((D, FAR), BF),
+            pltpu.VMEM((HEADS, 1, T), F32), pltpu.VMEM((T, D), BF), pltpu.VMEM((D, D), BF), pltpu.VMEM((D, D), BF),
+            pltpu.VMEM((D, D), BF), pltpu.VMEM((D, D), BF),
             pltpu.VMEM((8, 8, 128), F32), pltpu.VMEM((7, 8, 128), F32), pltpu.VMEM((7, 128, D), BF),
             pltpu.VMEM((T, D), BF), pltpu.VMEM((T, T), BF), pltpu.VMEM((256, T), BF), pltpu.VMEM((T, 256), BF),
+        dma((5,)), dma((12,)),
         ] + [dma((7,))] * 6,
         compiler_params=pltpu.CompilerParams(
             vmem_limit_bytes=60 << 20, collective_id=2, has_side_effects=True),
@@ -562,8 +606,13 @@
 
 
 def tail_kernel(x_ref, go_ref, attT_ref, dqT_ref, dk_ref, dv_ref, dk32_ref, dv32_ref, dkvf_ref, fin_ref, acc_ref,
-                wq_ref, wk_ref, wv_ref, wo_ref, enc_ref, emb_ref, out1_ref, out2_ref, out3_ref,
-                part, rx, dk, dv, fin2, fin3, home, bs, br, *scratch):
+                wq_hbm, wk_hbm, wv_hbm, wo_hbm, enc_ref, emb_ref, out1_ref, out2_ref, out3_ref,
+                wq_ref, wk_ref, wv_ref, wo_ref, ins, part, rx, dk, dv, fin2, fin3, home, bs, br, *scratch):
+    fetch = [pltpu.make_async_copy(a, b, ins.at[i]) for i, (a, b) in enumerate((
+        (dk_ref, dk.at[pl.ds(0, 3 * GR)]), (dv_ref, dv.at[pl.ds(0, 3 * GR)]), (wo_hbm, wo_ref), (wq_hbm, wq_ref),
+        (wk_hbm, wk_ref), (wv_hbm, wv_ref)))]
+    for c in fetch:
+        c.start()
     greet(all_peers())
     sems, older, newer = scratch[:12], scratch[12:18], scratch[18:]
     red2 = Reduction(None, None, acc_ref, *older[:4], fin2, None, None, *older[4:])
@@ -584,8 +633,6 @@
     red3.rows(3, nn(attT_ref[last:, :], go_ref[...]))
     red3.pair(3).start()
     spread1.middle()
-    dk[0:last, :] = dk_ref[...]
-    dv[0:last, :] = dv_ref[...]
     spot = lax.broadcasted_iota(jnp.int32, (T, T), 0)
     home[...] = (lax.broadcasted_iota(jnp.int32, (T, T), 1) == lax.rem(spot, RATE) * 64 + spot // RATE).astype(BF)
     red2.after_first()
@@ -598,6 +645,8 @@
     red2.after_second()
     red3.add_pairs()
     red3.start(red3.wave(0))
+    for c in fetch:
+        c.wait()
     enc = (x_ref[...].astype(F32) + nn(attT_ref[...].T, wo_ref[...])).astype(BF)
     red2.after_third()
     spread2.begin()
@@ -626,10 +675,11 @@
     older = reduction_scratch()
     return pl.pallas_call(
         tail_kernel,
-        in_specs=[vm()] * 15,
+        in_specs=[vm()] * 4 + [hbm()] * 2 + [vm()] * 5 + [hbm()] * 4,
         out_specs=[vm()] * 5,
         out_shape=[s((T, D), BF)] * 2 + [s((2, 4, GR, HALF), BF)] * 3,
         scratch_shapes=[
+            pltpu.VMEM((D, D), BF), pltpu.VMEM((D, D), BF), pltpu.VMEM((D, D), BF), pltpu.VMEM((D, D), BF), dma((6,)),
             pltpu.VMEM((FAR, 2 * GR), BF), pltpu.VMEM((7, 64, 2 * GR), BF),
             pltpu.VMEM((D, T), BF), pltpu.VMEM((D, T), BF), pltpu.VMEM((3, 16, HALF), BF),
             pltpu.VMEM((3, 16, HALF), BF), pltpu.VMEM((T, T), BF), dma((7,)), dma((7,)),
@@ -640,36 +690,44 @@
     )(*args)
 
 
-def lay_kernel(out0_ref, out1_ref, out2_ref, out3_ref, gq_ref, gk_ref, gv_ref, gout_ref, stage, sems):
-    copies = []
+def lay_kernel(enc_ref, emb_ref, out0_ref, out1_ref, out2_ref, out3_ref,
+               enc_out, emb_out, gq_ref, gk_ref, gv_ref, gout_ref, blocks, plain, stage, passing, ins, outs):
+    copies = [pltpu.make_async_copy(enc_ref, enc_out, passing.at[0]),
+              pltpu.make_async_copy(emb_ref, emb_out, passing.at[1])]
+    loads = [pltpu.make_async_copy(o.at[:, i], blocks.at[i, :, g], ins.at[i, g])
+             for i in range(4) for g, o in enumerate((out0_ref, out1_ref, out2_ref, out3_ref))]
+    for c in loads + copies:
+        c.start()
     for i, to in enumerate((gq_ref, gk_ref, gv_ref, gout_ref)):
-        blocks = [out0_ref, out1_ref, out2_ref, out3_ref]
-        for g, block in enumerate(blocks):
-            whole = jnp.concatenate([block[0, i], block[1, i]], axis=1)
+        for g in range(4):
+            loads[4 * i + g].wait()
             rows = slice(g * GR, (g + 1) * GR)
-            if i < 3:
-                stage[4, rows, :] = whole.astype(F32)
-            else:
-                stage[i, rows, :] = whole.astype(F32)
+            target = plain if i < 3 else stage.at[i]
+            target[rows, 0:HALF] = blocks[i, 0, g].astype(F32)
+            target[rows, HALF:D] = blocks[i, 1, g].astype(F32)
         if i < 3:
-            stage[i] = stage[4].T
-        copies.append(pltpu.make_async_copy(stage.at[i], to, sems.at[i]))
+            stage[i] = plain[...].T
+        copies.append(pltpu.make_async_copy(stage.at[i], to, outs.at[i]))
         copies[-1].start()
     for c in copies:
         c.wait()
 
 
-def lay_all(out0, out1, out2, out3):
+def lay_all(*args):
     s = jax.ShapeDtypeStruct
+    dma = pltpu.SemaphoreType.DMA
     return pl.pallas_call(
         lay_kernel,
-        in_specs=[vm()] * 4,
-        out_specs=[pl.BlockSpec(memory_space=pl.ANY)] * 4,
-        out_shape=[s((D, D), F32)] * 4,
-        scratch_shapes=[pltpu.VMEM((5, D, D), F32), pltpu.SemaphoreType.DMA((4,))],
+        in_specs=[hbm()] * 6,
+        out_specs=[hbm()] * 6,
+        out_shape=[s((T, D), BF)] * 2 + [s((D, D), F32)] * 4,
+        scratch_shapes=[
+            pltpu.VMEM((4, 2, 4, GR, HALF), BF), pltpu.VMEM((D, D), F32), pltpu.VMEM((4, D, D), F32),
+            dma((2,)), dma((4, 4)), dma((4,)),
+        ],
         compiler_params=pltpu.CompilerParams(vmem_limit_bytes=40 << 20),
         cost_estimate=pl.CostEstimate(flops=4 * D * D, bytes_accessed=24 * D * D, transcendentals=0),
-    )(out0, out1, out2, out3)
+    )(*args)
 
 
 def per_device(tile_embed, tile_source, slide_len, grad_out, w_query, w_key, w_value, w_out):
@@ -685,7 +743,7 @@
     enc, emb, out1, out2, out3 = tail_all(
         x, go, attT, dqT, dk, dv, dk32, dv32, dkvf, fin, acc, w_query, w_key, w_value, w_out
     )
-    summed = lay_all(out0, out1, out2, out3)
+    enc, emb, *summed = lay_all(enc, emb, out0, out1, out2, out3)
     return (enc[None], emb[None], summed[0], summed[1], summed[2], summed[3])
 
 

time: 233 us -> 227 us (0.974)
  Pallas kernels: 224 us -> 218 us
    pallas_call x4, Pallas kernels: 224 us -> 218 us  [the longest x1 92.9 us: attn(): pl.pallas_call(attn_kernel, grid=(HEADS,), in_specs=[sm()] + [vm()] * 10...]
    unnamed x14 -> x12, local copies, waits for them, and re-layouts: 6.92 us -> 6.62 us
where the time goes in v8:
time: 227 us; the launch traced here: 226 us
  Pallas kernels  218 us (96%)
  local copies, waits for them, and re-layouts  6.62 us (3%)
    pallas_call x1, Pallas kernels, attn(): pl.pallas_call(attn_kernel, grid=(HEADS,), in_specs=[sm()] + [vm()] * 10...  92.9 us
    pallas_call x1, Pallas kernels, front_all(): pl.pallas_call(front_kernel, in_specs=[sm()] + [vm()] * 2 + [hbm()] * 5,...  62.3 us
    pallas_call x1, Pallas kernels, tail_all(): pl.pallas_call(tail_kernel, in_specs=[vm()] * 4 + [hbm()] * 2 + [vm()] *...  56.9 us
    unnamed x12, local copies, waits for them, and re-layouts  6.62 us
    pallas_call x1, Pallas kernels, lay_all(): pl.pallas_call(lay_kernel, in_specs=[hbm()] * 6, out_specs=[hbm()] * 6, o...  5.45 us

profile of v8, /device:TPU:1, one launch (start us, length us, event | category | flops | bytes accessed | tf_op | source)
XLA Modules:
  0.0 226.3 jit_solution(1771036840030950927)
XLA Ops:
  1.3 0.6 pad_add_fusion.len_ref
  1.9 62.3 %shard_map.127 = (bf16[1024,768]{1,0:T(8,128)(2,1)}, bf16[1024,768]{1,0:T(8,128)(2,1)}, bf16[1024,768]{1,0:T(8,128)(2,1)}, bf16[1024,768]{1,0:T(8,128)(2,1)}, bf...) custom-call(s32[2]{0:T(128)} %pad_add_fusion.len_ref, ...), custom_call_target="tpu_custom_call" | custom-call | flops 7247757312 | bytes 20971520 | tf_op jit(solution)/shard_map/pallas_call | solution.py:407
  64.2 92.9 %shard_map.128 = (bf16[768,1024]{1,0:T(8,128)(2,1)}, bf16[768,1024]{1,0:T(8,128)(2,1)}, bf16[576,1024]{1,0:T(8,128)(2,1)}, bf16[576,1024]{1,0:T(8,128)(2,1)}, f3...) custom-call(s32[2]{0:T(128)} %pad_add_fusion.len_ref, ...), custom_call_target="tpu_custom_call" | custom-call | flops 60397977600 | bytes 31457280 | tf_op jit(solution)/shard_map/pallas_call | solution.py:200
  157.1 0.0 copy-start.2
  157.1 56.9 %shard_map.129 = (bf16[1024,768]{1,0:T(8,128)(2,1)}, bf16[1024,768]{1,0:T(8,128)(2,1)}, bf16[2,4,192,384]{3,2,1,0:T(8,128)(2,1)}, bf16[2,4,192,384]{3,2,1,0:T(8,128)(2,1)}, bf16[2,4,192,384]{3,2,1,0:T(8,128)(2,1)}) custom-call(bf16[1024,768]{1,0:T(8,128)(2,1)} %get-tuple-element.39.x_hbm.x_ref, bf16[1024,768]{1,0:T(8,128)(2,1)} %get-tuple-element.40.go_hbm.go_ref, ...), custom_call_target="tpu_custom_call" | custom-call | flops 9663676416 | bytes 31457280 | tf_op jit(solution)/shard_map/pallas_call | solution.py:676
  214.1 0.0 copy-done.2
  214.1 0.0 copy-start
  214.1 1.4 copy-done
  215.5 0.0 copy-start.1
  215.5 1.4 copy-done.1
  216.9 0.0 copy-start.3
  216.9 1.3 copy-done.3
  218.2 0.0 copy-start.4
  218.2 1.3 copy-done.4
  219.4 0.0 copy-start.5
  219.4 1.3 copy-done.5
  220.7 5.4 %shard_map.130 = (bf16[1024,768]{1,0:T(8,128)(2,1)}, bf16[1024,768]{1,0:T(8,128)(2,1)}, f32[768,768]{1,0:T(8,128)}, f32[768,768]{1,0:T(8,128)}, f32[768,768]{1,0:T(8,128)}, /*index=5*/f32[768,768]{1,0:T(8,128)}) custom-call(bf16[1024,768]{1,0:T(8,128)(2,1)S(1)} %copy-done, bf16[1024,768]{1,0:T(8,128)(2,1)S(1)} %copy-done.1, ...), custom_call_target="tpu_custom_call" | custom-call | flops 2359296 | bytes 14155776 | tf_op jit(solution)/shard_map/pallas_call | solution.py:719
Async XLA Ops:
  157.1 56.9 %copy-start.2 = (bf16[2,4,192,384]{3,2,1,0:T(8,128)(2,1)S(1)}, bf16[2,4,192,384]{3,2,1,0:T(8,128)(2,1)}, u32[]{:S(2)}) copy-start(bf16[2,4,192,384]{3,2,1,0:T(8,128)(2,1)} %get-tuple-element.62.out0_ref) | copy-start | bytes 3538948
  214.1 1.4 copy-start
  215.5 1.4 copy-start.1
  216.9 1.3 copy-start.3
  218.2 1.3 copy-start.4
  219.4 1.3 copy-start.5

commit v9 on v8

--- a/solution.py
+++ b/solution.py
@@ -607,7 +607,7 @@
 
 def tail_kernel(x_ref, go_ref, attT_ref, dqT_ref, dk_ref, dv_ref, dk32_ref, dv32_ref, dkvf_ref, fin_ref, acc_ref,
                 wq_hbm, wk_hbm, wv_hbm, wo_hbm, enc_ref, emb_ref, out1_ref, out2_ref, out3_ref,
-                wq_ref, wk_ref, wv_ref, wo_ref, ins, part, rx, dk, dv, fin2, fin3, home, bs, br, *scratch):
+                wq_ref, wk_ref, wv_ref, wo_ref, ins, part, rx, dk, dv, fin2, fin3, home, mid, bs, br, *scratch):
     fetch = [pltpu.make_async_copy(a, b, ins.at[i]) for i, (a, b) in enumerate((
         (dk_ref, dk.at[pl.ds(0, 3 * GR)]), (dv_ref, dv.at[pl.ds(0, 3 * GR)]), (wo_hbm, wo_ref), (wq_hbm, wq_ref),
         (wk_hbm, wk_ref), (wv_hbm, wv_ref)))]
@@ -620,48 +620,55 @@
     spread1 = Spread(red2, fin_ref.at[1], out1_ref, *sems[0:4])
     spread2 = Spread(red2, fin2, out2_ref, *sems[4:8])
     spread3 = Spread(red3, fin3, out3_ref, *sems[8:12])
+
+    def send_home(to):
+        @pl.loop(0, 4)
+        def _(i):
+            rows = pl.ds(pl.multiple_of(i * 256, 256), 256)
+            to[rows, :] = nn(home[rows, :], mid[...]).astype(BF)
+
     part[...] = dkvf_ref[...].T
     backs = back_copies(part, rx, bs, br)
     for c in backs:
         c.start()
     spread1.begin()
-    red2.start(red2.wave(0))
     last = 3 * GR
     xT = x_ref[...].T
     red3.rows(0, nt(dqT_ref[last:, :], xT))
     red3.pair(0).start()
     red3.rows(3, nn(attT_ref[last:, :], go_ref[...]))
     red3.pair(3).start()
-    spread1.middle()
+    for c in fetch:
+        c.wait()
+    mid[...] = (x_ref[...].astype(F32) + nn(attT_ref[...].T, wo_ref[...])).astype(BF)
     spot = lax.broadcasted_iota(jnp.int32, (T, T), 0)
     home[...] = (lax.broadcasted_iota(jnp.int32, (T, T), 1) == lax.rem(spot, RATE) * 64 + spot // RATE).astype(BF)
-    red2.after_first()
     add_back(backs, part, rx, 3, dk32_ref, dv32_ref, dk.at[last:D], dv.at[last:D])
+    red2.start(red2.wave(0))
     red3.rows(1, nt(dk[last:D, :], xT))
     red3.pair(1).start()
     red3.rows(2, nt(dv[last:D, :], xT))
     red3.pair(2).start()
-    spread1.end()
-    red2.after_second()
+    spread1.middle()
     red3.add_pairs()
     red3.start(red3.wave(0))
-    for c in fetch:
-        c.wait()
-    enc = (x_ref[...].astype(F32) + nn(attT_ref[...].T, wo_ref[...])).astype(BF)
+    send_home(enc_ref)
+    red2.after_first()
+    e = nn(wq_ref[...], dqT_ref[...]) + nn(wk_ref[...], dk[...])
+    red3.after_first()
+    red2.after_second()
+    spread1.end()
+    e = e + nn(wv_ref[...], dv[...])
+    red3.after_second()
     red2.after_third()
     spread2.begin()
-    enc_ref[...] = nn(home[...], enc).astype(BF)
-    red3.after_first()
-    spread2.middle()
-    e = nn(wq_ref[...], dqT_ref[...]) + nn(wk_ref[...], dk[...])
-    red3.after_second()
-    spread2.end()
-    e = e + nn(wv_ref[...], dv[...])
+    mid[...] = (go_ref[...].astype(F32) + e.T).astype(BF)
     red3.after_third()
     spread3.begin()
-    emb = (go_ref[...].astype(F32) + e.T).astype(BF)
+    spread2.middle()
+    send_home(emb_ref)
     spread3.middle()
-    emb_ref[...] = nn(home[...], emb).astype(BF)
+    spread2.end()
     spread3.end()
     red2.finish()
     red3.finish()
@@ -682,7 +689,7 @@
             pltpu.VMEM((D, D), BF), pltpu.VMEM((D, D), BF), pltpu.VMEM((D, D), BF), pltpu.VMEM((D, D), BF), dma((6,)),
             pltpu.VMEM((FAR, 2 * GR), BF), pltpu.VMEM((7, 64, 2 * GR), BF),
             pltpu.VMEM((D, T), BF), pltpu.VMEM((D, T), BF), pltpu.VMEM((3, 16, HALF), BF),
-            pltpu.VMEM((3, 16, HALF), BF), pltpu.VMEM((T, T), BF), dma((7,)), dma((7,)),
+            pltpu.VMEM((3, 16, HALF), BF), pltpu.VMEM((T, T), BF), pltpu.VMEM((T, D), BF), dma((7,)), dma((7,)),
         ] + [dma((2, 3, 3)), dma((2, 3, 3)), dma(()), dma(())] * 3 + older[3:7] + older[9:] + reduction_scratch(),
         compiler_params=pltpu.CompilerParams(
             vmem_limit_bytes=60 << 20, collective_id=3, has_side_effects=True),
@@ -725,7 +732,7 @@
             pltpu.VMEM((4, 2, 4, GR, HALF), BF), pltpu.VMEM((D, D), F32), pltpu.VMEM((4, D, D), F32),
             dma((2,)), dma((4, 4)), dma((4,)),
         ],
-        compiler_params=pltpu.CompilerParams(vmem_limit_bytes=40 << 20),
+        compiler_params=pltpu.CompilerParams(vmem_limit_bytes=60 << 20),
         cost_estimate=pl.CostEstimate(flops=4 * D * D, bytes_accessed=24 * D * D, transcendentals=0),
     )(*args)
 

time: 227 us -> 306 us (1.35)
  Pallas kernels: 218 us -> 304 us
  local copies, waits for them, and re-layouts: 6.62 us -> 0 us
    pallas_call x1, Pallas kernels: 5.45 us -> 96.6 us  [lay_all(): pl.pallas_call(lay_kernel, in_specs=[hbm()] * 6, out_specs=[hbm()] * 6, o...]
    unnamed x12 -> x0, local copies, waits for them, and re-layouts: 6.62 us -> none
    pallas_call x1, Pallas kernels: 56.9 us -> 51.9 us  [tail_all(): pl.pallas_call(tail_kernel, in_specs=[vm()] * 4 + [hbm()] * 2 + [vm()] *...]
where the time goes in v9:
time: 306 us
  Pallas kernels  304 us (99%)
    pallas_call x1, Pallas kernels, lay_all(): pl.pallas_call(lay_kernel, in_specs=[hbm()] * 6, out_specs=[hbm()] * 6, o...  96.6 us
    pallas_call x1, Pallas kernels, attn(): pl.pallas_call(attn_kernel, grid=(HEADS,), in_specs=[sm()] + [vm()] * 10...  92.9 us
    pallas_call x1, Pallas kernels, front_all(): pl.pallas_call(front_kernel, in_specs=[sm()] + [vm()] * 2 + [hbm()] * 5,...  62.3 us
    pallas_call x1, Pallas kernels, tail_all(): pl.pallas_call(tail_kernel, in_specs=[vm()] * 4 + [hbm()] * 2 + [vm()] *...  51.9 us

profile of v9, /device:TPU:1, one launch (start us, length us, event | category | flops | bytes accessed | tf_op | source)
XLA Modules:
  0.0 305.8 jit_solution(17926631115488727068)
XLA Ops:
  1.3 0.6 pad_add_fusion.len_ref
  1.9 62.3 %shard_map.127 = (bf16[1024,768]{1,0:T(8,128)(2,1)}, bf16[1024,768]{1,0:T(8,128)(2,1)}, bf16[1024,768]{1,0:T(8,128)(2,1)}, bf16[1024,768]{1,0:T(8,128)(2,1)}, bf...) custom-call(s32[2]{0:T(128)} %pad_add_fusion.len_ref, ...), custom_call_target="tpu_custom_call" | custom-call | flops 7247757312 | bytes 20971520 | tf_op jit(solution)/shard_map/pallas_call | solution.py:407
  64.2 92.9 %shard_map.128 = (bf16[768,1024]{1,0:T(8,128)(2,1)}, bf16[768,1024]{1,0:T(8,128)(2,1)}, bf16[576,1024]{1,0:T(8,128)(2,1)}, bf16[576,1024]{1,0:T(8,128)(2,1)}, f3...) custom-call(s32[2]{0:T(128)} %pad_add_fusion.len_ref, ...), custom_call_target="tpu_custom_call" | custom-call | flops 60397977600 | bytes 31457280 | tf_op jit(solution)/shard_map/pallas_call | solution.py:200
  157.1 51.9 %shard_map.129 = (bf16[1024,768]{1,0:T(8,128)(2,1)}, bf16[1024,768]{1,0:T(8,128)(2,1)}, bf16[2,4,192,384]{3,2,1,0:T(8,128)(2,1)}, bf16[2,4,192,384]{3,2,1,0:T(8,128)(2,1)}, bf16[2,4,192,384]{3,2,1,0:T(8,128)(2,1)}) custom-call(bf16[1024,768]{1,0:T(8,128)(2,1)} %get-tuple-element.39.x_hbm.x_ref, bf16[1024,768]{1,0:T(8,128)(2,1)} %get-tuple-element.40.go_hbm.go_ref, ...), custom_call_target="tpu_custom_call" | custom-call | flops 9663676416 | bytes 31457280 | tf_op jit(solution)/shard_map/pallas_call | solution.py:683
  209.0 96.6 %shard_map.130 = (bf16[1024,768]{1,0:T(8,128)(2,1)}, bf16[1024,768]{1,0:T(8,128)(2,1)}, f32[768,768]{1,0:T(8,128)}, f32[768,768]{1,0:T(8,128)}, f32[768,768]{1,0:T(8,128)}, /*index=5*/f32[768,768]{1,0:T(8,128)}) custom-call(bf16[1024,768]{1,0:T(8,128)(2,1)} %get-tuple-element.60.enc_ref, bf16[1024,768]{1,0:T(8,128)(2,1)} %get-tuple-element.61.emb_ref, ...), custom_call_target="tpu_custom_call" | custom-call | flops 2359296 | bytes 14155776 | tf_op jit(solution)/shard_map/pallas_call | solution.py:726

commit v10 on v9

--- a/solution.py
+++ b/solution.py
@@ -698,12 +698,14 @@
 
 
 def lay_kernel(enc_ref, emb_ref, out0_ref, out1_ref, out2_ref, out3_ref,
-               enc_out, emb_out, gq_ref, gk_ref, gv_ref, gout_ref, blocks, plain, stage, passing, ins, outs):
-    copies = [pltpu.make_async_copy(enc_ref, enc_out, passing.at[0]),
-              pltpu.make_async_copy(emb_ref, emb_out, passing.at[1])]
+               enc_out, emb_out, gq_ref, gk_ref, gv_ref, gout_ref, blocks, plain, stage, held, taking, passing, ins, outs):
+    takes = [pltpu.make_async_copy(enc_ref, held.at[0], taking.at[0]),
+             pltpu.make_async_copy(emb_ref, held.at[1], taking.at[1])]
+    copies = [pltpu.make_async_copy(held.at[0], enc_out, passing.at[0]),
+              pltpu.make_async_copy(held.at[1], emb_out, passing.at[1])]
     loads = [pltpu.make_async_copy(o.at[:, i], blocks.at[i, :, g], ins.at[i, g])
              for i in range(4) for g, o in enumerate((out0_ref, out1_ref, out2_ref, out3_ref))]
-    for c in loads + copies:
+    for c in loads + takes:
         c.start()
     for i, to in enumerate((gq_ref, gk_ref, gv_ref, gout_ref)):
         for g in range(4):
@@ -716,6 +718,9 @@
             stage[i] = plain[...].T
         copies.append(pltpu.make_async_copy(stage.at[i], to, outs.at[i]))
         copies[-1].start()
+        if i < 2:
+            takes[i].wait()
+            copies[i].start()
     for c in copies:
         c.wait()
 
@@ -730,7 +735,7 @@
         out_shape=[s((T, D), BF)] * 2 + [s((D, D), F32)] * 4,
         scratch_shapes=[
             pltpu.VMEM((4, 2, 4, GR, HALF), BF), pltpu.VMEM((D, D), F32), pltpu.VMEM((4, D, D), F32),
-            dma((2,)), dma((4, 4)), dma((4,)),
+            pltpu.VMEM((2, T, D), BF), dma((2,)), dma((2,)), dma((4, 4)), dma((4,)),
         ],
         compiler_params=pltpu.CompilerParams(vmem_limit_bytes=60 << 20),
         cost_estimate=pl.CostEstimate(flops=4 * D * D, bytes_accessed=24 * D * D, transcendentals=0),

time: 306 us -> 217 us (0.71)
  Pallas kernels: 304 us -> 214 us
    pallas_call x1, Pallas kernels: 96.6 us -> 7.33 us  [lay_all(): pl.pallas_call(lay_kernel, in_specs=[hbm()] * 6, out_specs=[hbm()] * 6, o...]
where the time goes in v10:
time: 217 us
  Pallas kernels  214 us (99%)
    pallas_call x1, Pallas kernels, attn(): pl.pallas_call(attn_kernel, grid=(HEADS,), in_specs=[sm()] + [vm()] * 10...  92.9 us
    pallas_call x1, Pallas kernels, front_all(): pl.pallas_call(front_kernel, in_specs=[sm()] + [vm()] * 2 + [hbm()] * 5,...  62.3 us
    pallas_call x1, Pallas kernels, tail_all(): pl.pallas_call(tail_kernel, in_specs=[vm()] * 4 + [hbm()] * 2 + [vm()] *...  51.9 us
    pallas_call x1, Pallas kernels, lay_all(): pl.pallas_call(lay_kernel, in_specs=[hbm()] * 6, out_specs=[hbm()] * 6, o...  7.33 us

profile of v10, /device:TPU:1, one launch (start us, length us, event | category | flops | bytes accessed | tf_op | source)
XLA Modules:
  0.0 216.5 jit_solution(13659163368650223735)
XLA Ops:
  1.3 0.6 pad_add_fusion.len_ref
  1.9 62.3 %shard_map.127 = (bf16[1024,768]{1,0:T(8,128)(2,1)}, bf16[1024,768]{1,0:T(8,128)(2,1)}, bf16[1024,768]{1,0:T(8,128)(2,1)}, bf16[1024,768]{1,0:T(8,128)(2,1)}, bf...) custom-call(s32[2]{0:T(128)} %pad_add_fusion.len_ref, ...), custom_call_target="tpu_custom_call" | custom-call | flops 7247757312 | bytes 20971520 | tf_op jit(solution)/shard_map/pallas_call | solution.py:407
  64.2 92.9 %shard_map.128 = (bf16[768,1024]{1,0:T(8,128)(2,1)}, bf16[768,1024]{1,0:T(8,128)(2,1)}, bf16[576,1024]{1,0:T(8,128)(2,1)}, bf16[576,1024]{1,0:T(8,128)(2,1)}, f3...) custom-call(s32[2]{0:T(128)} %pad_add_fusion.len_ref, ...), custom_call_target="tpu_custom_call" | custom-call | flops 60397977600 | bytes 31457280 | tf_op jit(solution)/shard_map/pallas_call | solution.py:200
  157.1 51.9 %shard_map.129 = (bf16[1024,768]{1,0:T(8,128)(2,1)}, bf16[1024,768]{1,0:T(8,128)(2,1)}, bf16[2,4,192,384]{3,2,1,0:T(8,128)(2,1)}, bf16[2,4,192,384]{3,2,1,0:T(8,128)(2,1)}, bf16[2,4,192,384]{3,2,1,0:T(8,128)(2,1)}) custom-call(bf16[1024,768]{1,0:T(8,128)(2,1)} %get-tuple-element.39.x_hbm.x_ref, bf16[1024,768]{1,0:T(8,128)(2,1)} %get-tuple-element.40.go_hbm.go_ref, ...), custom_call_target="tpu_custom_call" | custom-call | flops 9663676416 | bytes 31457280 | tf_op jit(solution)/shard_map/pallas_call | solution.py:683
  209.0 7.3 %shard_map.130 = (bf16[1024,768]{1,0:T(8,128)(2,1)}, bf16[1024,768]{1,0:T(8,128)(2,1)}, f32[768,768]{1,0:T(8,128)}, f32[768,768]{1,0:T(8,128)}, f32[768,768]{1,0:T(8,128)}, /*index=5*/f32[768,768]{1,0:T(8,128)}) custom-call(bf16[1024,768]{1,0:T(8,128)(2,1)} %get-tuple-element.60.enc_ref, bf16[1024,768]{1,0:T(8,128)(2,1)} %get-tuple-element.61.emb_ref, ...), custom_call_target="tpu_custom_call" | custom-call | flops 2359296 | bytes 14155776 | tf_op jit(solution)/shard_map/pallas_call | solution.py:731
